TPU v7x, 32 devices: a whole 2x2x4 slice. The times are simulated.
32 devices in a mesh: rep: 8 (over z, y), voc: 4 (over x, core).
Axes of the slice: x: 2, y: 2, z: 4, core: 2. Of those that a mesh axis runs over, the one named last changes fastest.
Arguments:
- token_ids: int32 [8, 1024], P('rep'), may hold values from 0 to 31999
- target_ids: int32 [8, 1024], P('rep'), may hold values from 0 to 31999
- embedding: float32 [32000, 512], P('voc'), may hold values from -0.6 to 0.6
- w_qkv: float32 [512, 1536], P('voc'), may hold values from -0.25 to 0.25
- w_out: float32 [512, 512], P('voc'), may hold values from -0.5 to 0.5
- w_up: float32 [512, 2048], P('voc'), may hold values from -0.25 to 0.25
- w_down: float32 [2048, 512], P('voc'), may hold values from -0.125 to 0.125
- norm_gains: float32 [3, 512], replicated, may hold values from 0.5 to 1.5
- embed_mom: bfloat16 [32000, 512], P('voc'), may hold values from -0.0019989014 to 0.0019989014
- qkv_mom: bfloat16 [512, 1536], P('voc'), may hold values from -0.0019989014 to 0.0019989014
- out_mom: bfloat16 [512, 512], P('voc'), may hold values from -0.0019989014 to 0.0019989014
- up_mom: bfloat16 [512, 2048], P('voc'), may hold values from -0.0019989014 to 0.0019989014
- down_mom: bfloat16 [2048, 512], P('voc'), may hold values from -0.0019989014 to 0.0019989014
- gain_mom: bfloat16 [3, 512], replicated, may hold values from -0.0019989014 to 0.0019989014
- embed_err: bfloat16 [8, 32000, 512], P('rep', 'voc'), may hold values from -0.0019989014 to 0.0019989014
- qkv_err: bfloat16 [8, 512, 1536], P('rep', 'voc'), may hold values from -0.0019989014 to 0.0019989014
- out_err: bfloat16 [8, 512, 512], P('rep', 'voc'), may hold values from -0.0019989014 to 0.0019989014
- up_err: bfloat16 [8, 512, 2048], P('rep', 'voc'), may hold values from -0.0019989014 to 0.0019989014
- down_err: bfloat16 [8, 2048, 512], P('rep', 'voc'), may hold values from -0.0019989014 to 0.0019989014
- embed_factor: float32 [4, 512, 8], P('voc'), may hold values from -6 to 6
- qkv_factor: float32 [4, 1536, 8], P('voc'), may hold values from -6 to 6
- out_factor: float32 [4, 512, 8], P('voc'), may hold values from -6 to 6
- up_factor: float32 [4, 2048, 8], P('voc'), may hold values from -6 to 6
- down_factor: float32 [4, 512, 8], P('voc'), may hold values from -6 to 6
Outputs:
- losses: float32 [8], P('rep')
- norms: float32 [8], P('rep')
- embed_update: float32 [32000, 512], P('voc')
- new_qkv: float32 [512, 1536], P('voc')
- new_out: float32 [512, 512], P('voc')
- new_up: float32 [512, 2048], P('voc')
- new_down: float32 [2048, 512], P('voc')
- gain_update: float32 [3, 512], replicated
- next_embed_mom: float32 [32000, 512], P('voc')
- next_qkv_mom: float32 [512, 1536], P('voc')
- next_out_mom: float32 [512, 512], P('voc')
- next_up_mom: float32 [512, 2048], P('voc')
- next_down_mom: float32 [2048, 512], P('voc')
- next_gain_mom: float32 [3, 512], replicated
- next_embed_err: float32 [8, 32000, 512], P('rep', 'voc')
- next_qkv_err: float32 [8, 512, 1536], P('rep', 'voc')
- next_out_err: float32 [8, 512, 512], P('rep', 'voc')
- next_up_err: float32 [8, 512, 2048], P('rep', 'voc')
- next_down_err: float32 [8, 2048, 512], P('rep', 'voc')
- next_embed_factor: float32 [4, 512, 8], P('voc')
- next_qkv_factor: float32 [4, 1536, 8], P('voc')
- next_out_factor: float32 [4, 512, 8], P('voc')
- next_up_factor: float32 [4, 2048, 8], P('voc')
- next_down_factor: float32 [4, 512, 8], P('voc')
All inputs are finite; a program needn't handle non-finite values.
Results may differ from a plain program's by a relative error of at most 0.009.
The roundings to bfloat16 on the way count: a program that leaves them out, or rounds other values in their place, can miss the bound.
Values may be sent and summed in bfloat16 or wider, within the bound.
A program may use at most 320 MiB of HBM per device.

v0:
```python
import jax
import jax.numpy as jnp
from jax import lax
from jax.sharding import PartitionSpec as P

HEADS = 8
HD = 64


HIGHEST_PREC = lax.Precision.HIGHEST
MOMENTUM = 0.9
LEARN_RATE = 10.0
CLIP_NORM = 1.0
ZLOSS_WEIGHT = 0.01


def rms_norm(values, weight):
    return values * lax.rsqrt(jnp.mean(values * values, axis=-1, keepdims=True) + 1e-06) * weight


def rotate(heads_in, length):
    halfway = heads_in.shape[-1] // 2
    positions = jnp.arange(length).astype(jnp.float32)
    inverse = 10000.0 ** (-jnp.arange(halfway).astype(jnp.float32) / halfway)
    angles = positions[:, None] * inverse[None, :]
    cosine_table = jnp.cos(angles)[:, None, :]
    sine_table = jnp.sin(angles)[:, None, :]
    first_half = heads_in[..., :halfway]
    second_half = heads_in[..., halfway:]
    return jnp.concatenate(
        [
            first_half * cosine_table - second_half * sine_table,
            first_half * sine_table + second_half * cosine_table,
        ],
        axis=-1,
    )


def orthonormal(matrix):
    columns = []
    for column_pos in range(matrix.shape[1]):
        vector = matrix[:, column_pos]
        for earlier in columns:
            vector = vector - jnp.sum(earlier * vector) * earlier
        vector = vector * lax.rsqrt(jnp.sum(vector * vector) + 1e-20)
        columns.append(vector)
    return jnp.stack(columns, axis=1)


def block_scores(rows_query, key_seq, first_row):
    row_count = rows_query.shape[0]
    scores = jnp.einsum(
        "qhd,khd->hqk", rows_query, key_seq, preferred_element_type=jnp.float32
    ) * HD ** (-0.5)
    causal = (first_row + jnp.arange(row_count))[:, None] >= jnp.arange(key_seq.shape[0])[None, :]
    return jnp.where(causal[None], scores, -1e30)


def attend(query_seq, key_seq, value_seq):
    length = query_seq.shape[0]
    block_len = min(512, length)
    mixed_parts, lse_parts = ([], [])
    for first_row in range(0, length, block_len):
        scores = block_scores(query_seq[first_row : first_row + block_len], key_seq, first_row)
        log_total = jax.nn.logsumexp(scores, axis=-1)
        attn_probs = jnp.exp(scores - log_total[..., None]).astype(jnp.bfloat16)
        mixed_parts.append(
            jnp.einsum("hqk,khd->qhd", attn_probs, value_seq, preferred_element_type=jnp.float32)
        )
        lse_parts.append(log_total)
    return (jnp.concatenate(mixed_parts, axis=0), jnp.concatenate(lse_parts, axis=1))


def attend_back(query_seq, key_seq, value_seq, lse_seq, grad_mixed):
    length = query_seq.shape[0]
    block_len = min(512, length)
    grad_query_parts = []
    grad_key = jnp.zeros(key_seq.shape, jnp.float32)
    grad_value = jnp.zeros(value_seq.shape, jnp.float32)
    for first_row in range(0, length, block_len):
        rows_query = query_seq[first_row : first_row + block_len]
        rows_grad = grad_mixed[first_row : first_row + block_len]
        scores = block_scores(rows_query, key_seq, first_row)
        attn_probs = jnp.exp(scores - lse_seq[:, first_row : first_row + block_len, None])
        grad_probs = jnp.einsum(
            "qhd,khd->hqk", rows_grad, value_seq, preferred_element_type=jnp.float32
        )
        row_delta = jnp.sum(attn_probs * grad_probs, axis=-1, keepdims=True)
        grad_scores = (attn_probs * (grad_probs - row_delta)).astype(jnp.bfloat16)
        grad_query_parts.append(
            jnp.einsum("hqk,khd->qhd", grad_scores, key_seq, preferred_element_type=jnp.float32)
            * HD ** (-0.5)
        )
        grad_key = grad_key + jnp.einsum(
            "hqk,qhd->khd", grad_scores, rows_query, preferred_element_type=jnp.float32
        ) * HD ** (-0.5)
        grad_value = grad_value + jnp.einsum(
            "hqk,qhd->khd",
            attn_probs.astype(jnp.bfloat16),
            rows_grad,
            preferred_element_type=jnp.float32,
        )
    return (jnp.concatenate(grad_query_parts, axis=0), grad_key, grad_value)


def layer_forward(stream_in, norm_gains, projections, seq_count, length):
    proj_qkv, proj_out, proj_up, proj_down = projections
    tok_count = seq_count * length
    normed_in = rms_norm(stream_in, norm_gains[0]).astype(jnp.bfloat16)
    packed = jnp.dot(normed_in, proj_qkv, preferred_element_type=jnp.float32).reshape(
        seq_count, length, 3, HEADS, HD
    )
    query_list, key_list, value_list, mixed_list, lse_list = ([], [], [], [], [])
    query_seq = rotate(packed[0, :, 0], length).astype(jnp.bfloat16)
    key_seq = rotate(packed[0, :, 1], length).astype(jnp.bfloat16)
    value_seq = packed[0, :, 2].astype(jnp.bfloat16)
    mixed_seq, lse_seq = attend(query_seq, key_seq, value_seq)
    query_list.append(query_seq)
    key_list.append(key_seq)
    value_list.append(value_seq)
    mixed_list.append(mixed_seq)
    lse_list.append(lse_seq)
    mixed = jnp.stack(mixed_list).reshape(tok_count, HEADS * HD).astype(jnp.bfloat16)
    stream_mid = stream_in + jnp.dot(mixed, proj_out, preferred_element_type=jnp.float32)
    normed_mid = rms_norm(stream_mid, norm_gains[1]).astype(jnp.bfloat16)
    hidden = jnp.dot(normed_mid, proj_up, preferred_element_type=jnp.float32)
    active = jax.nn.gelu(hidden, approximate=False).astype(jnp.bfloat16)
    stream_out = stream_mid + jnp.dot(active, proj_down, preferred_element_type=jnp.float32)
    kept = (
        stream_in,
        stream_mid,
        normed_in,
        query_list,
        key_list,
        value_list,
        lse_list,
        mixed,
        normed_mid,
        hidden,
        active,
    )
    return (stream_out, kept)


def layer_backward(grad_out, kept, norm_gains, projections, seq_count, length):
    proj_qkv, proj_out, proj_up, proj_down = projections
    (
        stream_in,
        stream_mid,
        normed_in,
        query_list,
        key_list,
        value_list,
        lse_list,
        mixed,
        normed_mid,
        hidden,
        active,
    ) = kept
    tok_count = seq_count * length
    grad_branch = grad_out.astype(jnp.bfloat16)
    grad_down = jnp.einsum("tf,td->fd", active, grad_branch, preferred_element_type=jnp.float32)
    grad_active = jnp.einsum(
        "td,fd->tf", grad_branch, proj_down, preferred_element_type=jnp.float32
    )
    gelu_pull = jax.vjp(lambda pre_act: jax.nn.gelu(pre_act, approximate=False), hidden)[1]
    grad_hidden = gelu_pull(grad_active)[0].astype(jnp.bfloat16)
    grad_up = jnp.einsum("td,tf->df", normed_mid, grad_hidden, preferred_element_type=jnp.float32)
    grad_normed_mid = jnp.einsum(
        "tf,df->td", grad_hidden, proj_up, preferred_element_type=jnp.float32
    )
    grad_mid_part, grad_gain_mid = jax.vjp(rms_norm, stream_mid, norm_gains[1])[1](grad_normed_mid)
    grad_mid = grad_out + grad_mid_part
    grad_attn = grad_mid.astype(jnp.bfloat16)
    grad_outproj = jnp.einsum("tc,td->cd", mixed, grad_attn, preferred_element_type=jnp.float32)
    grad_mixed = jnp.einsum("td,cd->tc", grad_attn, proj_out, preferred_element_type=jnp.float32)
    grad_mixed = grad_mixed.astype(jnp.bfloat16).reshape(seq_count, length, HEADS, HD)
    grad_query, grad_key, grad_value = attend_back(
        query_list[0], key_list[0], value_list[0], lse_list[0], grad_mixed[0]
    )
    unrotate = jax.vjp(lambda heads_in: rotate(heads_in, length), grad_query)[1]
    packed_grads = [jnp.stack([unrotate(grad_query)[0], unrotate(grad_key)[0], grad_value], axis=1)]
    grad_packed = jnp.stack(packed_grads).reshape(tok_count, 3 * HEADS * HD).astype(jnp.bfloat16)
    grad_qkv = jnp.einsum("td,tc->dc", normed_in, grad_packed, preferred_element_type=jnp.float32)
    grad_normed_in = jnp.einsum(
        "tc,dc->td", grad_packed, proj_qkv, preferred_element_type=jnp.float32
    )
    grad_in_part, grad_gain_in = jax.vjp(rms_norm, stream_in, norm_gains[0])[1](grad_normed_in)
    return (
        grad_mid + grad_in_part,
        (grad_qkv, grad_outproj, grad_up, grad_down),
        (grad_gain_in, grad_gain_mid),
    )


def body(
    token_ids,
    target_ids,
    embedding,
    w_qkv,
    w_out,
    w_up,
    w_down,
    norm_gains,
    embed_mom,
    qkv_mom,
    out_mom,
    up_mom,
    down_mom,
    gain_mom,
    embed_err,
    qkv_err,
    out_err,
    up_err,
    down_err,
    embed_factor,
    qkv_factor,
    out_factor,
    up_factor,
    down_factor,
):
    seq_count, length = token_ids.shape
    tok_count = seq_count * length
    vocab_rows = embedding.shape[0]
    shard_pos = lax.axis_index("voc")
    workers = lax.axis_size("rep")
    vocab_table = embedding.astype(jnp.bfloat16)
    slices = (w_qkv, w_out, w_up, w_down)
    projections = (
        lax.all_gather(w_qkv.astype(jnp.bfloat16), "voc", axis=0, tiled=True),
        lax.all_gather(w_out.astype(jnp.bfloat16), "voc", axis=0, tiled=True),
        lax.all_gather(w_up.astype(jnp.bfloat16), "voc", axis=0, tiled=True),
        lax.all_gather(w_down.astype(jnp.bfloat16), "voc", axis=0, tiled=True),
    )
    local_ids = token_ids.reshape(-1) - shard_pos * vocab_rows
    inside = (local_ids >= 0) & (local_ids < vocab_rows)
    safe_ids = jnp.clip(local_ids, 0, vocab_rows - 1)
    own_rows = jnp.where(inside[:, None], vocab_table[safe_ids].astype(jnp.float32), 0.0)
    stream_in = lax.psum(own_rows.astype(jnp.bfloat16), "voc").astype(jnp.float32)
    stream_out, kept = layer_forward(stream_in, norm_gains, projections, seq_count, length)
    normed_out = rms_norm(stream_out, norm_gains[2]).astype(jnp.bfloat16)
    logits = jnp.einsum("td,vd->tv", normed_out, vocab_table, preferred_element_type=jnp.float32)
    local_targets = target_ids.reshape(-1) - shard_pos * vocab_rows
    target_hit = jnp.arange(vocab_rows)[None, :] == local_targets[:, None]
    picked_local = jnp.sum(jnp.where(target_hit, logits, 0.0), axis=-1)
    local_top = jnp.max(logits, axis=-1)
    top_all = lax.pmax(local_top, "voc")
    total_all, picked = lax.psum(
        (jnp.sum(jnp.exp(logits - top_all[:, None]), axis=-1), picked_local), "voc"
    )
    partition = top_all + jnp.log(total_all)
    loss_value = jnp.mean(partition - picked) + ZLOSS_WEIGHT * jnp.mean(partition * partition)
    soft_probs = jnp.exp(logits - partition[:, None])
    grad_logits = (
        (
            soft_probs * (1.0 + 2.0 * ZLOSS_WEIGHT * partition)[:, None]
            - target_hit.astype(jnp.float32)
        )
        / tok_count
    ).astype(jnp.bfloat16)
    grad_table_head = jnp.einsum(
        "tv,td->vd", grad_logits, normed_out, preferred_element_type=jnp.float32
    )
    hidden_terms = jnp.dot(grad_logits, vocab_table, preferred_element_type=jnp.float32)
    grad_normed_out = lax.psum(hidden_terms, "voc")
    grad_stream, grad_gain_out = jax.vjp(rms_norm, stream_out, norm_gains[2])[1](grad_normed_out)
    grad_in, grad_mats, gain_pair = layer_backward(
        grad_stream, kept, norm_gains, projections, seq_count, length
    )
    lookup_grad = (
        jnp.zeros(embedding.shape, jnp.float32)
        .at[safe_ids]
        .add(jnp.where(inside[:, None], grad_in, 0.0))
    )
    grad_gains = jnp.stack([gain_pair[0], gain_pair[1], grad_gain_out])
    own_grads = [grad_table_head + lookup_grad] + [
        lax.dynamic_slice_in_dim(full_grad, shard_pos * own_slice.shape[0], own_slice.shape[0], 0)
        for full_grad, own_slice in zip(grad_mats, slices)
    ]
    squares = sum((jnp.sum(grad_part * grad_part) for grad_part in own_grads))
    squares = squares + jnp.where(shard_pos == 0, jnp.sum(grad_gains * grad_gains), 0.0)
    total_norm = jnp.sqrt(lax.psum(squares, "voc"))
    clip_factor = jnp.minimum(1.0, CLIP_NORM / total_norm)
    errors = (embed_err, qkv_err, out_err, up_err, down_err)
    starts = (embed_factor, qkv_factor, out_factor, up_factor, down_factor)
    matrices = [
        clip_factor * grad_part + error_in[0].astype(jnp.float32)
        for grad_part, error_in in zip(own_grads, errors)
    ]
    lefts = [
        jnp.dot(matrix, start_in[0], precision=HIGHEST_PREC)
        for matrix, start_in in zip(matrices, starts)
    ]
    left_sums = lax.psum(
        (lefts[0], lefts[1], lefts[2], lefts[3], lefts[4], clip_factor * grad_gains), "rep"
    )
    bases = [orthonormal(left_sum) for left_sum in left_sums[:5]]
    rights = [
        jnp.einsum("rc,rk->ck", matrix, basis, precision=HIGHEST_PREC)
        for matrix, basis in zip(matrices, bases)
    ]
    right_sums = (
        lax.psum(rights[0].astype(jnp.bfloat16), "rep").astype(jnp.float32),
        lax.psum(rights[1].astype(jnp.bfloat16), "rep").astype(jnp.float32),
        lax.psum(rights[2].astype(jnp.bfloat16), "rep").astype(jnp.float32),
        lax.psum(rights[3].astype(jnp.bfloat16), "rep").astype(jnp.float32),
        lax.psum(rights[4].astype(jnp.bfloat16), "rep").astype(jnp.float32),
    )
    right_means = [right_sum / workers for right_sum in right_sums]
    weights_all = (embedding, w_qkv, w_out, w_up, w_down)
    moments = (embed_mom, qkv_mom, out_mom, up_mom, down_mom)
    new_weights, new_moments, new_errors, changes = ([], [], [], [])
    for member in range(5):
        mean_grad = jnp.dot(bases[member], right_means[member].T, precision=HIGHEST_PREC)
        projected = jnp.einsum("rk,rc->kc", bases[member], matrices[member], precision=HIGHEST_PREC)
        new_errors.append(
            (matrices[member] - jnp.dot(bases[member], projected, precision=HIGHEST_PREC))[None]
        )
        new_momentum = MOMENTUM * moments[member].astype(jnp.float32) + mean_grad
        new_moments.append(new_momentum)
        change = -LEARN_RATE * new_momentum
        changes.append(change)
        new_weights.append(weights_all[member] + change)
    next_gain_mom = MOMENTUM * gain_mom.astype(jnp.float32) + left_sums[5] / workers
    gain_change = -LEARN_RATE * next_gain_mom
    return (
        loss_value.reshape(1),
        total_norm.reshape(1),
        changes[0],
        new_weights[1],
        new_weights[2],
        new_weights[3],
        new_weights[4],
        gain_change,
        new_moments[0],
        new_moments[1],
        new_moments[2],
        new_moments[3],
        new_moments[4],
        next_gain_mom,
        new_errors[0],
        new_errors[1],
        new_errors[2],
        new_errors[3],
        new_errors[4],
        right_means[0][None],
        right_means[1][None],
        right_means[2][None],
        right_means[3][None],
        right_means[4][None],
    )


def solution(mesh):
    in_specs = (
        P("rep", None),
        P("rep", None),
        P("voc", None),
        P("voc", None),
        P("voc", None),
        P("voc", None),
        P("voc", None),
        P(),
        P("voc", None),
        P("voc", None),
        P("voc", None),
        P("voc", None),
        P("voc", None),
        P(),
        P("rep", "voc", None),
        P("rep", "voc", None),
        P("rep", "voc", None),
        P("rep", "voc", None),
        P("rep", "voc", None),
        P("voc", None, None),
        P("voc", None, None),
        P("voc", None, None),
        P("voc", None, None),
        P("voc", None, None),
    )
    out_specs = (
        P("rep"),
        P("rep"),
        P("voc", None),
        P("voc", None),
        P("voc", None),
        P("voc", None),
        P("voc", None),
        P(),
        P("voc", None),
        P("voc", None),
        P("voc", None),
        P("voc", None),
        P("voc", None),
        P(),
        P("rep", "voc", None),
        P("rep", "voc", None),
        P("rep", "voc", None),
        P("rep", "voc", None),
        P("rep", "voc", None),
        P("voc", None, None),
        P("voc", None, None),
        P("voc", None, None),
        P("voc", None, None),
        P("voc", None, None),
    )
    return jax.shard_map(body, mesh=mesh, in_specs=in_specs, out_specs=out_specs, check_vma=False)
```

profile of v0, /device:TPU:0, one launch (start us, length us, event | category | flops | bytes accessed | tf_op | source)
XLA Modules:
  0.0 1057.6 jit_solution(10563401274349962907)
XLA Ops:
  8.7 8.8 convert_element_type.238
  17.6 8.5 gather_fusion
  34.5 11.0 %all_gather.13 = bf16[512,512]{1,0:T(8,128)(2,1)S(1)} all-gather(bf16[128,512]{1,0:T(8,128)(2,1)S(1)} %convert_element_type.250), channel_id=1, replica_groups=mesh['rep'=8,'voc'=4] {'voc'}, dimensions={0}, use_global_device_ids=true | all-gather | bytes 655360 | tf_op jit(solution)/shard_map/all_gather | solution.py:231
  46.0 25.2 %all-reduce.12.cloned.1.call-done = bf16[1024,512]{0,1:T(8,128)(2,1)} async-done(((bf16[1024,512]{0,1:T(8,128)(2,1)}), bf16[1024,512]{0,1:T(8,128)(2,1)}) %all-reduce.12.cloned.1.call-update) | async-done | bytes 1048592 | tf_op jit(solution)/shard_map/psum | solution.py:239
  72.7 20.8 %all-gather.4.cloned.1.call-done = bf16[512,1536]{1,0:T(8,128)(2,1)} async-done(((bf16[128,1536]{1,0:T(8,128)(2,1)}), bf16[512,1536]{1,0:T(8,128)(2,1)}) %all-gather.4.cloned.1.call-update) | async-done | bytes 1572880 | tf_op jit(solution)/shard_map/all_gather | solution.py:230
  108.8 6.1 fusion.25
  123.8 6.2 fusion.26
  131.7 24.2 %multiply_convert_fusion.3 = (bf16[1024,2048]{1,0:T(8,128)(2,1)}, f32[1024,2048]{1,0:T(8,128)}, f32[1024,2048]{1,0:T(8,128)}) fusion(bf16[512,2048]{1,0:T(8,128)(2,1)} %all-gather.6.cloned.1.call-done, f32[1024,512]{0,1:T(8,128)S(1)} %get-tuple-element.389, f32[512]{0:T(512)S(1)} %bitcast.500, f32[1024]{0:T(1024)S(1)} %fusion.66), kind=kOutput, calls=%fused_computation.27 | convolution fusion | flops 2285371392 | bytes 25171968 | tf_op jit(solution)/shard_map/dot_general | solution.py:126
  155.9 5.8 multiply_reduce_fusion.7
  161.7 18.4 %fusion.120 = (f32[1024]{0:T(1024)S(1)}, f32[1024,8000]{0,1:T(8,128)}) fusion(bf16[8000,512]{1,0:T(8,128)(2,1)} %convert_element_type.238, f32[1024,512]{0,1:T(8,128)S(1)} %get-tuple-element.392, f32[512]{0:T(512)S(1)} %bitcast.483, f32[1024]{0:T(1024)S(1)} %fusion.67), kind=kOutput, calls=%fused_computation.653 | convolution fusion | flops 8398371840 | bytes 43067392 | tf_op jit(solution)/shard_map/td,vd->tv/dot_general | solution.py:242
  180.1 6.0 pmax.7
  186.1 15.6 %select_reduce_fusion = (f32[1024]{0:T(1024)}, f32[1024]{0:T(1024)S(1)}) fusion(f32[1024,8000]{0,1:T(8,128)} %get-tuple-element.394, s32[1024]{0:T(1024)S(1)} %bitcast.489, f32[1024]{0:T(1024)S(1)} %pmax.7), kind=kLoop, calls=%fused_computation.3 | loop fusion | flops 40957952 | bytes 32784384 | tf_op jit(solution)/shard_map/reduce_sum | solution.py:245
  201.7 5.6 psum.113
  207.3 25.1 %fusion.114 = f32[1024,512]{0,1:T(8,128)} fusion(bf16[8000,512]{1,0:T(8,128)(2,1)} %convert_element_type.238, f32[1024,8000]{0,1:T(8,128)} %get-tuple-element.394, f32[1024]{0:T(1024)S(1)} %get-tuple-element.351, f32[1024]{0:T(1024)S(1)} %get-tuple-element.352, s32[1024]{0:T(1024)S(1)} %bitcast.490), kind=kOutput, calls=%fused_computation.648 | convolution fusion | flops 8445952000 | bytes 43069440 | tf_op jit(solution)/shard_map/dot_general | solution.py:264
  232.5 21.1 %fusion.108 = f32[8000,512]{1,0:T(8,128)} fusion(f32[1024,512]{0,1:T(8,128)S(1)} %get-tuple-element.392, f32[512]{0:T(512)S(1)} %bitcast.484, f32[1024]{0:T(1024)S(1)} %fusion.67, f32[1024,8000]{0,1:T(8,128)} %get-tuple-element.394, f32[1024]{0:T(1024)S(1)} %get-tuple-element.351, f32[1024]{0:T(1024)S(1)} %get-tuple-element.352, s32[1024]{0:T(1024)S(1)} %bitcast.491), kind=kOutput, calls=%fused_computation.642 | convolution fusion | flops 8447524864 | bytes 51267584 | tf_op jit(solution)/shard_map/tv,td->vd/dot_general | solution.py:261
  253.6 31.3 %all-reduce.14.cloned.1.call-done = f32[1024,512]{0,1:T(8,128)} async-done(((f32[1024,512]{0,1:T(8,128)}), f32[1024,512]{0,1:T(8,128)}) %all-reduce.14.cloned.1.call-update) | async-done | bytes 2097168 | tf_op jit(solution)/shard_map/psum | solution.py:265
  289.8 9.7 add_convert_fusion
  306.4 13.2 %multiply_reduce_fusion.1 = (f32[8,512]{1,0:T(8,128)S(1)}, f32[8,512,1024]{2,1,0:T(8,128)}) fusion(f32[8,512,1024]{2,1,0:T(8,128)} %copy-done.2, f32[8,512]{1,0:T(8,128)S(1)} %copy-done.54, pred[512,1024]{1,0:T(8,128)(4,1)S(1)} %copy-done.14, bf16[512,8,64]{0,2,1:T(8,128)(2,1)S(1)} %bitcast.452, f32[1,1024,3,8,64]{1,4,3,2,0:T(8,128)} %bitcast.444), kind=kOutput, calls=%fused_computation.9 | convolution fusion | flops 557838336 | bytes 35684352 | tf_op jit(solution)/shard_map/qhd,khd->hqk/dot_general | solution.py:85
  319.6 12.9 %multiply_convert_fusion.2 = bf16[8,512,1024]{2,1,0:T(8,128)(2,1)S(1)} fusion(f32[8,512,1024]{2,1,0:T(8,128)} %get-tuple-element.399, f32[8,512,1024]{2,1,0:T(8,128)} %copy-done.2, f32[8,512]{1,0:T(8,128)S(1)} %get-tuple-element.398, f32[8,512]{1,0:T(8,128)S(1)} %copy-done.54, pred[512,1024]{1,0:T(8,128)(4,1)S(1)} %copy-done.14), kind=kLoop, calls=%fused_computation.8 | loop fusion | flops 25165824 | bytes 42500096 | tf_op jit(solution)/shard_map/convert_element_type | solution.py:89
  335.6 4.8 fusion.24
  340.5 6.8 fusion.98
  358.1 13.0 %multiply_reduce_fusion = (f32[8,512]{1,0:T(8,128)S(1)}, f32[8,512,1024]{2,1,0:T(8,128)}) fusion(f32[8,512,1024]{2,1,0:T(8,128)} %copy-done.1, f32[8,512]{1,0:T(8,128)S(1)} %copy-done.52, pred[512,1024]{1,0:T(8,128)(4,1)S(1)} %copy-done.6, bf16[512,8,64]{0,2,1:T(8,128)(2,1)S(1)} %bitcast.451, f32[1,1024,3,8,64]{1,4,3,2,0:T(8,128)} %bitcast.445), kind=kOutput, calls=%fused_computation.7 | convolution fusion | flops 557838336 | bytes 35684352 | tf_op jit(solution)/shard_map/qhd,khd->hqk/dot_general | solution.py:85
  371.1 12.5 %multiply_convert_fusion.1 = bf16[8,512,1024]{2,1,0:T(8,128)(2,1)S(1)} fusion(f32[8,512,1024]{2,1,0:T(8,128)} %get-tuple-element.397, f32[8,512,1024]{2,1,0:T(8,128)} %copy-done.1, f32[8,512]{1,0:T(8,128)S(1)} %get-tuple-element.396, f32[8,512]{1,0:T(8,128)S(1)} %copy-done.52, pred[512,1024]{1,0:T(8,128)(4,1)S(1)} %copy-done.6), kind=kLoop, calls=%fused_computation.6 | loop fusion | flops 25165824 | bytes 42500096 | tf_op jit(solution)/shard_map/convert_element_type | solution.py:89
  387.3 5.0 multiply_bitcast_fusion
  392.3 7.1 fusion.21
  413.7 18.7 %scatter_fusion = f32[8000,512]{1,0:T(8,128)} fusion(f32[8000,512]{1,0:T(8,128)} %fusion.108, s32[1024]{0:T(1024)S(1)} %bitcast.461, f32[1024,512]{1,0:T(8,128)S(1)} %copy.62), kind=kCustom, calls=%fused_computation.1 | custom fusion | flops 524288 | bytes 6295552 | tf_op jit(solution)/shard_map/scatter-add | solution.py:273
  432.5 10.6 %multiply_reduce_fusion.2 = f32[]{:T(128)} fusion(f32[8000,512]{1,0:T(8,128)} %scatter_fusion), kind=kLoop, calls=%fused_computation.19 | loop fusion | flops 8191999 | bytes 16384004 | tf_op jit(solution)/shard_map/reduce_sum | solution.py:280
  450.4 6.4 all-reduce.5
  464.3 38.0 %all-reduce.4 = (f32[128,8]{0,1:T(8,128)S(1)}, f32[128,8]{0,1:T(8,128)S(1)}, f32[128,8]{0,1:T(8,128)S(1)}, f32[512,8]{0,1:T(8,128)S(1)}, f32[3,512]{1,0:T(4,128)S(1)}) all-reduce(f32[128,8]{0,1:T(8,128)S(1)} %fusion.47, f32[128,8]{0,1:T(8,128)S(1)} %fusion.54, f32[128,8]{0,1:T(8,128)S(1)} %fusion.44, ...), channel_id=1, replica_groups=mesh['rep'=8,'voc'=4] {'rep'}, use_global_device_ids=true, to_apply=%region_71.72 | all-reduce | flops 8704 | bytes 69632 | tf_op jit(solution)/shard_map/psum | solution.py:294
  506.1 5.1 multiply_reduce_fusion.57
  515.8 6.4 multiply_reduce_fusion.56
  545.5 17.8 %subtract_multiply_fusion.7 = (f32[512,1]{0,1:T(1,128)S(1)}, f32[512,1]{0,1:T(1,128)S(1)}, f32[512,1]{0,1:T(1,128)S(1)}, f32[512,1]{0,1:T(1,128)S(1)}, f32[512,1...) fusion(f32[512,1]{0,1:T(1,128)S(1)} %get-tuple-element.372, f32[]{:T(128)S(6)} %rsqrt.195, ...), kind=kLoop, calls=%fused_computation.282 | loop fusion | flops 32256 | bytes 30860 | tf_op jit(solution)/shard_map/mul | solution.py:45
  587.5 5.1 multiply_reduce_fusion.120
  607.5 17.7 %subtract_multiply_fusion.21 = (f32[128,1]{0,1:T(1,128)S(1)}, f32[128,1]{0,1:T(1,128)S(1)}, f32[128,1]{0,1:T(1,128)S(1)}, f32[128,1]{0,1:T(1,128)S(1)}, f32[128,...) fusion(f32[128,1]{0,1:T(1,128)S(1)} %get-tuple-element.286, f32[]{:T(128)S(6)} %rsqrt.179, ...), kind=kLoop, calls=%fused_computation.499 | loop fusion | flops 8064 | bytes 7820 | tf_op jit(solution)/shard_map/mul | solution.py:45
  646.2 5.2 multiply_reduce_fusion.149
  666.4 17.7 %subtract_multiply_fusion.28 = (f32[128,1]{0,1:T(1,128)S(1)}, f32[128,1]{0,1:T(1,128)S(1)}, f32[128,1]{0,1:T(1,128)S(1)}, f32[128,1]{0,1:T(1,128)S(1)}, f32[128,...) fusion(f32[128,1]{0,1:T(1,128)S(1)} %get-tuple-element.320, f32[]{:T(128)S(6)} %rsqrt.171, ...), kind=kLoop, calls=%fused_computation.555 | loop fusion | flops 8064 | bytes 7820 | tf_op jit(solution)/shard_map/mul | solution.py:45
  711.4 5.3 multiply_reduce_fusion.91
  731.7 17.6 %subtract_multiply_fusion.14 = (f32[128,1]{0,1:T(1,128)S(1)}, f32[128,1]{0,1:T(1,128)S(1)}, f32[128,1]{0,1:T(1,128)S(1)}, f32[128,1]{0,1:T(1,128)S(1)}, f32[128,...) fusion(f32[128,1]{0,1:T(1,128)S(1)} %get-tuple-element.252, f32[]{:T(128)S(6)} %rsqrt.187, ...), kind=kLoop, calls=%fused_computation.443 | loop fusion | flops 8064 | bytes 7820 | tf_op jit(solution)/shard_map/mul | solution.py:45
  758.5 20.7 %fusion.56 = f32[8000,8]{0,1:T(8,128)} fusion(f32[1,512,8]{1,2,0:T(8,128)S(1)} %copy-done.74, f32[8000,512]{1,0:T(8,128)} %scatter_fusion, bf16[1,8000,512]{2,1,0:T(8,128)(2,1)} %param.38, f32[]{:T(128)S(6)} %min.16), kind=kOutput, calls=%fused_computation.245 | convolution fusion | flops 405504000 | bytes 24848388 | tf_op jit(solution)/shard_map/dot_general | solution.py:291
  784.4 62.0 %all-reduce.16.cloned.1.call-done = f32[8000,8]{0,1:T(8,128)} async-done(((f32[8000,8]{0,1:T(8,128)}), f32[8000,8]{0,1:T(8,128)}) %all-reduce.16.cloned.1.call-update) | async-done | bytes 256016 | tf_op jit(solution)/shard_map/psum | solution.py:294
  854.1 5.2 multiply_reduce_fusion.19
  861.7 7.1 multiply_reduce_fusion.18
  891.4 20.4 %subtract_multiply_fusion = (f32[8000,1]{0,1:T(1,128)S(1)}, f32[8000,1]{0,1:T(1,128)S(1)}, f32[8000,1]{0,1:T(1,128)S(1)}, f32[8000,1]{0,1:T(1,128)S(1)}, f32[800...) fusion(f32[8000,1]{0,1:T(1,128)S(1)} %get-tuple-element.350, ...), kind=kLoop, calls=%fused_computation.223 | loop fusion | flops 504000 | bytes 480140 | tf_op jit(solution)/shard_map/mul | solution.py:45
  912.2 12.8 %fusion.113 = f32[8,512]{1,0:T(8,128)S(1)} fusion(f32[8000,8]{0,1:T(8,128)S(1)} %stack.29, f32[8000,512]{1,0:T(8,128)} %scatter_fusion, bf16[1,8000,512]{2,1,0:T(8,128)(2,1)} %param.38, f32[]{:T(128)S(6)} %min.16), kind=kOutput, calls=%fused_computation.647 | convolution fusion | flops 405504000 | bytes 24848388 | tf_op jit(solution)/shard_map/rk,rc->kc/dot_general | solution.py:315
  925.0 15.5 %convolution_convert_fusion.7 = bf16[512,8]{0,1:T(8,128)(2,1)} fusion(f32[8000,8]{0,1:T(8,128)S(1)} %stack.29, f32[8000,512]{1,0:T(8,128)} %scatter_fusion, bf16[1,8000,512]{2,1,0:T(8,128)(2,1)} %param.38, f32[]{:T(128)S(6)} %min.16), kind=kOutput, calls=%fused_computation.107 | convolution fusion | flops 405508096 | bytes 24840196 | tf_op jit(solution)/shard_map/rc,rk->ck/dot_general | solution.py:299
  940.5 21.1 %subtract_bitcast_fusion = f32[1,8000,512]{2,1,0:T(8,128)} fusion(f32[8000,8]{0,1:T(8,128)S(1)} %stack.29, f32[8,512]{1,0:T(8,128)S(1)} %fusion.113, bf16[1,8000,512]{2,1,0:T(8,128)(2,1)} %param.38, f32[8000,512]{1,0:T(8,128)} %scatter_fusion, f32[]{:T(128)S(6)} %min.16), kind=kOutput, calls=%fused_computation.17 | convolution fusion | flops 409600000 | bytes 41232388 | tf_op jit(solution)/shard_map/dot_general | solution.py:317
  961.7 49.4 %all-reduce.18.cloned.1.call-done = (bf16[512,8]{0,1:T(8,128)(2,1)}, bf16[1536,8]{0,1:T(8,128)(2,1)}, bf16[512,8]{0,1:T(8,128)(2,1)}, bf16[2048,8]{0,1:T(8,128)(2,1)}, bf16[512,8]{0,1:T(8,128)(2,1)}) async-done(((bf16[512,8]{0,1:T(8,128)(2,1)}, bf16[1536,8]{0,1:T(8,128)(2,1)}, bf16[512,8]{0,1:T(8,128)(2,1)}, bf16[2048,8]{0,1:T(8,128)(2,1)}, bf16[512,8]{0,1:T(8,128)(2,1)}), (bf16[512,8]{0,1:T(8,128)(2,1)}, ...) | async-done | bytes 81936 | tf_op jit(solution)/shard_map/psum | solution.py:303
  1027.7 20.6 %broadcast_multiply_fusion = (f32[8000,512]{1,0:T(8,128)}, f32[8000,512]{1,0:T(8,128)}) fusion(f32[8000,8]{0,1:T(8,128)S(1)} %stack.29, bf16[512,8]{0,1:T(8,128)(2,1)S(1)} %copy-done.63, bf16[8000,512]{1,0:T(8,128)(2,1)} %param.32), kind=kOutput, calls=%fused_computation.41 | convolution fusion | flops 409608192 | bytes 41224192 | tf_op jit(solution)/shard_map/dot_general | solution.py:314
  (380 shorter events, 275.8 us)
Async XLA Ops:
  7.2 452.6 %copy-start = (f32[1,2048,8]{1,2,0:T(8,128)S(1)}, f32[1,2048,8]{1,2,0:T(8,128)}, u32[]{:S(2)}) copy-start(f32[1,2048,8]{1,2,0:T(8,128)} %param.46) | copy-start | bytes 196612
  7.2 64.0 %all-reduce.12.cloned.1.call-start = ((), (), s32[]{:S(2)}) async-start(), calls=%async_computation | async-start | bytes 2097152 | tf_op jit(solution)/shard_map/psum | solution.py:239
  8.7 18.7 %copy-start.75 = (pred[1024]{0:T(1024)(128)(4,1)}, pred[1024]{0:T(1024)(128)(4,1)S(1)}, u32[]{:S(2)}) copy-start(pred[1024]{0:T(1024)(128)(4,1)S(1)} %and_reduce_fusion) | copy-start | bytes 3076
  17.6 16.5 %copy-start.82 = (f32[3,512]{1,0:T(4,128)S(1)}, f32[3,512]{1,0:T(4,128)}, u32[]{:S(2)}) copy-start(f32[3,512]{1,0:T(4,128)} %param.31) | copy-start | bytes 18436
  26.1 19.4 %copy-start.84 = (s32[1,1024]{1,0:T(1,128)S(1)}, s32[1,1024]{1,0:T(1,128)}, u32[]{:S(2)}) copy-start(s32[1,1024]{1,0:T(1,128)} %param.25) | copy-start | bytes 12292
  29.9 63.6 %all-gather.4.cloned.1.call-start = ((), (), s32[]{:S(2)}) async-start(), calls=%async_computation.1 | async-start | bytes 1966080 | tf_op jit(solution)/shard_map/all_gather | solution.py:230
  31.9 99.8 %all-gather.6.cloned.1.call-start = ((), (), s32[]{:S(2)}) async-start(), calls=%async_computation.2 | async-start | bytes 2621440 | tf_op jit(solution)/shard_map/all_gather | solution.py:232
  32.8 123.0 %all-gather.8.cloned.1.call-start = ((), (), s32[]{:S(2)}) async-start(), calls=%async_computation.3 | async-start | bytes 2621440 | tf_op jit(solution)/shard_map/all_gather | solution.py:233
  33.8 251.1 %all-reduce.14.cloned.1.call-start = ((), (), s32[]{:S(2)}) async-start(), calls=%async_computation.4 | async-start | bytes 4194304 | tf_op jit(solution)/shard_map/psum | solution.py:265
  34.0 73.5 %copy-start.13 = (pred[512,1024]{1,0:T(8,128)(4,1)}, pred[512,1024]{1,0:T(8,128)(4,1)S(1)}, u32[]{:S(2)}) copy-start(pred[512,1024]{1,0:T(8,128)(4,1)S(1)} %iota_compare_fusion.2) | copy-start | bytes 1572868
  34.0 63.7 %copy-start.77 = (f32[1,512]{1,0:T(1,128)}, f32[1,512]{1,0:T(1,128)S(1)}, u32[]{:S(2)}) copy-start(f32[1,512]{1,0:T(1,128)S(1)} %get-tuple-element.380) | copy-start | bytes 6148
  34.1 268.9 %copy-start.80 = (f32[1,512]{1,0:T(1,128)}, f32[1,512]{1,0:T(1,128)S(1)}, u32[]{:S(2)}) copy-start(f32[1,512]{1,0:T(1,128)S(1)} %get-tuple-element.381) | copy-start | bytes 6148
  34.4 88.0 %copy-start.5 = (pred[512,1024]{1,0:T(8,128)(4,1)}, pred[512,1024]{1,0:T(8,128)(4,1)S(1)}, u32[]{:S(2)}) copy-start(pred[512,1024]{1,0:T(8,128)(4,1)S(1)} %iota_compare_fusion.1) | copy-start | bytes 1572868
  45.5 84.7 %copy-start.33 = (bf16[512,512]{1,0:T(8,128)(2,1)}, bf16[512,512]{1,0:T(8,128)(2,1)S(1)}, u32[]{:S(2)}) copy-start(bf16[512,512]{1,0:T(8,128)(2,1)S(1)} %all_gather.13) | copy-start | bytes 1572868
  46.0 51.7 %copy-start.45 = (f32[1024,32]{0,1:T(8,128)}, f32[1024,32]{0,1:T(8,128)S(1)}, u32[]{:S(2)}) copy-start(f32[1024,32]{0,1:T(8,128)S(1)} %get-tuple-element.382) | copy-start | bytes 393220
  46.0 51.7 %copy-start.46 = (f32[1024,32]{0,1:T(8,128)}, f32[1024,32]{0,1:T(8,128)S(1)}, u32[]{:S(2)}) copy-start(f32[1024,32]{0,1:T(8,128)S(1)} %get-tuple-element.383) | copy-start | bytes 393220
  72.7 25.0 %copy-start.57 = (f32[1024]{0:T(1024)}, f32[1024]{0:T(1024)S(1)}, u32[]{:S(2)}) copy-start(f32[1024]{0:T(1024)S(1)} %fusion.19) | copy-start | bytes 12292
  72.7 25.0 %copy-start.65 = (f32[1024]{0:T(1024)}, f32[1024]{0:T(1024)S(1)}, u32[]{:S(2)}) copy-start(f32[1024]{0:T(1024)S(1)} %fusion.65) | copy-start | bytes 12292
  98.5 16.4 %copy-start.15 = (bf16[1024,8,32]{0,2,1:T(8,128)(2,1)}, bf16[1024,8,32]{0,2,1:T(8,128)(2,1)S(1)}, u32[]{:S(2)}) copy-start(bf16[1024,8,32]{0,2,1:T(8,128)(2,1)S(1)} %get-tuple-element.369) | copy-start | bytes 1572868
  98.5 16.4 %copy-start.17 = (bf16[1024,8,32]{0,2,1:T(8,128)(2,1)}, bf16[1024,8,32]{0,2,1:T(8,128)(2,1)S(1)}, u32[]{:S(2)}) copy-start(bf16[1024,8,32]{0,2,1:T(8,128)(2,1)S(1)} %get-tuple-element.370) | copy-start | bytes 1572868
  98.5 16.4 %copy-start.19 = (bf16[1024,8,32]{0,2,1:T(8,128)(2,1)}, bf16[1024,8,32]{0,2,1:T(8,128)(2,1)S(1)}, u32[]{:S(2)}) copy-start(bf16[1024,8,32]{0,2,1:T(8,128)(2,1)S(1)} %get-tuple-element.361) | copy-start | bytes 1572868
  98.5 16.4 %copy-start.21 = (bf16[1024,8,32]{0,2,1:T(8,128)(2,1)}, bf16[1024,8,32]{0,2,1:T(8,128)(2,1)S(1)}, u32[]{:S(2)}) copy-start(bf16[1024,8,32]{0,2,1:T(8,128)(2,1)S(1)} %get-tuple-element.362) | copy-start | bytes 1572868
  131.1 24.8 %copy-start.27 = (f32[1024,512]{0,1:T(8,128)}, f32[1024,512]{0,1:T(8,128)S(1)}, u32[]{:S(2)}) copy-start(f32[1024,512]{0,1:T(8,128)S(1)} %get-tuple-element.389) | copy-start | bytes 6291460
  131.7 171.2 %copy-start.69 = (f32[1024]{0:T(1024)}, f32[1024]{0:T(1024)S(1)}, u32[]{:S(2)}) copy-start(f32[1024]{0:T(1024)S(1)} %fusion.66) | copy-start | bytes 12292
  207.3 25.2 %copy-start.72 = (f32[1024]{0:T(1024)}, f32[1024]{0:T(1024)S(1)}, u32[]{:S(2)}) copy-start(f32[1024]{0:T(1024)S(1)} %get-tuple-element.352) | copy-start | bytes 12292
  232.4 614.0 %all-reduce.16.cloned.1.call-start = ((), (), s32[]{:S(2)}) async-start(), calls=%async_computation.5 | async-start | bytes 516096 | tf_op jit(solution)/shard_map/psum | solution.py:294
  319.6 20.9 %slice-start.4 = ((s8[16777216]{0:T(1024)(128)(4,1)}), s8[4194304]{0:T(1024)(128)(4,1)S(1)}, s32[]{:S(2)}) async-start(s8[16777216]{0:T(1024)(128)(4,1)} %bitcast.439), calls=%async_computation.11 | async-start | bytes 8388608
  319.6 20.9 %slice-start.5 = ((s8[16777216]{0:T(1024)(128)(4,1)}), s8[4194304]{0:T(1024)(128)(4,1)S(1)}, s32[]{:S(2)}) async-start(s8[16777216]{0:T(1024)(128)(4,1)} %bitcast.439), calls=%async_computation.12 | async-start | bytes 8388608
  319.6 20.8 %slice-start.6 = ((s8[16777216]{0:T(1024)(128)(4,1)}), s8[4194304]{0:T(1024)(128)(4,1)S(1)}, s32[]{:S(2)}) async-start(s8[16777216]{0:T(1024)(128)(4,1)} %bitcast.439), calls=%async_computation.13 | async-start | bytes 8388608
  432.4 16.7 %copy-start.64 = (f32[512]{0:T(512)S(1)}, f32[512]{0:T(512)}, u32[]{:S(2)}) copy-start(f32[512]{0:T(512)} %get-tuple-element.28) | copy-start | bytes 6148
  432.4 16.7 %copy-start.79 = (f32[512]{0:T(512)S(1)}, f32[512]{0:T(512)}, u32[]{:S(2)}) copy-start(f32[512]{0:T(512)} %get-tuple-element.26) | copy-start | bytes 6148
  432.4 18.0 %copy-start.68 = (f32[1024]{0:T(1024)S(1)}, f32[1024]{0:T(1024)}, u32[]{:S(2)}) copy-start(f32[1024]{0:T(1024)} %get-tuple-element.24) | copy-start | bytes 12292
  432.4 25.1 %copy-start.25 = (bf16[1,512,512]{2,1,0:T(8,128)(2,1)S(1)}, bf16[1,512,512]{2,1,0:T(8,128)(2,1)}, u32[]{:S(2)}) copy-start(bf16[1,512,512]{2,1,0:T(8,128)(2,1)} %param.42) | copy-start | bytes 1572868
  432.4 25.1 %copy-start.67 = (f32[1,512,8]{1,2,0:T(8,128)S(1)}, f32[1,512,8]{1,2,0:T(8,128)}, u32[]{:S(2)}) copy-start(f32[1,512,8]{1,2,0:T(8,128)} %param.47) | copy-start | bytes 49156
  432.4 27.5 %copy-start.26 = (bf16[1,128,2048]{2,1,0:T(8,128)(2,1)S(1)}, bf16[1,128,2048]{2,1,0:T(8,128)(2,1)}, u32[]{:S(2)}) copy-start(bf16[1,128,2048]{2,1,0:T(8,128)(2,1)} %param.41) | copy-start | bytes 1572868
  432.4 29.6 %copy-start.42 = (bf16[1,128,512]{2,1,0:T(8,128)(2,1)S(1)}, bf16[1,128,512]{2,1,0:T(8,128)(2,1)}, u32[]{:S(2)}) copy-start(bf16[1,128,512]{2,1,0:T(8,128)(2,1)} %param.40) | copy-start | bytes 393220
  432.4 29.6 %copy-start.71 = (f32[1,512,8]{1,2,0:T(8,128)S(1)}, f32[1,512,8]{1,2,0:T(8,128)}, u32[]{:S(2)}) copy-start(f32[1,512,8]{1,2,0:T(8,128)} %param.45) | copy-start | bytes 49156
  432.4 29.9 %copy-start.30 = (bf16[1,128,1536]{2,1,0:T(8,128)(2,1)S(1)}, bf16[1,128,1536]{2,1,0:T(8,128)(2,1)}, u32[]{:S(2)}) copy-start(bf16[1,128,1536]{2,1,0:T(8,128)(2,1)} %param.39) | copy-start | bytes 1179652
  432.4 29.9 %copy-start.56 = (f32[1,1536,8]{1,2,0:T(8,128)S(1)}, f32[1,1536,8]{1,2,0:T(8,128)}, u32[]{:S(2)}) copy-start(f32[1,1536,8]{1,2,0:T(8,128)} %param.44) | copy-start | bytes 147460
  563.3 195.2 %copy-start.74 = (f32[1,512,8]{1,2,0:T(8,128)S(1)}, f32[1,512,8]{1,2,0:T(8,128)}, u32[]{:S(2)}) copy-start(f32[1,512,8]{1,2,0:T(8,128)} %param.43) | copy-start | bytes 49156
  758.5 20.8 %copy-start.83 = (bf16[3,512]{1,0:T(4,128)(2,1)S(1)}, bf16[3,512]{1,0:T(4,128)(2,1)}, u32[]{:S(2)}) copy-start(bf16[3,512]{1,0:T(4,128)(2,1)} %param.37) | copy-start | bytes 9220
  758.5 21.4 %copy-start.73 = (f32[1024]{0:T(1024)S(1)}, f32[1024]{0:T(1024)}, u32[]{:S(2)}) copy-start(f32[1024]{0:T(1024)} %copy-done.72) | copy-start | bytes 12292
  779.2 231.8 %all-reduce.18.cloned.1.call-start = ((), (), s32[]{:S(2)}) async-start(), calls=%async_computation.6 | async-start | bytes 163840 | tf_op jit(solution)/shard_map/psum | solution.py:303
  940.5 71.9 %copy-start.38 = (f32[512,512]{1,0:T(8,128)S(1)}, f32[512,512]{1,0:T(8,128)}, u32[]{:S(2)}) copy-start(f32[512,512]{1,0:T(8,128)} %param.30) | copy-start | bytes 3145732
  940.5 76.9 %copy-start.40 = (f32[128,2048]{1,0:T(8,128)S(1)}, f32[128,2048]{1,0:T(8,128)}, u32[]{:S(2)}) copy-start(f32[128,2048]{1,0:T(8,128)} %param.29) | copy-start | bytes 3145732
  940.5 81.7 %copy-start.48 = (f32[128,512]{1,0:T(8,128)S(1)}, f32[128,512]{1,0:T(8,128)}, u32[]{:S(2)}) copy-start(f32[128,512]{1,0:T(8,128)} %param.28) | copy-start | bytes 786436
  961.7 63.3 %copy-start.41 = (f32[128,1536]{1,0:T(8,128)S(1)}, f32[128,1536]{1,0:T(8,128)}, u32[]{:S(2)}) copy-start(f32[128,1536]{1,0:T(8,128)} %param.27) | copy-start | bytes 2359300
  1011.1 16.0 %copy-start.63 = (bf16[512,8]{0,1:T(8,128)(2,1)S(1)}, bf16[512,8]{0,1:T(8,128)(2,1)}, u32[]{:S(2)}) copy-start(bf16[512,8]{0,1:T(8,128)(2,1)} %get-tuple-element.184) | copy-start | bytes 24580
  (58 other events, 385.9 us)
Sparse Core Ops, SparseCore 0:
  30.0 41.1 all-reduce.11
  73.3 20.0 all-gather.3
  95.6 22.5 all-gather.5
  120.2 22.5 all-gather.7
  232.5 52.2 all-reduce.13
  779.3 67.0 all-reduce.15
  940.6 70.4 all-reduce.17
where the time goes:
time: 1070 us; the launch traced here: 1060 us
  other arithmetic  395 us (37%)
  matrix products  336 us (31%)
  waiting for transfers between devices  189 us (18%)
  blocking collectives  66.9 us (6%)
  between operations  50.7 us (5%)
  local copies, waits for them, and re-layouts  20.6 us (2%)
    reduce_sum x48, other arithmetic, orthonormal(): vector = vector - jnp.sum(earlier * vector) * earlier  137 us
    mul x6, other arithmetic, orthonormal(): vector = vector * lax.rsqrt(jnp.sum(vector * vector) + 1e-20)  92.4 us
    psum x1, waiting for transfers between devices, body(): lax.psum((lefts[0], lefts[1], lefts[2], lefts[3], lefts[4], clip_factor *...  62 us
    psum x1, waiting for transfers between devices, body(): lax.psum(rights[0].astype(jnp.bfloat16), 'rep').astype(jnp.float32)  49.4 us
    reduce_sum x26, other arithmetic, orthonormal(): vector = vector * lax.rsqrt(jnp.sum(vector * vector) + 1e-20)  39.7 us
    psum x1, blocking collectives, body(): lax.psum((lefts[0], lefts[1], lefts[2], lefts[3], lefts[4], clip_factor *...  38 us
    dot_general x5, matrix products, body(): jnp.dot(bases[member], right_means[member].T, precision=HIGHEST_PREC)  31.9 us
    dot_general x5, matrix products, body(): jnp.dot(bases[member], projected, precision=HIGHEST_PREC)  31.6 us
  transfers between devices with their start and end apart: 7, of which 5 were waited for; matrix products, arithmetic and copies ran while one was open for 10% of the time, Pallas kernels for 0%

commit v1 on v0

--- a/solution.py
+++ b/solution.py
@@ -1,6 +1,10 @@
+import functools
+
 import jax
 import jax.numpy as jnp
 from jax import lax
+from jax.experimental import pallas as pl
+from jax.experimental.pallas import tpu as pltpu
 from jax.sharding import PartitionSpec as P
 
 HEADS = 8
@@ -12,6 +16,461 @@
 LEARN_RATE = 10.0
 CLIP_NORM = 1.0
 ZLOSS_WEIGHT = 0.01
+
+
+TB = 1024
+RK = 8
+F32 = jnp.float32
+BF16 = jnp.bfloat16
+MESH_ID = pl.DeviceIdType.MESH
+
+
+def round_up(value, step):
+    return (value + step - 1) // step * step
+
+
+def halves(value):
+    high = value.astype(BF16).astype(F32)
+    return high, value - high
+
+
+def dims_of(value, contract_left, contract_right):
+    return (((contract_left,), (contract_right,)), ((), ()))
+
+
+def left_of(matrix, start_t):
+    s_high, s_low = halves(start_t)
+    both = jnp.concatenate([s_high, s_low], axis=0).astype(BF16)
+    high = matrix.astype(BF16)
+    low = (matrix - high.astype(F32)).astype(BF16)
+    nt = (((1,), (1,)), ((), ()))
+    main = lax.dot_general(both, high, nt, preferred_element_type=F32)
+    rest = lax.dot_general(s_high.astype(BF16), low, nt, preferred_element_type=F32)
+    return main[:RK] + main[RK:] + rest
+
+
+def left_of_bf16(matrix, start_t):
+    s_high, s_low = halves(start_t)
+    both = jnp.concatenate([s_high, s_low], axis=0).astype(BF16)
+    main = lax.dot_general(both, matrix, (((1,), (1,)), ((), ())), preferred_element_type=F32)
+    return main[:RK] + main[RK:]
+
+
+def right_of(basis_t, matrix):
+    b_high, b_low = halves(basis_t)
+    both = jnp.concatenate([b_high, b_low], axis=0).astype(BF16)
+    high = matrix.astype(BF16)
+    low = (matrix - high.astype(F32)).astype(BF16)
+    main = jnp.dot(both, high, preferred_element_type=F32)
+    rest = jnp.dot(b_high.astype(BF16), low, preferred_element_type=F32)
+    return main[:RK] + main[RK:] + rest
+
+
+def product_of(basis_t, right_t):
+    b_high, b_low = halves(basis_t)
+    r_high, r_low = halves(right_t)
+    zero_b, zero_r = jnp.zeros_like(b_high), jnp.zeros_like(r_high)
+    left = jnp.concatenate([b_high, b_low, b_high, zero_b], axis=0).astype(BF16)
+    right = jnp.concatenate([r_high, r_high, r_low, zero_r], axis=0).astype(BF16)
+    return lax.dot_general(left, right, (((0,), (0,)), ((), ())), preferred_element_type=F32)
+
+
+def keep_rows(value, first_row, rows):
+    at = first_row + lax.broadcasted_iota(jnp.int32, value.shape, 0)
+    return jnp.where(at < rows, value, jnp.zeros_like(value))
+
+
+def fold_squares(value):
+    squares = value * value
+    rows, columns = value.shape
+    by_sublane = jnp.sum(squares.reshape(rows // 8, 8, columns), axis=0)
+    total = by_sublane[:, :512]
+    for start in range(512, columns, 512):
+        total = total + by_sublane[:, start : start + 512]
+    return total
+
+
+def small_places(rows_list):
+    places, at = [], 0
+    for rows in rows_list:
+        places.append(at)
+        at += round_up(rows, 128)
+    return places, at
+
+
+def sketch_kernel(rows, row_list, *refs):
+    grads, errs, starts = refs[0:5], refs[5:10], refs[10:15]
+    gq_ref, eq_ref, gs_ref, es_ref, sq_ref = refs[15:20]
+    step = pl.program_id(0)
+    places, _ = small_places(row_list)
+
+    @pl.when(step == 0)
+    def _():
+        gs_ref[...] = jnp.zeros_like(gs_ref)
+        es_ref[...] = jnp.zeros_like(es_ref)
+        total = jnp.zeros(sq_ref.shape, F32)
+        for k in range(4):
+            grad = grads[k + 1][...]
+            start_t = starts[k + 1][...]
+            at = pl.ds(places[k], row_list[k])
+            gs_ref[:, at] = left_of(grad, start_t)
+            es_ref[:, at] = left_of_bf16(errs[k + 1][...], start_t)
+            total = total + fold_squares(grad)
+        sq_ref[...] = total
+
+    start_t = starts[0][...]
+    grad = keep_rows(grads[0][...], step * TB, rows)
+    err = keep_rows(errs[0][...].astype(F32), step * TB, rows).astype(BF16)
+    gq_ref[...] = left_of(grad, start_t)
+    eq_ref[...] = left_of_bf16(err, start_t)
+    sq_ref[...] += fold_squares(grad)
+
+
+def whole(shape):
+    return pl.BlockSpec(shape, lambda *_: (0,) * len(shape))
+
+
+def sketch(grads, errs, starts_t):
+    rows, width = grads[0].shape
+    blocks = pl.cdiv(rows, TB)
+    row_list = [g.shape[0] for g in grads[1:]]
+    _, small = small_places(row_list)
+    block = pl.BlockSpec((TB, width), lambda i: (i, 0))
+    lanes = pl.BlockSpec((RK, TB), lambda i: (0, i))
+    return pl.pallas_call(
+        functools.partial(sketch_kernel, rows, row_list),
+        grid=(blocks,),
+        in_specs=[block]
+        + [whole(g.shape) for g in grads[1:]]
+        + [block]
+        + [whole(e.shape) for e in errs[1:]]
+        + [whole(s.shape) for s in starts_t],
+        out_specs=[lanes, lanes, whole((RK, small)), whole((RK, small)), whole((8, 512))],
+        out_shape=[
+            jax.ShapeDtypeStruct((RK, blocks * TB), F32),
+            jax.ShapeDtypeStruct((RK, blocks * TB), F32),
+            jax.ShapeDtypeStruct((RK, small), F32),
+            jax.ShapeDtypeStruct((RK, small), F32),
+            jax.ShapeDtypeStruct((8, 512), F32),
+        ],
+        name="sketch",
+    )(*grads, *errs, *starts_t)
+
+
+def clip_of(norm_tile):
+    return jnp.minimum(1.0, CLIP_NORM / norm_tile[0:1, 0:1])
+
+
+def orthonormal_t(parts):
+    row_at = lax.broadcasted_iota(jnp.int32, (RK, 1), 0)
+    for row in range(RK):
+        total = None
+        for part in parts:
+            term = part * part[row : row + 1, :]
+            for start in range(0, term.shape[1], 128):
+                piece = term[:, start : start + 128]
+                total = piece if total is None else total + piece
+        dots = jnp.sum(total, axis=1, keepdims=True)
+        inverse = lax.rsqrt(dots[row : row + 1, :] + 1e-20)
+        scale = jnp.where(row_at == row, inverse, 1.0)
+        taken = jnp.where(row_at > row, -dots * inverse * inverse, 0.0)
+        parts = [part * scale + taken * part[row : row + 1, :] for part in parts]
+    return parts
+
+
+def ring_sum(x, landing, y, send_sem, land_sem, spread_sem, gather_sem, axis, count):
+    me = lax.axis_index(axis)
+    first = []
+    for step in range(1, count):
+        peer = lax.rem(me + step, count)
+        copy = pltpu.make_async_remote_copy(
+            src_ref=x.at[peer],
+            dst_ref=landing.at[step],
+            send_sem=send_sem.at[step],
+            recv_sem=land_sem.at[step],
+            device_id={axis: peer},
+            device_id_type=MESH_ID,
+        )
+        copy.start()
+        first.append(copy)
+    total = x[me]
+    for step in range(1, count):
+        first[step - 1].wait_recv()
+        total = total + landing[step]
+    y[me] = total
+    second = []
+    for step in range(1, count):
+        peer = lax.rem(me + step, count)
+        copy = pltpu.make_async_remote_copy(
+            src_ref=y.at[me],
+            dst_ref=y.at[me],
+            send_sem=spread_sem.at[step],
+            recv_sem=gather_sem.at[step],
+            device_id={axis: peer},
+            device_id_type=MESH_ID,
+        )
+        copy.start()
+        second.append(copy)
+    for copy in first:
+        copy.wait_send()
+    for step in range(1, count):
+        source = lax.rem(me - step + count, count)
+        pltpu.make_async_remote_copy(
+            src_ref=y.at[source],
+            dst_ref=y.at[source],
+            send_sem=spread_sem.at[step],
+            recv_sem=gather_sem.at[step],
+            device_id={axis: source},
+            device_id_type=MESH_ID,
+        ).wait_recv()
+    for copy in second:
+        copy.wait_send()
+
+
+def greet(axes):
+    barrier = pltpu.get_barrier_semaphore()
+    greeted = 0
+    for axis, count in axes:
+        me = lax.axis_index(axis)
+        for step in range(1, count):
+            pl.semaphore_signal(
+                barrier,
+                inc=1,
+                device_id={axis: lax.rem(me + step, count)},
+                device_id_type=MESH_ID,
+            )
+        greeted += count - 1
+    pl.semaphore_wait(barrier, greeted)
+
+
+def basis_kernel(
+    workers, shards, row_list, gains_at,
+    gq_ref, eq_ref, gs_ref, es_ref, gains_ref, sq_ref,
+    ph_ref, phs_ref, gsum_ref, norm_ref,
+    x, landing, y, small, sq_all, send_sem, land_sem, spread_sem, gather_sem, sq_send, sq_recv,
+):
+    greet((("rep", workers), ("voc", shards)))
+    shard = lax.axis_index("voc")
+    own = jnp.sum(sq_ref[...].reshape(8, 4, 128), axis=1)
+    own = jnp.sum(jnp.sum(own, axis=0, keepdims=True), axis=1, keepdims=True)
+    sq_all[shard] = jnp.broadcast_to(own, (8, 128))
+    copies = []
+    for step in range(1, shards):
+        peer = lax.rem(shard + step, shards)
+        copy = pltpu.make_async_remote_copy(
+            src_ref=sq_all.at[shard],
+            dst_ref=sq_all.at[shard],
+            send_sem=sq_send.at[step],
+            recv_sem=sq_recv.at[step],
+            device_id={"voc": peer},
+            device_id_type=MESH_ID,
+        )
+        copy.start()
+        copies.append(copy)
+    gains = gains_ref[...]
+    total = jnp.sum(jnp.sum(gains * gains, axis=0, keepdims=True), axis=1, keepdims=True)
+    small[...] = jnp.zeros_like(small)
+    for step in range(1, shards):
+        source = lax.rem(shard - step + shards, shards)
+        pltpu.make_async_remote_copy(
+            src_ref=sq_all.at[source],
+            dst_ref=sq_all.at[source],
+            send_sem=sq_send.at[step],
+            recv_sem=sq_recv.at[step],
+            device_id={"voc": source},
+            device_id_type=MESH_ID,
+        ).wait_recv()
+    for copy in copies:
+        copy.wait_send()
+    for peer in range(shards):
+        total = total + sq_all[peer][0:1, 0:1]
+    norm = jnp.sqrt(total)
+    norm_ref[...] = jnp.broadcast_to(norm, (8, 128))
+    clip = jnp.minimum(1.0, CLIP_NORM / norm)
+
+    chunk = gq_ref.shape[1] // workers
+    part = small.shape[1] // workers
+    span = gs_ref.shape[1]
+    small[:, :span] = clip * gs_ref[...] + es_ref[...]
+    small[:, gains_at : gains_at + gains.shape[1]] = clip * gains
+    for j in range(workers):
+        at = slice(j * chunk, (j + 1) * chunk)
+        x[j, :, :chunk] = clip * gq_ref[:, at] + eq_ref[:, at]
+        x[j, :, chunk:] = small[:, j * part : (j + 1) * part]
+    ring_sum(x, landing, y, send_sem, land_sem, spread_sem, gather_sem, "rep", workers)
+    parts = orthonormal_t([y[j, :, :chunk] for j in range(workers)])
+    for j in range(workers):
+        ph_ref[:, j * chunk : (j + 1) * chunk] = parts[j]
+        small[:, j * part : (j + 1) * part] = y[j, :, chunk:]
+    gsum_ref[...] = small[:, gains_at : gains_at + gains.shape[1]]
+    places, _ = small_places(row_list)
+    for place, rows in zip(places, row_list):
+        lanes = round_up(rows, 128)
+        phs_ref[:, place : place + lanes] = orthonormal_t([small[:, place : place + lanes]])[0]
+
+
+def basis(sketches, gains, row_list, workers, shards):
+    gq, eq, gs, es, sq = sketches
+    gains_at = gs.shape[1]
+    small = round_up(gains_at + gains.shape[1], workers * 128)
+    lanes = (gq.shape[1] + small) // workers
+    vmem = pl.BlockSpec(memory_space=pltpu.VMEM)
+    return pl.pallas_call(
+        functools.partial(basis_kernel, workers, shards, row_list, gains_at),
+        in_specs=[vmem] * 6,
+        out_specs=[vmem] * 4,
+        out_shape=[
+            jax.ShapeDtypeStruct(gq.shape, F32),
+            jax.ShapeDtypeStruct(gs.shape, F32),
+            jax.ShapeDtypeStruct(gains.shape, F32),
+            jax.ShapeDtypeStruct((8, 128), F32),
+        ],
+        scratch_shapes=[
+            pltpu.VMEM((workers, RK, lanes), F32),
+            pltpu.VMEM((workers, RK, lanes), F32),
+            pltpu.VMEM((workers, RK, lanes), F32),
+            pltpu.VMEM((RK, small), F32),
+            pltpu.VMEM((shards, 8, 128), F32),
+        ]
+        + [pltpu.SemaphoreType.DMA((workers,))] * 4
+        + [pltpu.SemaphoreType.DMA((shards,))] * 2,
+        compiler_params=pltpu.CompilerParams(collective_id=1, has_side_effects=True),
+        name="basis",
+    )(gq, eq, gs, es, gains, sq)
+
+
+def residual_kernel(rows, row_list, *refs):
+    grads, errs = refs[0:5], refs[5:10]
+    ph_ref, phs_ref, norm_ref = refs[10:13]
+    outs, rights = refs[13:18], refs[18:23]
+    kept = refs[23]
+    phase, step = pl.program_id(0), pl.program_id(1)
+    places, _ = small_places(row_list)
+    clip = clip_of(norm_ref[...])
+    at = pl.multiple_of(step * TB, TB)
+
+    @pl.when((phase == 0) & (step == 0))
+    def _():
+        rights[0][...] = jnp.zeros_like(rights[0])
+        for k in range(4):
+            matrix = clip * grads[k + 1][...] + errs[k + 1][...].astype(F32)
+            basis_t = phs_ref[:, places[k] : places[k] + row_list[k]]
+            right_t = right_of(basis_t, matrix)
+            rights[k + 1][...] = right_t
+            outs[k + 1][...] = matrix - product_of(basis_t, right_t)
+
+    @pl.when(phase == 0)
+    def _():
+        matrix = clip * grads[0][...] + errs[0][...].astype(F32)
+        matrix = keep_rows(matrix, step * TB, rows)
+        kept[pl.ds(at, TB), :] = matrix
+        rights[0][...] += right_of(ph_ref[:, pl.ds(at, TB)], matrix)
+
+    @pl.when(phase == 1)
+    def _():
+        outs[0][...] = kept[pl.ds(at, TB), :] - product_of(ph_ref[:, pl.ds(at, TB)], rights[0][...])
+
+
+def residual(grads, errs, ph, phs, norm):
+    rows, width = grads[0].shape
+    blocks = pl.cdiv(rows, TB)
+    row_list = [g.shape[0] for g in grads[1:]]
+    block_in = pl.BlockSpec((TB, width), lambda p, i: (jnp.where(p == 0, i, blocks - 1), 0))
+    block_out = pl.BlockSpec((TB, width), lambda p, i: (jnp.where(p == 0, 0, i), 0))
+    out = pl.pallas_call(
+        functools.partial(residual_kernel, rows, row_list),
+        grid=(2, blocks),
+        in_specs=[block_in]
+        + [whole(g.shape) for g in grads[1:]]
+        + [block_in]
+        + [whole(e.shape) for e in errs[1:]]
+        + [whole(ph.shape), whole(phs.shape), whole(norm.shape)],
+        out_specs=[block_out]
+        + [whole(g.shape) for g in grads[1:]]
+        + [whole((RK, g.shape[1])) for g in grads],
+        out_shape=[jax.ShapeDtypeStruct(g.shape, F32) for g in grads]
+        + [jax.ShapeDtypeStruct((RK, g.shape[1]), F32) for g in grads],
+        scratch_shapes=[pltpu.VMEM((blocks * TB, width), F32)],
+        compiler_params=pltpu.CompilerParams(vmem_limit_bytes=60 << 20),
+        name="residual",
+    )(*grads, *errs, ph, phs, norm)
+    return out[:5], out[5:]
+
+
+def mean_right_kernel(workers, r0, r1, r2, r3, r4, out_ref, flat, x, landing, y, s1, s2, s3, s4):
+    greet((("rep", workers),))
+    part = x.shape[2]
+    flat[...] = jnp.zeros_like(flat)
+    at = 0
+    for ref in (r0, r1, r2, r3, r4):
+        flat[:, at : at + ref.shape[1]] = ref[...]
+        at += ref.shape[1]
+    for j in range(workers):
+        x[j] = flat[:, j * part : (j + 1) * part]
+    ring_sum(x, landing, y, s1, s2, s3, s4, "rep", workers)
+    for j in range(workers):
+        out_ref[:, j * part : (j + 1) * part] = y[j] * (1.0 / workers)
+
+
+def mean_right(rights, workers):
+    lanes = round_up(sum(r.shape[1] for r in rights), workers * 128)
+    vmem = pl.BlockSpec(memory_space=pltpu.VMEM)
+    part = (workers, RK, lanes // workers)
+    return pl.pallas_call(
+        functools.partial(mean_right_kernel, workers),
+        in_specs=[vmem] * 5,
+        out_specs=vmem,
+        out_shape=jax.ShapeDtypeStruct((RK, lanes), F32),
+        scratch_shapes=[pltpu.VMEM((RK, lanes), F32)]
+        + [pltpu.VMEM(part, F32)] * 3
+        + [pltpu.SemaphoreType.DMA((workers,))] * 4,
+        compiler_params=pltpu.CompilerParams(collective_id=2, has_side_effects=True),
+        name="mean_right",
+    )(*rights)
+
+
+def update_kernel(row_list, widths, *refs):
+    moms, weights = refs[0:5], refs[5:9]
+    ph_ref, phs_ref, right_ref = refs[9:12]
+    out_moms, outs = refs[12:17], refs[17:22]
+    places, _ = small_places(row_list)
+
+    @pl.when(pl.program_id(0) == 0)
+    def _():
+        at = widths[0]
+        for k in range(4):
+            basis_t = phs_ref[:, places[k] : places[k] + row_list[k]]
+            mean = product_of(basis_t, right_ref[:, at : at + widths[k + 1]])
+            at += widths[k + 1]
+            moved = MOMENTUM * moms[k + 1][...].astype(F32) + mean
+            out_moms[k + 1][...] = moved
+            outs[k + 1][...] = weights[k][...] + -LEARN_RATE * moved
+
+    mean = product_of(ph_ref[...], right_ref[:, : widths[0]])
+    moved = MOMENTUM * moms[0][...].astype(F32) + mean
+    out_moms[0][...] = moved
+    outs[0][...] = -LEARN_RATE * moved
+
+
+def update(moms, weights, ph, phs, right):
+    rows, width = moms[0].shape
+    blocks = pl.cdiv(rows, TB)
+    row_list = [m.shape[0] for m in moms[1:]]
+    widths = [m.shape[1] for m in moms]
+    block = pl.BlockSpec((TB, width), lambda i: (i, 0))
+    out = pl.pallas_call(
+        functools.partial(update_kernel, row_list, widths),
+        grid=(blocks,),
+        in_specs=[block]
+        + [whole(m.shape) for m in moms[1:]]
+        + [whole(w.shape) for w in weights]
+        + [pl.BlockSpec((RK, TB), lambda i: (0, i)), whole(phs.shape), whole(right.shape)],
+        out_specs=([block] + [whole(m.shape) for m in moms[1:]]) * 2,
+        out_shape=[jax.ShapeDtypeStruct(m.shape, F32) for m in moms] * 2,
+        compiler_params=pltpu.CompilerParams(vmem_limit_bytes=60 << 20),
+        name="update",
+    )(*moms, *weights, ph, phs, right)
+    return out[:5], out[5:]
 
 
 def rms_norm(values, weight):
@@ -34,17 +493,6 @@
         ],
         axis=-1,
     )
-
-
-def orthonormal(matrix):
-    columns = []
-    for column_pos in range(matrix.shape[1]):
-        vector = matrix[:, column_pos]
-        for earlier in columns:
-            vector = vector - jnp.sum(earlier * vector) * earlier
-        vector = vector * lax.rsqrt(jnp.sum(vector * vector) + 1e-20)
-        columns.append(vector)
-    return jnp.stack(columns, axis=1)
 
 
 def block_scores(rows_query, key_seq, first_row):
@@ -277,77 +725,40 @@
         lax.dynamic_slice_in_dim(full_grad, shard_pos * own_slice.shape[0], own_slice.shape[0], 0)
         for full_grad, own_slice in zip(grad_mats, slices)
     ]
-    squares = sum((jnp.sum(grad_part * grad_part) for grad_part in own_grads))
-    squares = squares + jnp.where(shard_pos == 0, jnp.sum(grad_gains * grad_gains), 0.0)
-    total_norm = jnp.sqrt(lax.psum(squares, "voc"))
-    clip_factor = jnp.minimum(1.0, CLIP_NORM / total_norm)
-    errors = (embed_err, qkv_err, out_err, up_err, down_err)
-    starts = (embed_factor, qkv_factor, out_factor, up_factor, down_factor)
-    matrices = [
-        clip_factor * grad_part + error_in[0].astype(jnp.float32)
-        for grad_part, error_in in zip(own_grads, errors)
+    errors = [e[0] for e in (embed_err, qkv_err, out_err, up_err, down_err)]
+    starts_t = [
+        f[0].T for f in (embed_factor, qkv_factor, out_factor, up_factor, down_factor)
     ]
-    lefts = [
-        jnp.dot(matrix, start_in[0], precision=HIGHEST_PREC)
-        for matrix, start_in in zip(matrices, starts)
-    ]
-    left_sums = lax.psum(
-        (lefts[0], lefts[1], lefts[2], lefts[3], lefts[4], clip_factor * grad_gains), "rep"
-    )
-    bases = [orthonormal(left_sum) for left_sum in left_sums[:5]]
-    rights = [
-        jnp.einsum("rc,rk->ck", matrix, basis, precision=HIGHEST_PREC)
-        for matrix, basis in zip(matrices, bases)
-    ]
-    right_sums = (
-        lax.psum(rights[0].astype(jnp.bfloat16), "rep").astype(jnp.float32),
-        lax.psum(rights[1].astype(jnp.bfloat16), "rep").astype(jnp.float32),
-        lax.psum(rights[2].astype(jnp.bfloat16), "rep").astype(jnp.float32),
-        lax.psum(rights[3].astype(jnp.bfloat16), "rep").astype(jnp.float32),
-        lax.psum(rights[4].astype(jnp.bfloat16), "rep").astype(jnp.float32),
-    )
-    right_means = [right_sum / workers for right_sum in right_sums]
-    weights_all = (embedding, w_qkv, w_out, w_up, w_down)
-    moments = (embed_mom, qkv_mom, out_mom, up_mom, down_mom)
-    new_weights, new_moments, new_errors, changes = ([], [], [], [])
-    for member in range(5):
-        mean_grad = jnp.dot(bases[member], right_means[member].T, precision=HIGHEST_PREC)
-        projected = jnp.einsum("rk,rc->kc", bases[member], matrices[member], precision=HIGHEST_PREC)
-        new_errors.append(
-            (matrices[member] - jnp.dot(bases[member], projected, precision=HIGHEST_PREC))[None]
-        )
-        new_momentum = MOMENTUM * moments[member].astype(jnp.float32) + mean_grad
-        new_moments.append(new_momentum)
-        change = -LEARN_RATE * new_momentum
-        changes.append(change)
-        new_weights.append(weights_all[member] + change)
-    next_gain_mom = MOMENTUM * gain_mom.astype(jnp.float32) + left_sums[5] / workers
+    row_list = [g.shape[0] for g in own_grads[1:]]
+    gains_flat = jnp.pad(grad_gains.reshape(RK, -1), ((0, 0), (0, 64)))
+    sketches = sketch(own_grads, errors, starts_t)
+    ph, phs, gain_sum, norm = basis(sketches, gains_flat, row_list, workers, lax.axis_size("voc"))
+    new_errors, rights = residual(own_grads, errors, ph, phs, norm)
+    right_mean = mean_right(rights, workers)
+    new_moments, changed = update(
+        (embed_mom, qkv_mom, out_mom, up_mom, down_mom),
+        (w_qkv, w_out, w_up, w_down),
+        ph,
+        phs,
+        right_mean,
+    )
+    total_norm = norm[0, 0]
+    factors, at = [], 0
+    for grad_part in own_grads:
+        factors.append(right_mean[:, at : at + grad_part.shape[1]].T[None])
+        at += grad_part.shape[1]
+    gain_mean = gain_sum[:, :192].reshape(3, -1) / workers
+    next_gain_mom = MOMENTUM * gain_mom.astype(jnp.float32) + gain_mean
     gain_change = -LEARN_RATE * next_gain_mom
     return (
         loss_value.reshape(1),
         total_norm.reshape(1),
-        changes[0],
-        new_weights[1],
-        new_weights[2],
-        new_weights[3],
-        new_weights[4],
+        *changed,
         gain_change,
-        new_moments[0],
-        new_moments[1],
-        new_moments[2],
-        new_moments[3],
-        new_moments[4],
+        *new_moments,
         next_gain_mom,
-        new_errors[0],
-        new_errors[1],
-        new_errors[2],
-        new_errors[3],
-        new_errors[4],
-        right_means[0][None],
-        right_means[1][None],
-        right_means[2][None],
-        right_means[3][None],
-        right_means[4][None],
+        *(e[None] for e in new_errors),
+        *factors,
     )
 
 

time: 1070 us -> 554 us (0.52)
  other arithmetic: 395 us -> 96.5 us
  matrix products: 336 us -> 200 us
  waiting for transfers between devices: 189 us -> 74.7 us
  Pallas kernels: 0 us -> 102 us
  blocking collectives: 66.9 us -> 22.8 us
  between operations: 50.7 us -> 17.8 us
    reduce_sum x80 -> x0, other arithmetic: 194 us -> none  [the longest x48 137 us: orthonormal(): vector = vector - jnp.sum(earlier * vector) * earlier]
    dot_general x25 -> x0, matrix products: 133 us -> none  [the longest x5 31.9 us: body(): jnp.dot(bases[member], right_means[member].T, precision=HIGHEST_PREC)]
    psum x2 -> x0, waiting for transfers between devices: 111 us -> none  [the longest x1 62 us: body(): lax.psum((lefts[0], lefts[1], lefts[2], lefts[3], lefts[4], clip_factor *...]
    pallas_call x0 -> x5, Pallas kernels: none -> 102 us  [the longest x1 24.6 us: basis(): pl.pallas_call(functools.partial(basis_kernel, workers, shards, row_list,...]
    mul x7 -> x0, other arithmetic: 92.4 us -> none  [the longest x6 92.4 us: orthonormal(): vector = vector * lax.rsqrt(jnp.sum(vector * vector) + 1e-20)]
    psum x1 -> x0, blocking collectives: 38 us -> none  [body(): lax.psum((lefts[0], lefts[1], lefts[2], lefts[3], lefts[4], clip_factor *...]
  transfers between devices with their start and end apart: 7 -> 5, of which waited for: 5 -> 3; matrix products, arithmetic and copies ran while one was open for 10% -> 16% of each run, Pallas kernels for 0% -> 0%
where the time goes in v1:
time: 554 us; the launch traced here: 545 us
  matrix products  200 us (36%)
  Pallas kernels  102 us (18%)
  other arithmetic  96.5 us (17%)
  waiting for transfers between devices  74.7 us (13%)
  local copies, waits for them, and re-layouts  30.7 us (6%)
  blocking collectives  22.8 us (4%)
  between operations  17.8 us (3%)
    psum x1, waiting for transfers between devices, body(): grad_normed_out = lax.psum(hidden_terms, 'voc')  28.6 us
    dot_general x2, matrix products, attend_back(): jnp.einsum('qhd,khd->hqk', rows_grad, value_seq, preferred_element_type=j...  26.4 us
    convert_element_type x2, other arithmetic, attend_back(): grad_scores = (attn_probs * (grad_probs - row_delta)).astype(jnp.bfloat16)  25.4 us
    psum x1, waiting for transfers between devices, body(): lax.psum(own_rows.astype(jnp.bfloat16), 'voc').astype(jnp.float32)  25.2 us
    pallas_call x1, Pallas kernels, basis(): pl.pallas_call(functools.partial(basis_kernel, workers, shards, row_list,...  24.6 us
    dot_general x1, matrix products, layer_forward(): hidden = jnp.dot(normed_mid, proj_up, preferred_element_type=jnp.float32)  24.5 us
    pallas_call x1, Pallas kernels, residual(): pl.pallas_call(functools.partial(residual_kernel, rows, row_list), grid=(...  23.5 us
    dot_general x1, matrix products, body(): jnp.einsum('tv,td->vd', grad_logits, normed_out, preferred_element_type=j...  21.9 us
  transfers between devices with their start and end apart: 5, of which 3 were waited for; matrix products, arithmetic and copies ran while one was open for 16% of the time, Pallas kernels for 0%

profile of v1, /device:TPU:0, one launch (start us, length us, event | category | flops | bytes accessed | tf_op | source)
XLA Modules:
  0.0 544.8 jit_solution(1000524269488339365)
XLA Ops:
  8.7 8.8 %convert_element_type.165 = bf16[8000,512]{1,0:T(8,128)(2,1)} convert(f32[8000,512]{1,0:T(8,128)} %param.26) | non-fusion elementwise | flops 4096000 | bytes 24576000 | tf_op jit(solution)/shard_map/convert_element_type | solution.py:675
  17.6 8.5 %gather_fusion = bf16[1024,512]{1,0:T(8,128)(2,1)S(1)} fusion(bf16[8000,512]{1,0:T(8,128)(2,1)} %convert_element_type.165, s32[1024]{0:T(1024)S(1)} %broadcast_clamp_fusion), kind=kCustom, calls=%fused_computation | custom fusion | bytes 2101248 | tf_op jit(solution)/shard_map/gather | solution.py:686
  27.5 1.9 convert_element_type.170
  32.0 11.0 %all_gather.13 = bf16[512,512]{1,0:T(8,128)(2,1)S(1)} all-gather(bf16[128,512]{1,0:T(8,128)(2,1)S(1)} %convert_element_type.177), channel_id=1, replica_groups=mesh['rep'=8,'voc'=4] {'voc'}, dimensions={0}, use_global_device_ids=true | all-gather | bytes 655360 | tf_op jit(solution)/shard_map/all_gather | solution.py:679
  43.5 25.2 %all-reduce.9.cloned.1.call-done = bf16[1024,512]{1,0:T(8,128)(2,1)} async-done(((bf16[1024,512]{1,0:T(8,128)(2,1)}), bf16[1024,512]{1,0:T(8,128)(2,1)}) %all-reduce.9.cloned.1.call-update) | async-done | bytes 1048592 | tf_op jit(solution)/shard_map/psum | solution.py:687
  70.3 20.7 %all-gather.4.cloned.1.call-done = bf16[512,1536]{1,0:T(8,128)(2,1)} async-done(((bf16[128,1536]{1,0:T(8,128)(2,1)}), bf16[512,1536]{1,0:T(8,128)(2,1)}) %all-gather.4.cloned.1.call-update) | async-done | bytes 1572880 | tf_op jit(solution)/shard_map/all_gather | solution.py:678
  91.0 3.7 fusion.46
  97.5 3.1 fusion
  100.6 4.6 exponential_reduce_fusion.2
  106.4 6.1 %fusion.26 = bf16[512,8,64]{0,2,1:T(8,128)(2,1)S(1)} fusion(f32[8,512,1024]{2,1,0:T(8,128)S(1)} %get-tuple-element.127, f32[8,512]{1,0:T(8,128)S(1)} %log_add_fusion.1, pred[512,1024]{1,0:T(8,128)(4,1)S(1)} %iota_compare_fusion.2, f32[1,1024,3,8,64]{1,4,3,2,0:T(8,128)} %bitcast.123), kind=kOutput, calls=%fused_computation.87 | convolution fusion | flops 553910272 | bytes 18890752 | tf_op jit(solution)/shard_map/hqk,khd->qhd/dot_general | solution.py:516
  112.5 3.1 fusion.1
  115.6 4.4 exponential_reduce_fusion.1
  121.3 6.2 %fusion.27 = bf16[512,8,64]{0,2,1:T(8,128)(2,1)S(1)} fusion(f32[8,512,1024]{2,1,0:T(8,128)S(1)} %get-tuple-element.125, f32[8,512]{1,0:T(8,128)S(1)} %log_add_fusion, pred[512,1024]{1,0:T(8,128)(4,1)S(1)} %iota_compare_fusion.1, f32[1,1024,3,8,64]{1,4,3,2,0:T(8,128)} %bitcast.124), kind=kOutput, calls=%fused_computation.88 | convolution fusion | flops 553910272 | bytes 18890752 | tf_op jit(solution)/shard_map/hqk,khd->qhd/dot_general | solution.py:516
  128.7 24.5 %multiply_convert_fusion.3 = (bf16[1024,2048]{1,0:T(8,128)(2,1)}, f32[1024,2048]{1,0:T(8,128)}, f32[1024,2048]{1,0:T(8,128)}) fusion(bf16[512,2048]{1,0:T(8,128)(2,1)} %all-gather.6.cloned.1.call-done, f32[1024,512]{1,0:T(8,128)S(1)} %get-tuple-element.129, f32[512]{0:T(512)S(1)} %bitcast.145, f32[1024]{0:T(1024)S(1)} %fusion.50), kind=kOutput, calls=%fused_computation.23 | convolution fusion | flops 2285371392 | bytes 25171968 | tf_op jit(solution)/shard_map/dot_general | solution.py:574
  153.2 5.3 multiply_reduce_fusion.6
  158.5 19.3 %fusion.71 = (f32[1024]{0:T(1024)S(1)}, f32[1024,8000]{0,1:T(8,128)}) fusion(bf16[8000,512]{1,0:T(8,128)(2,1)} %convert_element_type.165, f32[1024,512]{1,0:T(8,128)S(1)} %get-tuple-element.132, f32[512]{0:T(512)S(1)} %bitcast.149, f32[1024]{0:T(1024)S(1)} %fusion.51), kind=kOutput, calls=%fused_computation.173 | convolution fusion | flops 8398371840 | bytes 43067392 | tf_op jit(solution)/shard_map/td,vd->tv/dot_general | solution.py:690
  177.8 6.1 %pmax.7 = f32[1024]{0:T(1024)S(1)} all-reduce(f32[1024]{0:T(1024)S(1)} %get-tuple-element.133), channel_id=1, replica_groups=mesh['rep'=8,'voc'=4] {'voc'}, use_global_device_ids=true, to_apply=%region_9.10 | all-reduce | flops 1024 | bytes 8192 | tf_op jit(solution)/shard_map/pmax | solution.py:695
  183.9 15.0 %select_reduce_fusion = (f32[1024]{0:T(1024)S(1)}, f32[1024]{0:T(1024)S(1)}) fusion(f32[1024,8000]{0,1:T(8,128)} %get-tuple-element.134, s32[1024]{0:T(1024)S(1)} %bitcast.156, f32[1024]{0:T(1024)S(1)} %pmax.7), kind=kLoop, calls=%fused_computation.3 | loop fusion | flops 40957952 | bytes 32784384 | tf_op jit(solution)/shard_map/reduce_sum | solution.py:693
  198.9 5.8 %all-reduce.5 = (f32[1024]{0:T(1024)S(1)}, f32[1024]{0:T(1024)S(1)}) all-reduce(f32[1024]{0:T(1024)S(1)} %get-tuple-element.83, f32[1024]{0:T(1024)S(1)} %get-tuple-element.82), channel_id=1, replica_groups=mesh['rep'=8,'voc'=4] {'voc'}, use_global_device_ids=true, to_apply=%region_11.12 | all-reduce | flops 2048 | bytes 16384 | tf_op jit(solution)/shard_map/psum | solution.py:696
  204.7 19.4 %fusion.67 = f32[1024,512]{1,0:T(8,128)} fusion(bf16[8000,512]{1,0:T(8,128)(2,1)} %convert_element_type.165, f32[1024,8000]{0,1:T(8,128)} %get-tuple-element.134, f32[1024]{0:T(1024)S(1)} %get-tuple-element.96, f32[1024]{0:T(1024)S(1)} %get-tuple-element.97, s32[1024]{0:T(1024)S(1)} %bitcast.157), kind=kOutput, calls=%fused_computation.170 | convolution fusion | flops 8445952000 | bytes 43069440 | tf_op jit(solution)/shard_map/dot_general | solution.py:712
  224.1 21.9 %fusion.65 = f32[8000,512]{1,0:T(8,128)} fusion(f32[1024,512]{1,0:T(8,128)} %copy-done.12, f32[512]{0:T(512)S(1)} %bitcast.150, f32[1024]{0:T(1024)S(1)} %fusion.51, f32[1024,8000]{0,1:T(8,128)} %get-tuple-element.134, f32[1024]{0:T(1024)S(1)} %get-tuple-element.96, f32[1024]{0:T(1024)S(1)} %get-tuple-element.97, s32[1024]{0:T(1024)S(1)} %bitcast.158), kind=kOutput, calls=%fused_computation.168 | convolution fusion | flops 8447524864 | bytes 51267584 | tf_op jit(solution)/shard_map/tv,td->vd/dot_general | solution.py:709
  247.9 28.6 %all-reduce.11.cloned.1.call-done = f32[1024,512]{1,0:T(8,128)} async-done(((f32[1024,512]{1,0:T(8,128)}), f32[1024,512]{1,0:T(8,128)}) %all-reduce.11.cloned.1.call-update) | async-done | bytes 2097168 | tf_op jit(solution)/shard_map/psum | solution.py:713
  276.5 3.0 multiply_reduce_fusion.2
  279.5 2.7 add_add_fusion.2
  282.2 9.0 %add_convert_fusion = bf16[1024,2048]{1,0:T(8,128)(2,1)S(1)} fusion(f32[1024,2048]{1,0:T(8,128)} %get-tuple-element.99, f32[1024,2048]{1,0:T(8,128)} %get-tuple-element.130, bf16[2048,512]{1,0:T(8,128)(2,1)S(1)} %copy-done.64, f32[1024,512]{1,0:T(8,128)S(1)} %add_add_fusion.2), kind=kOutput, calls=%fused_computation.22 | convolution fusion | flops 2177368064 | bytes 25165824 | tf_op jit(solution)/shard_map/td,fd->tf/dot_general | solution.py:611
  291.2 2.6 multiply_reduce_fusion.3
  297.5 13.2 %multiply_reduce_fusion.1 = (f32[8,512]{1,0:T(8,128)S(1)}, f32[8,512,1024]{2,1,0:T(8,128)}) fusion(f32[8,512,1024]{2,1,0:T(8,128)} %copy-done.1, f32[8,512]{1,0:T(8,128)S(1)} %copy-done.47, pred[512,1024]{1,0:T(8,128)(4,1)S(1)} %copy-done.14, bf16[512,8,64]{0,2,1:T(8,128)(2,1)S(1)} %bitcast.137, f32[1,1024,3,8,64]{1,4,3,2,0:T(8,128)} %bitcast.125), kind=kOutput, calls=%fused_computation.9 | convolution fusion | flops 557838336 | bytes 35684352 | tf_op jit(solution)/shard_map/qhd,khd->hqk/dot_general | solution.py:533
  310.7 13.1 %multiply_convert_fusion.2 = bf16[8,512,1024]{2,1,0:T(8,128)(2,1)S(1)} fusion(f32[8,512,1024]{2,1,0:T(8,128)} %get-tuple-element.139, f32[8,512,1024]{2,1,0:T(8,128)} %copy-done.1, f32[8,512]{1,0:T(8,128)S(1)} %get-tuple-element.138, f32[8,512]{1,0:T(8,128)S(1)} %copy-done.47, pred[512,1024]{1,0:T(8,128)(4,1)S(1)} %copy-done.14), kind=kLoop, calls=%fused_computation.8 | loop fusion | flops 25165824 | bytes 42500096 | tf_op jit(solution)/shard_map/convert_element_type | solution.py:537
  323.9 2.9 fusion.60
  326.8 4.8 fusion.25
  331.7 6.7 %fusion.56 = f32[8,64,1024]{2,1,0:T(8,128)} fusion(bf16[512,8,64]{0,2,1:T(8,128)(2,1)} %bitcast.138, f32[8,512,1024]{2,1,0:T(8,128)S(1)} %bitcast.119, f32[8,512]{1,0:T(8,128)S(1)} %copy-done.47, pred[512,1024]{1,0:T(8,128)(4,1)S(1)} %copy-done.14), kind=kOutput, calls=%fused_computation.163 | convolution fusion | flops 553648128 | bytes 19939328 | tf_op jit(solution)/shard_map/hqk,qhd->khd/dot_general | solution.py:545
  338.4 4.6 fusion.63
  343.0 4.5 fusion.41
  349.2 13.2 %multiply_reduce_fusion = (f32[8,512]{1,0:T(8,128)S(1)}, f32[8,512,1024]{2,1,0:T(8,128)}) fusion(f32[8,512,1024]{2,1,0:T(8,128)} %copy-done, f32[8,512]{1,0:T(8,128)S(1)} %copy-done.45, pred[512,1024]{1,0:T(8,128)(4,1)S(1)} %copy-done.7, bf16[512,8,64]{0,2,1:T(8,128)(2,1)S(1)} %bitcast.136, f32[1,1024,3,8,64]{1,4,3,2,0:T(8,128)} %bitcast.126), kind=kOutput, calls=%fused_computation.7 | convolution fusion | flops 557838336 | bytes 35684352 | tf_op jit(solution)/shard_map/qhd,khd->hqk/dot_general | solution.py:533
  362.4 12.3 %multiply_convert_fusion.1 = bf16[8,512,1024]{2,1,0:T(8,128)(2,1)S(1)} fusion(f32[8,512,1024]{2,1,0:T(8,128)} %get-tuple-element.137, f32[8,512,1024]{2,1,0:T(8,128)} %copy-done, f32[8,512]{1,0:T(8,128)S(1)} %get-tuple-element.136, f32[8,512]{1,0:T(8,128)S(1)} %copy-done.45, pred[512,1024]{1,0:T(8,128)(4,1)S(1)} %copy-done.7), kind=kLoop, calls=%fused_computation.6 | loop fusion | flops 25165824 | bytes 42500096 | tf_op jit(solution)/shard_map/convert_element_type | solution.py:537
  374.7 3.6 fusion.24
  378.4 4.8 multiply_bitcast_fusion
  383.3 7.2 %fusion.23 = bf16[1024,1,8,64]{0,3,2,1:T(8,128)(2,1)} fusion(f32[8,64,1024]{2,1,0:T(8,128)} %fusion.56, bf16[512,8,64]{0,2,1:T(8,128)(2,1)} %bitcast.135, f32[8,512,1024]{2,1,0:T(8,128)S(1)} %bitcast.117, f32[8,512]{1,0:T(8,128)S(1)} %copy-done.45, pred[512,1024]{1,0:T(8,128)(4,1)} %copy-done.6), kind=kOutput, calls=%fused_computation.80 | convolution fusion | flops 554696704 | bytes 20987904 | tf_op jit(solution)/shard_map/hqk,qhd->khd/dot_general | solution.py:545
  393.8 3.5 fusion.13
  397.4 2.3 constant_dynamic-slice_fusion.1.refs_3_
  399.7 4.0 fusion.44
  406.9 2.3 constant_dynamic-slice_fusion.refs_4_
  409.2 19.8 %scatter_custom_fusion.refs_0_ = f32[8000,512]{1,0:T(8,128)} fusion(f32[8000,512]{1,0:T(8,128)} %fusion.65, s32[1024]{0:T(1024)} %bitcast.160, f32[1024,512]{1,0:T(8,128)S(1)} %copy-done.3, bf16[1024,512]{1,0:T(8,128)(2,1)S(1)} %copy-done.28, f32[1024,512]{1,0:T(8,128)} %get-tuple-element.140, f32[1024]{0:T(1024)S(1)} %multiply_multiply_fusion.5, ...), kind=kCustom, calls=%fused_computation.53 | custom fusion | flops 4718592 | bytes 21638656 | tf_op jit(solution)/shard_map/scatter-add | solution.py:721
  428.9 16.7 %sketch.1 = (f32[8,8192]{1,0:T(8,128)}, f32[8,8192]{1,0:T(8,128)}, f32[8,896]{1,0:T(8,128)}, f32[8,896]{1,0:T(8,128)}, f32[8,512]{1,0:T(8,128)}) custom-call(f32[8000,512]{1,0:T(8,128)} %scatter_custom_fusion.refs_0_, f32[128,1536]{1,0:T(8,128)} %constant_dynamic-slice_fusion.3.refs_1_, f32[128,512]{1,0:T(8,128)} %constant_dynamic-slice_fusion.2.refs_2_, ...), custom_call_target="tpu_custom_call" | custom-call | tf_op jit(solution)/shard_map/sketch/pallas_call | solution.py:140
  445.6 24.6 %basis.1 = (f32[8,8192]{1,0:T(8,128)}, f32[8,896]{1,0:T(8,128)}, f32[8,256]{1,0:T(8,128)}, f32[8,128]{1,0:T(8,128)}) custom-call(f32[8,8192]{1,0:T(8,128)} %get-tuple-element.53.gq_ref, f32[8,8192]{1,0:T(8,128)} %get-tuple-element.54.eq_ref, f32[8,896]{1,0:T(8,128)} %get-tuple-element.55.gs_ref, f32[8,896]{1,0:T(8,128)} %get-tuple-element.56.es_ref, ...), custom_call_target="tpu_custom_call" | custom-call | tf_op jit(solution)/shard_map/basis/pallas_call | solution.py:318
  470.3 23.5 %residual.1 = (f32[8000,512]{1,0:T(8,128)}, f32[128,1536]{1,0:T(8,128)}, f32[128,512]{1,0:T(8,128)}, f32[128,2048]{1,0:T(8,128)}, f32[512,512]{1,0:T(8,128)}, /*...) custom-call(f32[8000,512]{1,0:T(8,128)} %scatter_custom_fusion.refs_0_, ...), custom_call_target="tpu_custom_call" | custom-call | tf_op jit(solution)/shard_map/residual/pallas_call | solution.py:380
  493.8 18.4 %mean_right.1.refs_11_ = f32[8,5120]{1,0:T(8,128)} custom-call(f32[8,512]{1,0:T(8,128)} %get-tuple-element.61.r0, f32[8,1536]{1,0:T(8,128)} %get-tuple-element.62.r1, f32[8,512]{1,0:T(8,128)} %get-tuple-element.63.r2, f32[8,2048]{1,0:T(8,128)} %get-tuple-element.64.r3, f32[8,512]{1,0:T(8,128)} %get-tuple-element.65.r4), custom_call_target="tpu_custom_call" | custom-call | tf_op jit(solution)/shard_map/mean_right/pallas_call | solution.py:419
  518.4 18.3 %update.1 = (f32[8000,512]{1,0:T(8,128)}, f32[128,1536]{1,0:T(8,128)}, f32[128,512]{1,0:T(8,128)}, f32[128,2048]{1,0:T(8,128)}, f32[512,512]{1,0:T(8,128)}, /*in...) custom-call(bf16[8000,512]{1,0:T(8,128)(2,1)} %refs_0_.1, ...), custom_call_target="tpu_custom_call" | custom-call | tf_op jit(solution)/shard_map/update/pallas_call | solution.py:461
  (215 shorter events, 32.2 us)
Async XLA Ops:
  7.2 61.6 %all-reduce.9.cloned.1.call-start = ((), (), s32[]{:S(2)}) async-start(), calls=%async_computation | async-start | bytes 2097152 | tf_op jit(solution)/shard_map/psum | solution.py:687
  8.7 17.4 %copy-start.55 = (pred[1024]{0:T(1024)(128)(4,1)}, pred[1024]{0:T(1024)(128)(4,1)S(1)}, u32[]{:S(2)}) copy-start(pred[1024]{0:T(1024)(128)(4,1)S(1)} %and_reduce_fusion) | copy-start | bytes 3076
  17.5 11.9 %copy-start.31 = (f32[128,2048]{1,0:T(8,128)S(1)}, f32[128,2048]{1,0:T(8,128)}, u32[]{:S(2)}) copy-start(f32[128,2048]{1,0:T(8,128)} %refs_7_.1) | copy-start | bytes 3145732
  17.5 12.9 %copy-start.32 = (f32[512,512]{1,0:T(8,128)S(1)}, f32[512,512]{1,0:T(8,128)}, u32[]{:S(2)}) copy-start(f32[512,512]{1,0:T(8,128)} %refs_8_.1) | copy-start | bytes 3145732
  17.5 14.0 %copy-start.60 = (f32[3,512]{1,0:T(4,128)S(1)}, f32[3,512]{1,0:T(4,128)}, u32[]{:S(2)}) copy-start(f32[3,512]{1,0:T(4,128)} %param.31) | copy-start | bytes 18436
  17.5 14.4 %copy-start.42 = (f32[128,512]{1,0:T(8,128)S(1)}, f32[128,512]{1,0:T(8,128)}, u32[]{:S(2)}) copy-start(f32[128,512]{1,0:T(8,128)} %refs_6_.1) | copy-start | bytes 786436
  17.5 25.4 %copy-start.62 = (s32[1,1024]{1,0:T(1,128)S(1)}, s32[1,1024]{1,0:T(1,128)}, u32[]{:S(2)}) copy-start(s32[1,1024]{1,0:T(1,128)} %param.25) | copy-start | bytes 12292
  27.4 63.6 %all-gather.4.cloned.1.call-start = ((), (), s32[]{:S(2)}) async-start(), calls=%async_computation.1 | async-start | bytes 1966080 | tf_op jit(solution)/shard_map/all_gather | solution.py:678
  29.4 99.3 %all-gather.6.cloned.1.call-start = ((), (), s32[]{:S(2)}) async-start(), calls=%async_computation.2 | async-start | bytes 2621440 | tf_op jit(solution)/shard_map/all_gather | solution.py:680
  30.3 122.8 %all-gather.8.cloned.1.call-start = ((), (), s32[]{:S(2)}) async-start(), calls=%async_computation.3 | async-start | bytes 2621440 | tf_op jit(solution)/shard_map/all_gather | solution.py:681
  31.3 245.2 %all-reduce.11.cloned.1.call-start = ((), (), s32[]{:S(2)}) async-start(), calls=%async_computation.4 | async-start | bytes 4194304 | tf_op jit(solution)/shard_map/psum | solution.py:713
  31.5 73.7 %copy-start.13 = (pred[512,1024]{1,0:T(8,128)(4,1)}, pred[512,1024]{1,0:T(8,128)(4,1)S(1)}, u32[]{:S(2)}) copy-start(pred[512,1024]{1,0:T(8,128)(4,1)S(1)} %iota_compare_fusion.2) | copy-start | bytes 1572868
  31.6 63.7 %copy-start.57 = (f32[1,512]{1,0:T(1,128)}, f32[1,512]{1,0:T(1,128)S(1)}, u32[]{:S(2)}) copy-start(f32[1,512]{1,0:T(1,128)S(1)} %get-tuple-element.120) | copy-start | bytes 6148
  32.0 88.1 %copy-start.6 = (pred[512,1024]{1,0:T(8,128)(4,1)}, pred[512,1024]{1,0:T(8,128)(4,1)S(1)}, u32[]{:S(2)}) copy-start(pred[512,1024]{1,0:T(8,128)(4,1)S(1)} %iota_compare_fusion.1) | copy-start | bytes 1572868
  43.0 84.7 %copy-start.34 = (bf16[512,512]{1,0:T(8,128)(2,1)}, bf16[512,512]{1,0:T(8,128)(2,1)S(1)}, u32[]{:S(2)}) copy-start(bf16[512,512]{1,0:T(8,128)(2,1)S(1)} %all_gather.13) | copy-start | bytes 1572868
  43.5 51.8 %copy-start.38 = (f32[1024,32]{0,1:T(8,128)}, f32[1024,32]{0,1:T(8,128)S(1)}, u32[]{:S(2)}) copy-start(f32[1024,32]{0,1:T(8,128)S(1)} %get-tuple-element.122) | copy-start | bytes 393220
  43.5 51.8 %copy-start.40 = (f32[1024,32]{0,1:T(8,128)}, f32[1024,32]{0,1:T(8,128)S(1)}, u32[]{:S(2)}) copy-start(f32[1024,32]{0,1:T(8,128)S(1)} %get-tuple-element.123) | copy-start | bytes 393220
  70.3 25.1 %copy-start.48 = (f32[1024]{0:T(1024)}, f32[1024]{0:T(1024)S(1)}, u32[]{:S(2)}) copy-start(f32[1024]{0:T(1024)S(1)} %fusion.19) | copy-start | bytes 12292
  70.3 25.0 %copy-start.50 = (f32[1024]{0:T(1024)}, f32[1024]{0:T(1024)S(1)}, u32[]{:S(2)}) copy-start(f32[1024]{0:T(1024)S(1)} %fusion.49) | copy-start | bytes 12292
  96.1 16.4 %copy-start.15 = (bf16[1024,8,32]{0,2,1:T(8,128)(2,1)}, bf16[1024,8,32]{0,2,1:T(8,128)(2,1)S(1)}, u32[]{:S(2)}) copy-start(bf16[1024,8,32]{0,2,1:T(8,128)(2,1)S(1)} %get-tuple-element.114) | copy-start | bytes 1572868
  96.1 16.4 %copy-start.17 = (bf16[1024,8,32]{0,2,1:T(8,128)(2,1)}, bf16[1024,8,32]{0,2,1:T(8,128)(2,1)S(1)}, u32[]{:S(2)}) copy-start(bf16[1024,8,32]{0,2,1:T(8,128)(2,1)S(1)} %get-tuple-element.115) | copy-start | bytes 1572868
  96.1 16.4 %copy-start.19 = (bf16[1024,8,32]{0,2,1:T(8,128)(2,1)}, bf16[1024,8,32]{0,2,1:T(8,128)(2,1)S(1)}, u32[]{:S(2)}) copy-start(bf16[1024,8,32]{0,2,1:T(8,128)(2,1)S(1)} %get-tuple-element.106) | copy-start | bytes 1572868
  96.1 16.4 %copy-start.21 = (bf16[1024,8,32]{0,2,1:T(8,128)(2,1)}, bf16[1024,8,32]{0,2,1:T(8,128)(2,1)S(1)}, u32[]{:S(2)}) copy-start(bf16[1024,8,32]{0,2,1:T(8,128)(2,1)S(1)} %get-tuple-element.107) | copy-start | bytes 1572868
  128.6 24.6 %copy-start.52 = (f32[1024]{0:T(1024)}, f32[1024]{0:T(1024)S(1)}, u32[]{:S(2)}) copy-start(f32[1024]{0:T(1024)S(1)} %get-tuple-element.128) | copy-start | bytes 12292
  128.6 165.3 %copy-start.4 = (f32[1024,512]{1,0:T(8,128)}, f32[1024,512]{1,0:T(8,128)S(1)}, u32[]{:S(2)}) copy-start(f32[1024,512]{1,0:T(8,128)S(1)} %get-tuple-element.129) | copy-start | bytes 6291460
  158.5 19.3 %copy-start.12 = (f32[1024,512]{1,0:T(8,128)}, f32[1024,512]{1,0:T(8,128)S(1)}, u32[]{:S(2)}) copy-start(f32[1024,512]{1,0:T(8,128)S(1)} %get-tuple-element.132) | copy-start | bytes 6291460
  282.2 11.7 %copy-start.23 = (f32[1024,512]{1,0:T(8,128)}, f32[1024,512]{1,0:T(8,128)S(1)}, u32[]{:S(2)}) copy-start(f32[1024,512]{1,0:T(8,128)S(1)} %add_add_fusion.2) | copy-start | bytes 6291460
  282.2 9.0 %copy-start.63 = (bf16[512,2048]{1,0:T(8,128)(2,1)S(1)}, bf16[512,2048]{1,0:T(8,128)(2,1)}, u32[]{:S(2)}) copy-start(bf16[512,2048]{1,0:T(8,128)(2,1)} %all-gather.6.cloned.1.call-done) | copy-start | bytes 6291460
  297.5 13.2 %copy-start.37 = (bf16[512,512]{0,1:T(8,128)(2,1)}, bf16[512,512]{0,1:T(8,128)(2,1)S(1)}, u32[]{:S(2)}) copy-start(bf16[512,512]{0,1:T(8,128)(2,1)S(1)} %get-tuple-element.111) | copy-start | bytes 1572868
  310.7 13.2 %copy-start.16 = (bf16[1024,8,32]{0,2,1:T(8,128)(2,1)S(1)}, bf16[1024,8,32]{0,2,1:T(8,128)(2,1)}, u32[]{:S(2)}) copy-start(bf16[1024,8,32]{0,2,1:T(8,128)(2,1)} %copy-done.15) | copy-start | bytes 1572868
  310.7 13.2 %copy-start.18 = (bf16[1024,8,32]{0,2,1:T(8,128)(2,1)S(1)}, bf16[1024,8,32]{0,2,1:T(8,128)(2,1)}, u32[]{:S(2)}) copy-start(bf16[1024,8,32]{0,2,1:T(8,128)(2,1)} %copy-done.17) | copy-start | bytes 1572868
  310.7 21.0 %slice-start.4 = ((s8[16777216]{0:T(1024)(128)(4,1)}), s8[4194304]{0:T(1024)(128)(4,1)S(1)}, s32[]{:S(2)}) async-start(s8[16777216]{0:T(1024)(128)(4,1)} %bitcast.118), calls=%async_computation.9 | async-start | bytes 8388608
  310.7 20.9 %slice-start.5 = ((s8[16777216]{0:T(1024)(128)(4,1)}), s8[4194304]{0:T(1024)(128)(4,1)S(1)}, s32[]{:S(2)}) async-start(s8[16777216]{0:T(1024)(128)(4,1)} %bitcast.118), calls=%async_computation.10 | async-start | bytes 8388608
  310.7 20.9 %slice-start.6 = ((s8[16777216]{0:T(1024)(128)(4,1)}), s8[4194304]{0:T(1024)(128)(4,1)S(1)}, s32[]{:S(2)}) async-start(s8[16777216]{0:T(1024)(128)(4,1)} %bitcast.118), calls=%async_computation.11 | async-start | bytes 8388608
  323.8 7.8 %slice-start.7 = ((s8[16777216]{0:T(1024)(128)(4,1)}), s8[4194304]{0:T(1024)(128)(4,1)S(1)}, s32[]{:S(2)}) async-start(s8[16777216]{0:T(1024)(128)(4,1)} %bitcast.118), calls=%async_computation.12 | async-start | bytes 8388608
  362.4 12.3 %copy-start.20 = (bf16[1024,8,32]{0,2,1:T(8,128)(2,1)S(1)}, bf16[1024,8,32]{0,2,1:T(8,128)(2,1)}, u32[]{:S(2)}) copy-start(bf16[1024,8,32]{0,2,1:T(8,128)(2,1)} %copy-done.19) | copy-start | bytes 1572868
  362.4 12.3 %copy-start.22 = (bf16[1024,8,32]{0,2,1:T(8,128)(2,1)S(1)}, bf16[1024,8,32]{0,2,1:T(8,128)(2,1)}, u32[]{:S(2)}) copy-start(bf16[1024,8,32]{0,2,1:T(8,128)(2,1)} %copy-done.21) | copy-start | bytes 1572868
  374.7 8.5 %slice-start = ((s8[16777216]{0:T(1024)(128)(4,1)}), s8[4194304]{0:T(1024)(128)(4,1)S(1)}, s32[]{:S(2)}) async-start(s8[16777216]{0:T(1024)(128)(4,1)} %bitcast.116), calls=%async_computation.5 | async-start | bytes 8388608
  374.7 8.5 %slice-start.1 = ((s8[16777216]{0:T(1024)(128)(4,1)}), s8[4194304]{0:T(1024)(128)(4,1)S(1)}, s32[]{:S(2)}) async-start(s8[16777216]{0:T(1024)(128)(4,1)} %bitcast.116), calls=%async_computation.6 | async-start | bytes 8388608
  383.2 7.3 %copy-start.8 = (f32[1024,8,64]{0,2,1:T(8,128)S(1)}, f32[1024,8,64]{0,2,1:T(8,128)}, u32[]{:S(2)}) copy-start(f32[1024,8,64]{0,2,1:T(8,128)} %multiply_bitcast_fusion) | copy-start | bytes 6291460
  383.2 7.3 %copy-start.25 = (f32[512,8,64]{0,2,1:T(8,128)S(1)}, f32[512,8,64]{0,2,1:T(8,128)}, u32[]{:S(2)}) copy-start(f32[512,8,64]{0,2,1:T(8,128)} %fusion.25) | copy-start | bytes 3145732
  383.2 7.3 %copy-start.26 = (f32[512,8,64]{0,2,1:T(8,128)S(1)}, f32[512,8,64]{0,2,1:T(8,128)}, u32[]{:S(2)}) copy-start(f32[512,8,64]{0,2,1:T(8,128)} %fusion.24) | copy-start | bytes 3145732
  383.2 7.3 %copy-start.39 = (f32[1024,32]{0,1:T(8,128)S(1)}, f32[1024,32]{0,1:T(8,128)}, u32[]{:S(2)}) copy-start(f32[1024,32]{0,1:T(8,128)} %copy-done.38) | copy-start | bytes 393220
  383.3 7.3 %copy-start.41 = (f32[1024,32]{0,1:T(8,128)S(1)}, f32[1024,32]{0,1:T(8,128)}, u32[]{:S(2)}) copy-start(f32[1024,32]{0,1:T(8,128)} %copy-done.40) | copy-start | bytes 393220
  397.3 7.3 %copy-start.49 = (f32[1024]{0:T(1024)S(1)}, f32[1024]{0:T(1024)}, u32[]{:S(2)}) copy-start(f32[1024]{0:T(1024)} %copy-done.48) | copy-start | bytes 12292
  397.3 11.9 %copy-start.56 = (pred[1024]{0:T(1024)(128)(4,1)S(1)}, pred[1024]{0:T(1024)(128)(4,1)}, u32[]{:S(2)}) copy-start(pred[1024]{0:T(1024)(128)(4,1)} %copy-done.55) | copy-start | bytes 3076
  470.3 47.4 %copy-start.59 = (f32[8,256]{1,0:T(8,128)S(1)}, f32[8,256]{1,0:T(8,128)}, u32[]{:S(2)}) copy-start(f32[8,256]{1,0:T(8,128)} %get-tuple-element.71) | copy-start | bytes 24580
  470.3 47.5 %copy-start.61 = (bf16[3,512]{1,0:T(4,128)(2,1)S(1)}, bf16[3,512]{1,0:T(4,128)(2,1)}, u32[]{:S(2)}) copy-start(bf16[3,512]{1,0:T(4,128)(2,1)} %param.37) | copy-start | bytes 9220
  (32 other events, 132.5 us)
Sparse Core Ops, SparseCore 0:
  27.5 41.1 all-reduce.8
  70.9 20.0 all-gather.3
  93.2 22.5 all-gather.5
  117.8 22.5 all-gather.7
  224.2 52.2 all-reduce.10

commit v2 on v1

--- a/solution.py
+++ b/solution.py
@@ -7,11 +7,9 @@
 from jax.experimental.pallas import tpu as pltpu
 from jax.sharding import PartitionSpec as P
 
-HEADS = 8
 HD = 64
 
 
-HIGHEST_PREC = lax.Precision.HIGHEST
 MOMENTUM = 0.9
 LEARN_RATE = 10.0
 CLIP_NORM = 1.0
@@ -473,172 +471,786 @@
     return out[:5], out[5:]
 
 
-def rms_norm(values, weight):
-    return values * lax.rsqrt(jnp.mean(values * values, axis=-1, keepdims=True) + 1e-06) * weight
-
-
-def rotate(heads_in, length):
-    halfway = heads_in.shape[-1] // 2
-    positions = jnp.arange(length).astype(jnp.float32)
-    inverse = 10000.0 ** (-jnp.arange(halfway).astype(jnp.float32) / halfway)
-    angles = positions[:, None] * inverse[None, :]
-    cosine_table = jnp.cos(angles)[:, None, :]
-    sine_table = jnp.sin(angles)[:, None, :]
-    first_half = heads_in[..., :halfway]
-    second_half = heads_in[..., halfway:]
-    return jnp.concatenate(
-        [
-            first_half * cosine_table - second_half * sine_table,
-            first_half * sine_table + second_half * cosine_table,
+EPS = 1e-06
+QB = 256
+INV_SQRT2 = 0.7071067811865476
+INV_SQRT_2PI = 0.3989422804014327
+
+
+def nt_dot(a, b):
+    return lax.dot_general(a, b, (((1,), (1,)), ((), ())), preferred_element_type=F32)
+
+
+def nn_dot(a, b):
+    return jnp.dot(a, b, preferred_element_type=F32)
+
+
+def scaled_rms(value, gain):
+    return value * lax.rsqrt(jnp.mean(value * value, axis=1, keepdims=True) + EPS) * gain
+
+
+def rms_back(grad, value, gain):
+    inverse = lax.rsqrt(jnp.mean(value * value, axis=1, keepdims=True) + EPS)
+    scaled = grad * gain
+    along = jnp.mean(scaled * value, axis=1, keepdims=True)
+    back = inverse * (scaled - value * (inverse * inverse * along))
+    return back, jnp.sum(grad * value * inverse, axis=0, keepdims=True)
+
+
+def turned(value_t, cos_t, sin_t, half):
+    first, second = value_t[:half], value_t[half:]
+    return jnp.concatenate([first * cos_t - second * sin_t, first * sin_t + second * cos_t], axis=0)
+
+
+def turned_back(value_t, cos_t, sin_t, half):
+    first, second = value_t[:half], value_t[half:]
+    return jnp.concatenate([first * cos_t + second * sin_t, second * cos_t - first * sin_t], axis=0)
+
+
+def causal_tile(scores_t, fill):
+    size = scores_t.shape[1]
+    key_at = lax.broadcasted_iota(jnp.int32, (size, size), 0)
+    query_at = lax.broadcasted_iota(jnp.int32, (size, size), 1)
+    tail = jnp.where(key_at <= query_at, scores_t[-size:], fill)
+    if scores_t.shape[0] == size:
+        return tail
+    return jnp.concatenate([scores_t[:-size], tail], axis=0)
+
+
+def forward_kernel(
+    shards, axis,
+    x0_ref, gains_ref, cos_ref, sin_ref, wqkv_ref, wo_own, wu_own, wd_own,
+    n1_ref, qkv_ref, lse_ref, mixed_ref, x1_ref, n2_ref, x2_ref, n3_ref, wo_all, wu_all, wd_all, hid_any,
+    hid_ref, hid_sem, wo_sems, wu_sems, wd_sems,
+):
+    tokens, width = x0_ref.shape
+    half = HD // 2
+    row_blocks = tokens // QB
+    greet_all(axis, shards)
+    shard = lax.axis_index(axis)
+    spreads = []
+    for own, full, sems in ((wo_own, wo_all, wo_sems), (wu_own, wu_all, wu_sems), (wd_own, wd_all, wd_sems)):
+        full[shard] = own[...].astype(BF16)
+        spreads.append(Spread(full, axis, shards, sems))
+    pl.semaphore_wait(pltpu.get_barrier_semaphore(), shards - 1)
+    for spread in spreads:
+        spread.start()
+
+    @pl.loop(0, row_blocks)
+    def _(block):
+        rows = pl.ds(pl.multiple_of(block * QB, QB), QB)
+        n1_ref[rows, :] = scaled_rms(x0_ref[rows, :].astype(F32), gains_ref[0:1, :]).astype(BF16)
+
+    group = 4 * HD
+
+    @pl.loop(0, width // group)
+    def _(at):
+        n1 = n1_ref[...]
+        for part in range(3):
+            start = pl.multiple_of(part * width + at * group, group)
+            packed_t = nn_dot(n1, wqkv_ref[:, pl.ds(start, group)]).T
+            if part < 2:
+                cos_t, sin_t = cos_ref[...], sin_ref[...]
+                packed_t = jnp.concatenate(
+                    [
+                        turned(packed_t[head * HD : (head + 1) * HD], cos_t, sin_t, half)
+                        for head in range(4)
+                    ],
+                    axis=0,
+                )
+            if part == 0:
+                packed_t = packed_t * HD ** (-0.5)
+            qkv_ref[part, pl.ds(pl.multiple_of(at * group, group), group), :] = packed_t.astype(BF16)
+
+    spreads[0].relay()
+
+    def attend(head):
+        rows = pl.ds(pl.multiple_of(head * HD, HD), HD)
+        query_t, key_t, value_t = qkv_ref[0, rows, :], qkv_ref[1, rows, :], qkv_ref[2, rows, :]
+        keys = key_t.T
+        mixed_parts, lse_parts = [], []
+        for block in range(row_blocks):
+            count = (block + 1) * QB
+            scores = causal_tile(
+                nn_dot(keys[:count], query_t[:, block * QB : count]), -1e30
+            )
+            top = jnp.max(scores, axis=0, keepdims=True)
+            weight = jnp.exp(scores - top)
+            total = jnp.sum(weight, axis=0, keepdims=True)
+            probs = (weight * (1.0 / total)).astype(BF16)
+            mixed_parts.append(nn_dot(value_t[:, :count], probs))
+            lse_parts.append(top + jnp.log(total))
+        mixed_ref[rows, :] = jnp.concatenate(mixed_parts, axis=1).astype(BF16)
+        lse_ref[head] = jnp.concatenate(lse_parts, axis=1)
+
+    heads = width // HD
+    pl.loop(0, heads // 2)(attend)
+    spreads[1].relay()
+    pl.loop(heads // 2, heads)(attend)
+    spreads[0].finish()
+    spreads[2].relay()
+    @pl.loop(0, row_blocks)
+    def _(block):
+        rows = pl.ds(pl.multiple_of(block * QB, QB), QB)
+        mixed = mixed_ref[:, rows].T
+        stream = x0_ref[rows, :].astype(F32) + nn_dot(mixed, wo_all[...].reshape(width, width))
+        x1_ref[rows, :] = stream
+        x2_ref[rows, :] = stream
+        n2_ref[rows, :] = scaled_rms(stream, gains_ref[1:2, :]).astype(BF16)
+
+    spreads[1].finish()
+    spreads[2].finish()
+    chunk = hid_ref.shape[2]
+    chunks = wu_all.shape[2] // chunk
+    parts = chunk // wd_all.shape[1]
+
+    def put(slot, at):
+        return pltpu.make_async_copy(
+            hid_ref.at[slot],
+            hid_any.at[:, pl.ds(pl.multiple_of(at * chunk, chunk), chunk)],
+            hid_sem.at[slot],
+        )
+
+    @pl.loop(0, chunks)
+    def _(at):
+        slot = lax.rem(at, 2)
+        lanes = pl.ds(pl.multiple_of(at * chunk, chunk), chunk)
+
+        @pl.when(at >= 2)
+        def _():
+            put(slot, at - 2).wait()
+
+        for block in range(row_blocks):
+            rows = slice(block * QB, (block + 1) * QB)
+            hidden = nn_dot(n2_ref[rows, :], wu_all[:, :, lanes].reshape(width, chunk))
+            hid_ref[slot, rows, :] = hidden
+            active = (0.5 * hidden * (1.0 + lax.erf(hidden * INV_SQRT2))).astype(BF16)
+            down = wd_all[pl.ds(at * parts, parts)].reshape(chunk, width)
+            x2_ref[rows, :] += nn_dot(active, down)
+        put(slot, at).start()
+
+    @pl.loop(0, row_blocks)
+    def _(block):
+        rows = pl.ds(pl.multiple_of(block * QB, QB), QB)
+        n3_ref[rows, :] = scaled_rms(x2_ref[rows, :], gains_ref[2:3, :]).astype(BF16)
+
+    for at in range(max(0, chunks - 2), chunks):
+        put(at % 2, at).wait()
+
+
+VM = pl.BlockSpec(memory_space=pltpu.VMEM)
+ANYWHERE = pl.BlockSpec(memory_space=pl.ANY)
+
+
+def layer_forward(x0, gains, cos_t, sin_t, wqkv, slices, shards, axis):
+    tokens, width = x0.shape
+    hidden = slices[1].shape[1]
+    shape = jax.ShapeDtypeStruct
+    chunk = min(512, hidden)
+    sems = pltpu.SemaphoreType.DMA((4, max(2, shards // 2)))
+    return pl.pallas_call(
+        functools.partial(forward_kernel, shards, axis),
+        in_specs=[VM] * 8,
+        out_specs=[VM] * 11 + [ANYWHERE],
+        out_shape=[
+            shape((tokens, width), BF16),
+            shape((3, width, tokens), BF16),
+            shape((width // HD, 1, tokens), F32),
+            shape((width, tokens), BF16),
+            shape((tokens, width), F32),
+            shape((tokens, width), BF16),
+            shape((tokens, width), F32),
+            shape((tokens, width), BF16),
+        ]
+        + [shape((shards, *w.shape), BF16) for w in slices]
+        + [shape((tokens, hidden), F32)],
+        scratch_shapes=[
+            pltpu.VMEM((2, tokens, chunk), F32),
+            pltpu.SemaphoreType.DMA((2,)),
+            sems,
+            sems,
+            sems,
         ],
-        axis=-1,
+        compiler_params=pltpu.CompilerParams(
+            collective_id=5, has_side_effects=True, vmem_limit_bytes=60 << 20
+        ),
+        name="layer_forward",
+    )(x0, gains, cos_t, sin_t, wqkv, *slices)
+
+
+def backward_kernel(shard_axis, *refs):
+    anys, refs = refs[:13], refs[13:]
+    gains_ref, cos_ref, sin_ref, lse_ref = refs[0:4]
+    dx0_ref, gqkv_ref, gout_ref, gup_ref, gdown_ref, ggains_ref = refs[4:10]
+    kept, refs = refs[10:23], refs[23:]
+    dn3_ref, x2_ref, hid_ref, wd_ref, wu_ref, x1_ref, n2_ref, wo_ref, mixed_ref, qkv_ref, x0_ref, n1_ref, wqkv_ref = kept
+    grad_ref, part_ref, low_ref, act_ref, dhid_ref, dmixed_ref, dpacked_ref, turn_ref, load_sem = refs
+    shard = lax.axis_index(shard_axis) if shard_axis else 0
+    tokens, width = x2_ref.shape
+    half = HD // 2
+    row_blocks = tokens // QB
+    loads = [
+        pltpu.make_async_copy(src, dst, load_sem.at[at])
+        for at, (src, dst) in enumerate(zip(anys, kept))
+    ]
+    for load in loads:
+        load.start()
+
+    def block_rows(block):
+        return pl.ds(pl.multiple_of(block * QB, QB), QB)
+
+    loads[0].wait()
+    loads[1].wait()
+    ggains_ref[...] = jnp.zeros_like(ggains_ref)
+
+    @pl.loop(0, row_blocks)
+    def _(block):
+        rows = block_rows(block)
+        back, gain = rms_back(dn3_ref[:, rows].T, x2_ref[rows, :], gains_ref[2:3, :])
+        grad_ref[rows, :] = back
+        low_ref[rows, :] = back.astype(BF16)
+        part_ref[rows, :] = jnp.zeros_like(back)
+        ggains_ref[2:3, :] += gain
+
+    for at in (2, 3, 4):
+        loads[at].wait()
+    chunk = min(512, wu_ref.shape[1])
+
+    @pl.loop(0, wu_ref.shape[1] // chunk)
+    def _(at):
+        lanes = pl.ds(pl.multiple_of(at * chunk, chunk), chunk)
+        for block in range(row_blocks):
+            rows = slice(block * QB, (block + 1) * QB)
+            grad_act = nt_dot(low_ref[rows, :], wd_ref[lanes, :])
+            hidden = hid_ref[rows, lanes]
+            share = 0.5 + 0.5 * lax.erf(hidden * INV_SQRT2)
+            slope = share + hidden * (INV_SQRT_2PI * jnp.exp(-0.5 * hidden * hidden))
+            act_ref[rows, lanes] = (hidden * share).astype(BF16)
+            grad_hid = (slope * grad_act).astype(BF16)
+            dhid_ref[rows, lanes] = grad_hid
+            part_ref[rows, :] += nt_dot(grad_hid, wu_ref[:, lanes])
+
+    own = gdown_ref.shape[0]
+    gdown_ref[...] = nn_dot(act_ref[:, pl.ds(pl.multiple_of(shard * own, own), own)].T, low_ref[...])
+    loads[5].wait()
+    loads[6].wait()
+    own = gup_ref.shape[0]
+    turn_ref[...] = n2_ref[...].T
+    own_rows = pl.ds(pl.multiple_of(shard * own, own), own)
+
+    @pl.loop(0, wu_ref.shape[1] // chunk)
+    def _(at):
+        lanes = pl.ds(pl.multiple_of(at * chunk, chunk), chunk)
+        gup_ref[:, lanes] = nn_dot(turn_ref[own_rows, :], dhid_ref[:, lanes])
+
+    loads[7].wait()
+
+    @pl.loop(0, row_blocks)
+    def _(block):
+        rows = block_rows(block)
+        back, gain = rms_back(part_ref[rows, :], x1_ref[rows, :], gains_ref[1:2, :])
+        back = grad_ref[rows, :] + back
+        grad_ref[rows, :] = back
+        low = back.astype(BF16)
+        low_ref[rows, :] = low
+        ggains_ref[1:2, :] += gain
+        dmixed_ref[:, rows] = nt_dot(low, wo_ref[...]).astype(BF16).T
+
+    loads[8].wait()
+    loads[9].wait()
+    own = gout_ref.shape[0]
+    own_rows = pl.ds(pl.multiple_of(shard * own, own), own)
+    gout_ref[...] = nn_dot(mixed_ref[own_rows, :], low_ref[...])
+
+    @pl.loop(0, width // (2 * HD))
+    def _(pair):
+        made = ([], [], [])
+        for side in range(2):
+            head = pair * 2 + side
+            rows = pl.ds(pl.multiple_of(head * HD, HD), HD)
+            query_t, key_t, value_t = qkv_ref[0, rows, :], qkv_ref[1, rows, :], qkv_ref[2, rows, :]
+            dmix_t = dmixed_ref[rows, :]
+            query, key, value, dmix = query_t.T, key_t.T, value_t.T, dmix_t.T
+            lse = lse_ref[head]
+            dquery_parts = []
+            dkey = [None] * row_blocks
+            dvalue = [None] * row_blocks
+            for block in range(row_blocks):
+                count = (block + 1) * QB
+                at = slice(block * QB, count)
+                scores = nn_dot(key[:count], query_t[:, at])
+                probs = causal_tile(jnp.exp(scores - lse[:, at]), 0.0)
+                dprobs = nn_dot(value[:count], dmix_t[:, at])
+                delta = jnp.sum(probs * dprobs, axis=0, keepdims=True)
+                dscores = (probs * (dprobs - delta)).astype(BF16)
+                dquery_parts.append(nn_dot(key_t[:, :count], dscores))
+                more_key = nn_dot(dscores, query[at])
+                more_value = nn_dot(probs.astype(BF16), dmix[at])
+                for piece in range(block + 1):
+                    cut = slice(piece * QB, (piece + 1) * QB)
+                    if dkey[piece] is None:
+                        dkey[piece], dvalue[piece] = more_key[cut], more_value[cut]
+                    else:
+                        dkey[piece] = dkey[piece] + more_key[cut]
+                        dvalue[piece] = dvalue[piece] + more_value[cut]
+            cos_t, sin_t = cos_ref[...], sin_ref[...]
+            dquery_t = jnp.concatenate(dquery_parts, axis=1) * HD ** (-0.5)
+            dkey_t = jnp.concatenate(dkey, axis=0).T
+            made[0].append(turned_back(dquery_t, cos_t, sin_t, half).T)
+            made[1].append(turned_back(dkey_t, cos_t, sin_t, half).T)
+            made[2].append(jnp.concatenate(dvalue, axis=0))
+        for part in range(3):
+            lanes = pl.ds(pl.multiple_of(part * width + pair * 2 * HD, 2 * HD), 2 * HD)
+            dpacked_ref[:, lanes] = jnp.concatenate(made[part], axis=1).astype(BF16)
+
+    for at in (10, 11, 12):
+        loads[at].wait()
+    own = gqkv_ref.shape[0]
+    turn_ref[...] = n1_ref[...].T
+    own_rows = pl.ds(pl.multiple_of(shard * own, own), own)
+
+    @pl.loop(0, 3)
+    def _(at):
+        lanes = pl.ds(pl.multiple_of(at * width, width), width)
+        gqkv_ref[:, lanes] = nn_dot(turn_ref[own_rows, :], dpacked_ref[:, lanes])
+
+    @pl.loop(0, row_blocks)
+    def _(block):
+        rows = block_rows(block)
+        back, gain = rms_back(
+            nt_dot(dpacked_ref[rows, :], wqkv_ref[...]), x0_ref[rows, :].astype(F32), gains_ref[0:1, :]
+        )
+        dx0_ref[rows, :] = grad_ref[rows, :] + back
+        ggains_ref[0:1, :] += gain
+
+
+def layer_backward(shard_axis, slice_shapes, dn3_t, gains, cos_t, sin_t, projections, x0, kept):
+    n1, qkv, lse, mixed_t, x1, n2, x2, _, hid = kept
+    wqkv, wo, wu, wd = projections
+    tokens, width = x2.shape
+    shape = jax.ShapeDtypeStruct
+    moved = (dn3_t, x2, hid, wd, wu, x1, n2, wo, mixed_t, qkv, x0, n1, wqkv)
+    return pl.pallas_call(
+        functools.partial(backward_kernel, shard_axis),
+        in_specs=[ANYWHERE] * 13 + [VM] * 3 + [VM],
+        out_specs=[VM] * 6,
+        out_shape=[shape((tokens, width), F32)]
+        + [shape(s, F32) for s in slice_shapes]
+        + [shape((8, width), F32)],
+        scratch_shapes=[pltpu.VMEM(m.shape, m.dtype) for m in moved]
+        + [
+            pltpu.VMEM((tokens, width), F32),
+            pltpu.VMEM((tokens, width), F32),
+            pltpu.VMEM((tokens, width), BF16),
+            pltpu.VMEM(hid.shape, BF16),
+            pltpu.VMEM(hid.shape, BF16),
+            pltpu.VMEM((width, tokens), BF16),
+            pltpu.VMEM((tokens, 3 * width), BF16),
+            pltpu.VMEM((width, tokens), BF16),
+            pltpu.SemaphoreType.DMA((13,)),
+        ],
+        compiler_params=pltpu.CompilerParams(vmem_limit_bytes=62 << 20),
+        name="layer_backward",
+    )(*moved, gains, cos_t, sin_t, lse)
+
+
+def gather_kernel(ids_ref, table_any, out_ref, rows_ref, sem):
+    count = table_any.shape[0]
+    tokens = out_ref.shape[0]
+    rows_ref[...] = jnp.zeros_like(rows_ref)
+
+    def fetch(token, row):
+        return pltpu.make_async_copy(
+            table_any.at[pl.ds(row, 1), :], rows_ref.at[pl.ds(token, 1), :], sem
+        )
+
+    @pl.loop(0, tokens)
+    def _(token):
+        row = ids_ref[token]
+
+        @pl.when((row >= 0) & (row < count))
+        def _():
+            fetch(token, row).start()
+
+    @pl.loop(0, tokens)
+    def _(token):
+        row = ids_ref[token]
+
+        @pl.when((row >= 0) & (row < count))
+        def _():
+            fetch(token, row).wait()
+
+    out_ref[...] = rows_ref[...].astype(BF16)
+
+
+def gather_own(ids, table):
+    tokens, width = ids.shape[0], table.shape[1]
+    return pl.pallas_call(
+        gather_kernel,
+        grid_spec=pltpu.PrefetchScalarGridSpec(
+            num_scalar_prefetch=1,
+            grid=(1,),
+            in_specs=[ANYWHERE],
+            out_specs=whole((tokens, width)),
+            scratch_shapes=[pltpu.VMEM((tokens, width), F32), pltpu.SemaphoreType.DMA],
+        ),
+        out_shape=jax.ShapeDtypeStruct((tokens, width), BF16),
+        name="gather_own",
+    )(ids, table)
+
+
+class Spread:
+    def __init__(self, full, axis, shards, sems):
+        self.full, self.axis, self.sems = full, axis, sems
+        self.shard = lax.axis_index(axis)
+        self.core = lax.rem(self.shard, 2)
+        self.chip = self.shard // 2
+        self.partner = self.shard + 1 - 2 * self.core
+        self.chips = shards // 2
+
+    def chip_copy(self, peer_chip, slot, at):
+        return pltpu.make_async_remote_copy(
+            src_ref=self.full.at[slot], dst_ref=self.full.at[slot],
+            send_sem=self.sems.at[0, at], recv_sem=self.sems.at[1, at],
+            device_id={self.axis: peer_chip * 2 + self.core}, device_id_type=MESH_ID,
+        )
+
+    def core_copy(self, slot, at):
+        return pltpu.make_async_remote_copy(
+            src_ref=self.full.at[slot], dst_ref=self.full.at[slot],
+            send_sem=self.sems.at[2, at], recv_sem=self.sems.at[3, at],
+            device_id={self.axis: self.partner}, device_id_type=MESH_ID,
+        )
+
+    def source(self, at):
+        return lax.rem(self.chip - at + self.chips, self.chips)
+
+    def start(self):
+        for at in range(1, self.chips):
+            self.chip_copy(lax.rem(self.chip + at, self.chips), self.shard, at).start()
+        self.core_copy(self.shard, 0).start()
+
+    def relay(self):
+        for at in range(1, self.chips):
+            slot = self.source(at) * 2 + self.core
+            self.chip_copy(self.source(at), slot, at).wait_recv()
+            self.core_copy(slot, at).start()
+
+    def finish(self):
+        for at in range(self.chips):
+            slot = self.source(at) * 2 + 1 - self.core
+            self.core_copy(slot, at).wait_recv()
+        for at in range(1, self.chips):
+            self.chip_copy(lax.rem(self.chip + at, self.chips), self.shard, at).wait_send()
+        for at in range(self.chips):
+            self.core_copy(self.source(at) * 2 + self.core, at).wait_send()
+
+
+def greet_all(axis, count):
+    barrier = pltpu.get_barrier_semaphore()
+    me = lax.axis_index(axis)
+    for step in range(1, count):
+        pl.semaphore_signal(
+            barrier, inc=1, device_id={axis: lax.rem(me + step, count)}, device_id_type=MESH_ID
+        )
+
+
+def open_kernel(
+    shards, axis, own_ref, weight_ref, x0_ref, full_ref,
+    half_in, sums, core_send, core_recv, chip_send, chip_recv, back_send, back_recv, sems,
+):
+    greet_all(axis, shards)
+    shard = lax.axis_index(axis)
+    core = lax.rem(shard, 2)
+    chip = shard // 2
+    partner = shard + 1 - 2 * core
+    chips = shards // 2
+    half = own_ref.shape[0] // 2
+    own_half = pl.ds(pl.multiple_of(core * half, half), half)
+    other_half = pl.ds(pl.multiple_of((1 - core) * half, half), half)
+    spread = Spread(full_ref, axis, shards, sems)
+    full_ref[shard] = weight_ref[...].astype(BF16)
+
+    def chip_copy(peer_chip, slot, at):
+        return pltpu.make_async_remote_copy(
+            src_ref=sums.at[slot], dst_ref=sums.at[slot],
+            send_sem=chip_send.at[at], recv_sem=chip_recv.at[at],
+            device_id={axis: peer_chip * 2 + core}, device_id_type=MESH_ID,
+        )
+
+    def back_copy(rows):
+        return pltpu.make_async_remote_copy(
+            src_ref=x0_ref.at[rows, :], dst_ref=x0_ref.at[rows, :],
+            send_sem=back_send, recv_sem=back_recv,
+            device_id={axis: partner}, device_id_type=MESH_ID,
+        )
+
+    pl.semaphore_wait(pltpu.get_barrier_semaphore(), shards - 1)
+    first = pltpu.make_async_remote_copy(
+        src_ref=own_ref.at[other_half, :], dst_ref=half_in,
+        send_sem=core_send, recv_sem=core_recv,
+        device_id={axis: partner}, device_id_type=MESH_ID,
     )
-
-
-def block_scores(rows_query, key_seq, first_row):
-    row_count = rows_query.shape[0]
-    scores = jnp.einsum(
-        "qhd,khd->hqk", rows_query, key_seq, preferred_element_type=jnp.float32
-    ) * HD ** (-0.5)
-    causal = (first_row + jnp.arange(row_count))[:, None] >= jnp.arange(key_seq.shape[0])[None, :]
-    return jnp.where(causal[None], scores, -1e30)
-
-
-def attend(query_seq, key_seq, value_seq):
-    length = query_seq.shape[0]
-    block_len = min(512, length)
-    mixed_parts, lse_parts = ([], [])
-    for first_row in range(0, length, block_len):
-        scores = block_scores(query_seq[first_row : first_row + block_len], key_seq, first_row)
-        log_total = jax.nn.logsumexp(scores, axis=-1)
-        attn_probs = jnp.exp(scores - log_total[..., None]).astype(jnp.bfloat16)
-        mixed_parts.append(
-            jnp.einsum("hqk,khd->qhd", attn_probs, value_seq, preferred_element_type=jnp.float32)
+    first.start()
+    first.wait_recv()
+    sums[chip] = (own_ref[own_half, :].astype(F32) + half_in[...].astype(F32)).astype(BF16)
+    for at in range(1, chips):
+        chip_copy(lax.rem(chip + at, chips), chip, at).start()
+    spread.start()
+    first.wait_send()
+    total = sums[chip].astype(F32)
+    for at in range(1, chips):
+        source = lax.rem(chip - at + chips, chips)
+        chip_copy(source, source, at).wait_recv()
+        total = total + sums[source].astype(F32)
+    x0_ref[own_half, :] = total.astype(BF16)
+    back_copy(own_half).start()
+    spread.relay()
+    back_copy(other_half).wait_recv()
+    for at in range(1, chips):
+        chip_copy(lax.rem(chip + at, chips), chip, at).wait_send()
+    back_copy(own_half).wait_send()
+    spread.finish()
+
+
+def opening(own, weight, shards, axis):
+    tokens, width = own.shape
+    chips = shards // 2
+    shape = jax.ShapeDtypeStruct
+    return pl.pallas_call(
+        functools.partial(open_kernel, shards, axis),
+        in_specs=[VM] * 2,
+        out_specs=[VM] * 2,
+        out_shape=[shape((tokens, width), BF16), shape((shards, *weight.shape), BF16)],
+        scratch_shapes=[
+            pltpu.VMEM((tokens // 2, width), BF16),
+            pltpu.VMEM((chips, tokens // 2, width), BF16),
+        ]
+        + [pltpu.SemaphoreType.DMA] * 2
+        + [pltpu.SemaphoreType.DMA((max(2, chips),))] * 2
+        + [pltpu.SemaphoreType.DMA] * 2
+        + [pltpu.SemaphoreType.DMA((4, max(2, chips)))],
+        compiler_params=pltpu.CompilerParams(collective_id=4, has_side_effects=True),
+        name="opening",
+    )(own, weight)
+
+
+TOKEN_LANES = 256
+
+
+def vocab_block(rows):
+    best = 16
+    for size in range(16, 1025, 16):
+        if rows % size == 0:
+            best = size
+    return best
+
+
+def head_kernel(
+    shards, axis,
+    n3_ref, target_ref, table_ref,
+    gtable_ref, dn3_any, loss_ref,
+    dn3_ref, back_in, out_sem, kept, n3_t, tops, running, stats, z_ref, half_in, half_out,
+    stat_send, stat_recv, core_send, core_recv, chip_send, chip_recv, back_send, back_recv,
+):
+    phase, step = pl.program_id(0), pl.program_id(1)
+    last = pl.num_programs(1) - 1
+    shard = lax.axis_index(axis)
+    core = lax.rem(shard, 2)
+    chip = shard // 2
+    partner = shard + 1 - 2 * core
+    chips = shards // 2
+    tokens, width = n3_ref.shape
+    block_rows = table_ref.shape[0]
+    half = width // 2
+    own_half = pl.ds(pl.multiple_of(core * half, half), half)
+    other_half = pl.ds(pl.multiple_of((1 - core) * half, half), half)
+
+    def stat_copy(peer, slot, at):
+        return pltpu.make_async_remote_copy(
+            src_ref=stats.at[slot], dst_ref=stats.at[slot],
+            send_sem=stat_send.at[at], recv_sem=stat_recv.at[at],
+            device_id={axis: peer}, device_id_type=MESH_ID,
         )
-        lse_parts.append(log_total)
-    return (jnp.concatenate(mixed_parts, axis=0), jnp.concatenate(lse_parts, axis=1))
-
-
-def attend_back(query_seq, key_seq, value_seq, lse_seq, grad_mixed):
-    length = query_seq.shape[0]
-    block_len = min(512, length)
-    grad_query_parts = []
-    grad_key = jnp.zeros(key_seq.shape, jnp.float32)
-    grad_value = jnp.zeros(value_seq.shape, jnp.float32)
-    for first_row in range(0, length, block_len):
-        rows_query = query_seq[first_row : first_row + block_len]
-        rows_grad = grad_mixed[first_row : first_row + block_len]
-        scores = block_scores(rows_query, key_seq, first_row)
-        attn_probs = jnp.exp(scores - lse_seq[:, first_row : first_row + block_len, None])
-        grad_probs = jnp.einsum(
-            "qhd,khd->hqk", rows_grad, value_seq, preferred_element_type=jnp.float32
+
+    def core_copy():
+        return pltpu.make_async_remote_copy(
+            src_ref=dn3_ref.at[other_half, :], dst_ref=half_in,
+            send_sem=core_send, recv_sem=core_recv,
+            device_id={axis: partner}, device_id_type=MESH_ID,
         )
-        row_delta = jnp.sum(attn_probs * grad_probs, axis=-1, keepdims=True)
-        grad_scores = (attn_probs * (grad_probs - row_delta)).astype(jnp.bfloat16)
-        grad_query_parts.append(
-            jnp.einsum("hqk,khd->qhd", grad_scores, key_seq, preferred_element_type=jnp.float32)
-            * HD ** (-0.5)
+
+    def chip_copy(peer_chip, slot, at):
+        return pltpu.make_async_remote_copy(
+            src_ref=half_out.at[slot], dst_ref=half_out.at[slot],
+            send_sem=chip_send.at[at], recv_sem=chip_recv.at[at],
+            device_id={axis: peer_chip * 2 + core}, device_id_type=MESH_ID,
         )
-        grad_key = grad_key + jnp.einsum(
-            "hqk,qhd->khd", grad_scores, rows_query, preferred_element_type=jnp.float32
-        ) * HD ** (-0.5)
-        grad_value = grad_value + jnp.einsum(
-            "hqk,qhd->khd",
-            attn_probs.astype(jnp.bfloat16),
-            rows_grad,
-            preferred_element_type=jnp.float32,
+
+    def back_copy():
+        return pltpu.make_async_remote_copy(
+            src_ref=dn3_ref.at[own_half, :], dst_ref=back_in,
+            send_sem=back_send, recv_sem=back_recv,
+            device_id={axis: partner}, device_id_type=MESH_ID,
         )
-    return (jnp.concatenate(grad_query_parts, axis=0), grad_key, grad_value)
-
-
-def layer_forward(stream_in, norm_gains, projections, seq_count, length):
-    proj_qkv, proj_out, proj_up, proj_down = projections
-    tok_count = seq_count * length
-    normed_in = rms_norm(stream_in, norm_gains[0]).astype(jnp.bfloat16)
-    packed = jnp.dot(normed_in, proj_qkv, preferred_element_type=jnp.float32).reshape(
-        seq_count, length, 3, HEADS, HD
-    )
-    query_list, key_list, value_list, mixed_list, lse_list = ([], [], [], [], [])
-    query_seq = rotate(packed[0, :, 0], length).astype(jnp.bfloat16)
-    key_seq = rotate(packed[0, :, 1], length).astype(jnp.bfloat16)
-    value_seq = packed[0, :, 2].astype(jnp.bfloat16)
-    mixed_seq, lse_seq = attend(query_seq, key_seq, value_seq)
-    query_list.append(query_seq)
-    key_list.append(key_seq)
-    value_list.append(value_seq)
-    mixed_list.append(mixed_seq)
-    lse_list.append(lse_seq)
-    mixed = jnp.stack(mixed_list).reshape(tok_count, HEADS * HD).astype(jnp.bfloat16)
-    stream_mid = stream_in + jnp.dot(mixed, proj_out, preferred_element_type=jnp.float32)
-    normed_mid = rms_norm(stream_mid, norm_gains[1]).astype(jnp.bfloat16)
-    hidden = jnp.dot(normed_mid, proj_up, preferred_element_type=jnp.float32)
-    active = jax.nn.gelu(hidden, approximate=False).astype(jnp.bfloat16)
-    stream_out = stream_mid + jnp.dot(active, proj_down, preferred_element_type=jnp.float32)
-    kept = (
-        stream_in,
-        stream_mid,
-        normed_in,
-        query_list,
-        key_list,
-        value_list,
-        lse_list,
-        mixed,
-        normed_mid,
-        hidden,
-        active,
-    )
-    return (stream_out, kept)
-
-
-def layer_backward(grad_out, kept, norm_gains, projections, seq_count, length):
-    proj_qkv, proj_out, proj_up, proj_down = projections
-    (
-        stream_in,
-        stream_mid,
-        normed_in,
-        query_list,
-        key_list,
-        value_list,
-        lse_list,
-        mixed,
-        normed_mid,
-        hidden,
-        active,
-    ) = kept
-    tok_count = seq_count * length
-    grad_branch = grad_out.astype(jnp.bfloat16)
-    grad_down = jnp.einsum("tf,td->fd", active, grad_branch, preferred_element_type=jnp.float32)
-    grad_active = jnp.einsum(
-        "td,fd->tf", grad_branch, proj_down, preferred_element_type=jnp.float32
-    )
-    gelu_pull = jax.vjp(lambda pre_act: jax.nn.gelu(pre_act, approximate=False), hidden)[1]
-    grad_hidden = gelu_pull(grad_active)[0].astype(jnp.bfloat16)
-    grad_up = jnp.einsum("td,tf->df", normed_mid, grad_hidden, preferred_element_type=jnp.float32)
-    grad_normed_mid = jnp.einsum(
-        "tf,df->td", grad_hidden, proj_up, preferred_element_type=jnp.float32
-    )
-    grad_mid_part, grad_gain_mid = jax.vjp(rms_norm, stream_mid, norm_gains[1])[1](grad_normed_mid)
-    grad_mid = grad_out + grad_mid_part
-    grad_attn = grad_mid.astype(jnp.bfloat16)
-    grad_outproj = jnp.einsum("tc,td->cd", mixed, grad_attn, preferred_element_type=jnp.float32)
-    grad_mixed = jnp.einsum("td,cd->tc", grad_attn, proj_out, preferred_element_type=jnp.float32)
-    grad_mixed = grad_mixed.astype(jnp.bfloat16).reshape(seq_count, length, HEADS, HD)
-    grad_query, grad_key, grad_value = attend_back(
-        query_list[0], key_list[0], value_list[0], lse_list[0], grad_mixed[0]
-    )
-    unrotate = jax.vjp(lambda heads_in: rotate(heads_in, length), grad_query)[1]
-    packed_grads = [jnp.stack([unrotate(grad_query)[0], unrotate(grad_key)[0], grad_value], axis=1)]
-    grad_packed = jnp.stack(packed_grads).reshape(tok_count, 3 * HEADS * HD).astype(jnp.bfloat16)
-    grad_qkv = jnp.einsum("td,tc->dc", normed_in, grad_packed, preferred_element_type=jnp.float32)
-    grad_normed_in = jnp.einsum(
-        "tc,dc->td", grad_packed, proj_qkv, preferred_element_type=jnp.float32
-    )
-    grad_in_part, grad_gain_in = jax.vjp(rms_norm, stream_in, norm_gains[0])[1](grad_normed_in)
-    return (
-        grad_mid + grad_in_part,
-        (grad_qkv, grad_outproj, grad_up, grad_down),
-        (grad_gain_in, grad_gain_mid),
-    )
+
+    @pl.when((phase == 0) & (step == 0))
+    def _():
+        barrier = pltpu.get_barrier_semaphore()
+        for at in range(1, shards):
+            pl.semaphore_signal(
+                barrier, inc=1,
+                device_id={axis: lax.rem(shard + at, shards)}, device_id_type=MESH_ID,
+            )
+        n3_t[...] = n3_ref[...].T
+        row_at = lax.broadcasted_iota(jnp.int32, running.shape, 0)
+        running[...] = jnp.where(row_at == 0, -1e30, 0.0)
+        dn3_ref[...] = jnp.zeros_like(dn3_ref)
+
+    def hits(lanes):
+        row_at = lax.broadcasted_iota(jnp.int32, (block_rows, TOKEN_LANES), 0)
+        return row_at == target_ref[:, lanes] - step * block_rows
+
+    @pl.when(phase == 0)
+    def _():
+        table = table_ref[...].astype(BF16)
+        for start in range(0, tokens, TOKEN_LANES):
+            lanes = slice(start, start + TOKEN_LANES)
+            logits = nn_dot(table, n3_t[:, lanes])
+            top = jnp.max(logits, axis=0, keepdims=True)
+            weight = jnp.exp(logits - top)
+            kept[step, :, lanes] = weight
+            tops[step, :, lanes] = top
+            total = jnp.sum(weight, axis=0, keepdims=True)
+            picked = jnp.sum(jnp.where(hits(lanes), logits, 0.0), axis=0, keepdims=True)
+            old = running[0:1, lanes]
+            new = jnp.maximum(old, top)
+            running[0:1, lanes] = new
+            running[1:2, lanes] = running[1:2, lanes] * jnp.exp(old - new) + total * jnp.exp(top - new)
+            running[2:3, lanes] += picked
+
+    @pl.when((phase == 1) & (step == 0))
+    def _():
+        stats[shard] = running[...]
+        pl.semaphore_wait(pltpu.get_barrier_semaphore(), shards - 1)
+        sends = [stat_copy(lax.rem(shard + at, shards), shard, at) for at in range(1, shards)]
+        for send in sends:
+            send.start()
+        for at in range(1, shards):
+            source = lax.rem(shard - at + shards, shards)
+            stat_copy(source, source, at).wait_recv()
+        for send in sends:
+            send.wait_send()
+        top = stats[0, 0:1, :]
+        for at in range(1, shards):
+            top = jnp.maximum(top, stats[at, 0:1, :])
+        total, picked = jnp.zeros_like(top), jnp.zeros_like(top)
+        for at in range(shards):
+            total = total + stats[at, 1:2, :] * jnp.exp(stats[at, 0:1, :] - top)
+            picked = picked + stats[at, 2:3, :]
+        z = top + jnp.log(total)
+        z_ref[...] = z
+        terms = (z - picked) + ZLOSS_WEIGHT * (z * z)
+        loss = jnp.sum(terms, axis=1, keepdims=True) * (1.0 / tokens)
+        loss_ref[...] = jnp.broadcast_to(loss, loss_ref.shape)
+
+    def grad_logits(lanes):
+        z = z_ref[:, lanes]
+        factor = jnp.exp(tops[step, :, lanes] - z) * (1.0 + 2.0 * ZLOSS_WEIGHT * z) * (1.0 / tokens)
+        return (kept[step, :, lanes] * factor - jnp.where(hits(lanes), 1.0 / tokens, 0.0)).astype(BF16)
+
+    @pl.when(phase == 1)
+    def _():
+        table_t = table_ref[...].astype(BF16).T
+        for start in range(0, tokens, TOKEN_LANES):
+            lanes = slice(start, start + TOKEN_LANES)
+            dn3_ref[:, lanes] += nn_dot(table_t, grad_logits(lanes))
+
+    @pl.when((phase == 2) & (step == 0))
+    def _():
+        core_copy().start()
+
+    @pl.when((phase == 2) & (step == jnp.minimum(2, last)))
+    def _():
+        core_copy().wait()
+        half_out[chip] = (dn3_ref[own_half, :] + half_in[...]).astype(BF16)
+        for at in range(1, chips):
+            chip_copy(lax.rem(chip + at, chips), chip, at).start()
+
+    @pl.when(phase == 2)
+    def _():
+        total = None
+        for start in range(0, tokens, TOKEN_LANES):
+            lanes = slice(start, start + TOKEN_LANES)
+            part = nn_dot(grad_logits(lanes), n3_ref[lanes, :])
+            total = part if total is None else total + part
+        gtable_ref[...] = total
+
+    @pl.when((phase == 2) & (step == last))
+    def _():
+        for at in range(1, chips):
+            source = lax.rem(chip - at + chips, chips)
+            chip_copy(source, source, at).wait_recv()
+        for at in range(1, chips):
+            chip_copy(lax.rem(chip + at, chips), chip, at).wait_send()
+        whole_sum = half_out[0].astype(F32)
+        for at in range(1, chips):
+            whole_sum = whole_sum + half_out[at].astype(F32)
+        dn3_ref[own_half, :] = whole_sum
+        back_copy().start()
+        puts = [
+            pltpu.make_async_copy(dn3_ref.at[own_half, :], dn3_any.at[own_half, :], out_sem.at[0]),
+            pltpu.make_async_copy(back_in, dn3_any.at[other_half, :], out_sem.at[1]),
+        ]
+        puts[0].start()
+        back_copy().wait()
+        puts[1].start()
+        for put in puts:
+            put.wait()
+
+
+def vocabulary_head(n3, local_targets, table, shards, axis):
+    rows, width = table.shape
+    tokens = n3.shape[0]
+    size = vocab_block(rows)
+    blocks = rows // size
+    shape = jax.ShapeDtypeStruct
+    return pl.pallas_call(
+        functools.partial(head_kernel, shards, axis),
+        grid=(3, blocks),
+        in_specs=[
+            whole((tokens, width)),
+            whole((1, tokens)),
+            pl.BlockSpec((size, width), lambda p, i: (jnp.where(p == 2, blocks - 1, i), 0)),
+        ],
+        out_specs=[
+            pl.BlockSpec((size, width), lambda p, i: (jnp.where(p == 2, i, 0), 0)),
+            pl.BlockSpec(memory_space=pl.ANY),
+            whole((8, 128)),
+        ],
+        out_shape=[shape((rows, width), F32), shape((width, tokens), F32), shape((8, 128), F32)],
+        scratch_shapes=[
+            pltpu.VMEM((width, tokens), F32),
+            pltpu.VMEM((width // 2, tokens), F32),
+            pltpu.SemaphoreType.DMA((2,)),
+            pltpu.VMEM((blocks, size, tokens), F32),
+            pltpu.VMEM((width, tokens), BF16),
+            pltpu.VMEM((blocks, 1, tokens), F32),
+            pltpu.VMEM((8, tokens), F32),
+            pltpu.VMEM((shards, 8, tokens), F32),
+            pltpu.VMEM((1, tokens), F32),
+            pltpu.VMEM((width // 2, tokens), F32),
+            pltpu.VMEM((shards // 2, width // 2, tokens), BF16),
+        ]
+        + [pltpu.SemaphoreType.DMA((shards,))] * 2
+        + [pltpu.SemaphoreType.DMA] * 2
+        + [pltpu.SemaphoreType.DMA((max(2, shards // 2),))] * 2
+        + [pltpu.SemaphoreType.DMA] * 2,
+        compiler_params=pltpu.CompilerParams(
+            collective_id=3, has_side_effects=True, vmem_limit_bytes=62 << 20
+        ),
+        name="vocabulary_head",
+    )(n3, local_targets, table)
 
 
 def body(
@@ -672,59 +1284,36 @@
     vocab_rows = embedding.shape[0]
     shard_pos = lax.axis_index("voc")
     workers = lax.axis_size("rep")
-    vocab_table = embedding.astype(jnp.bfloat16)
     slices = (w_qkv, w_out, w_up, w_down)
-    projections = (
-        lax.all_gather(w_qkv.astype(jnp.bfloat16), "voc", axis=0, tiled=True),
-        lax.all_gather(w_out.astype(jnp.bfloat16), "voc", axis=0, tiled=True),
-        lax.all_gather(w_up.astype(jnp.bfloat16), "voc", axis=0, tiled=True),
-        lax.all_gather(w_down.astype(jnp.bfloat16), "voc", axis=0, tiled=True),
-    )
+    shards = lax.axis_size("voc")
     local_ids = token_ids.reshape(-1) - shard_pos * vocab_rows
     inside = (local_ids >= 0) & (local_ids < vocab_rows)
     safe_ids = jnp.clip(local_ids, 0, vocab_rows - 1)
-    own_rows = jnp.where(inside[:, None], vocab_table[safe_ids].astype(jnp.float32), 0.0)
-    stream_in = lax.psum(own_rows.astype(jnp.bfloat16), "voc").astype(jnp.float32)
-    stream_out, kept = layer_forward(stream_in, norm_gains, projections, seq_count, length)
-    normed_out = rms_norm(stream_out, norm_gains[2]).astype(jnp.bfloat16)
-    logits = jnp.einsum("td,vd->tv", normed_out, vocab_table, preferred_element_type=jnp.float32)
-    local_targets = target_ids.reshape(-1) - shard_pos * vocab_rows
-    target_hit = jnp.arange(vocab_rows)[None, :] == local_targets[:, None]
-    picked_local = jnp.sum(jnp.where(target_hit, logits, 0.0), axis=-1)
-    local_top = jnp.max(logits, axis=-1)
-    top_all = lax.pmax(local_top, "voc")
-    total_all, picked = lax.psum(
-        (jnp.sum(jnp.exp(logits - top_all[:, None]), axis=-1), picked_local), "voc"
+    x0, qkv_all = opening(gather_own(local_ids, embedding), w_qkv, shards, "voc")
+    wqkv = qkv_all.reshape(-1, w_qkv.shape[1])
+    half = HD // 2
+    angles = (10000.0 ** (-jnp.arange(half).astype(F32) / half))[:, None] * jnp.arange(length).astype(F32)[None, :]
+    cos_t, sin_t = jnp.cos(angles), jnp.sin(angles)
+    *kept, n3, wo, wu, wd, hid = layer_forward(
+        x0, norm_gains, cos_t, sin_t, wqkv, slices[1:], shards, "voc"
     )
-    partition = top_all + jnp.log(total_all)
-    loss_value = jnp.mean(partition - picked) + ZLOSS_WEIGHT * jnp.mean(partition * partition)
-    soft_probs = jnp.exp(logits - partition[:, None])
-    grad_logits = (
-        (
-            soft_probs * (1.0 + 2.0 * ZLOSS_WEIGHT * partition)[:, None]
-            - target_hit.astype(jnp.float32)
-        )
-        / tok_count
-    ).astype(jnp.bfloat16)
-    grad_table_head = jnp.einsum(
-        "tv,td->vd", grad_logits, normed_out, preferred_element_type=jnp.float32
+    kept = (*kept, n3, hid)
+    projections = (wqkv, *(w.reshape(-1, w.shape[2]) for w in (wo, wu, wd)))
+    local_targets = target_ids.reshape(1, -1) - shard_pos * vocab_rows
+    grad_table_head, dn3_t, loss_tile = vocabulary_head(
+        n3, local_targets, embedding, lax.axis_size("voc"), "voc"
     )
-    hidden_terms = jnp.dot(grad_logits, vocab_table, preferred_element_type=jnp.float32)
-    grad_normed_out = lax.psum(hidden_terms, "voc")
-    grad_stream, grad_gain_out = jax.vjp(rms_norm, stream_out, norm_gains[2])[1](grad_normed_out)
-    grad_in, grad_mats, gain_pair = layer_backward(
-        grad_stream, kept, norm_gains, projections, seq_count, length
+    loss_value = loss_tile[0, 0]
+    grad_in, *grad_mats, grad_gains = layer_backward(
+        "voc", [w.shape for w in slices], dn3_t, norm_gains, cos_t, sin_t, projections, x0, kept
     )
+    grad_gains = grad_gains[:3]
     lookup_grad = (
         jnp.zeros(embedding.shape, jnp.float32)
         .at[safe_ids]
         .add(jnp.where(inside[:, None], grad_in, 0.0))
     )
-    grad_gains = jnp.stack([gain_pair[0], gain_pair[1], grad_gain_out])
-    own_grads = [grad_table_head + lookup_grad] + [
-        lax.dynamic_slice_in_dim(full_grad, shard_pos * own_slice.shape[0], own_slice.shape[0], 0)
-        for full_grad, own_slice in zip(grad_mats, slices)
-    ]
+    own_grads = [grad_table_head + lookup_grad] + grad_mats
     errors = [e[0] for e in (embed_err, qkv_err, out_err, up_err, down_err)]
     starts_t = [
         f[0].T for f in (embed_factor, qkv_factor, out_factor, up_factor, down_factor)

time: 554 us -> 338 us (0.61); the launches traced: 545 us -> 337 us
  Pallas kernels: 102 us -> 309 us
  matrix products: 200 us -> 0 us
  waiting for transfers between devices: 74.7 us -> 0 us
  other arithmetic: 96.5 us -> 22.8 us
  local copies, waits for them, and re-layouts: 30.7 us -> 5.06 us
  blocking collectives: 22.8 us -> 0 us
  between operations: 17.8 us -> 0.83 us
    pallas_call x0 -> x5, Pallas kernels: none -> 206 us  [the longest x1 58.5 us: vocabulary_head(): pl.pallas_call(functools.partial(head_kernel, shards, axis), grid=(3, blo...]
    dot_general x27 -> x0, matrix products: 200 us -> none  [the longest x2 26.4 us: attend_back(): jnp.einsum('qhd,khd->hqk', rows_grad, value_seq, preferred_element_type=j...]
    psum x2 -> x0, waiting for transfers between devices: 53.8 us -> none  [the longest x1 28.6 us: body(): grad_normed_out = lax.psum(hidden_terms, 'voc')]
    convert_element_type x9 -> x1, other arithmetic: 39.2 us -> 0.01 us  [body(): jnp.arange(length).astype(F32)[None, :]]
    reduce_sum x6 -> x0, other arithmetic: 29 us -> none  [the longest x1 15 us: body(): picked_local = jnp.sum(jnp.where(target_hit, logits, 0.0), axis=-1)]
    all_gather x3 -> x0, waiting for transfers between devices: 20.8 us -> none  [the longest x1 20.7 us: body(): lax.all_gather(w_qkv.astype(jnp.bfloat16), 'voc', axis=0, tiled=True)]
    all_gather x1 -> x0, blocking collectives: 11 us -> none  [body(): lax.all_gather(w_out.astype(jnp.bfloat16), 'voc', axis=0, tiled=True)]
    gather x1 -> x0, local copies, waits for them, and re-layouts: 8.52 us -> none  [body(): vocab_table[safe_ids].astype(jnp.float32)]
  transfers between devices with their start and end apart: 5 -> 0, of which waited for: 3 -> 0; matrix products, arithmetic and copies ran while one was open for 16% -> 0% of each run, Pallas kernels for 0% -> 0%
where the time goes in v2:
time: 338 us; the launch traced here: 337 us
  Pallas kernels  309 us (91%)
  other arithmetic  22.8 us (7%)
  local copies, waits for them, and re-layouts  5.06 us (1%)
    pallas_call x1, Pallas kernels, vocabulary_head(): pl.pallas_call(functools.partial(head_kernel, shards, axis), grid=(3, blo...  58.5 us
    pallas_call x1, Pallas kernels, layer_backward(): pl.pallas_call(functools.partial(backward_kernel, shard_axis), in_specs=[...  48.7 us
    pallas_call x1, Pallas kernels, layer_forward(): pl.pallas_call(functools.partial(forward_kernel, shards, axis), in_specs=...  46.6 us
    pallas_call x1, Pallas kernels, opening(): pl.pallas_call(functools.partial(open_kernel, shards, axis), in_specs=[VM...  30 us
    pallas_call x1, Pallas kernels, basis(): pl.pallas_call(functools.partial(basis_kernel, workers, shards, row_list,...  26 us
    pallas_call x1, Pallas kernels, residual(): pl.pallas_call(functools.partial(residual_kernel, rows, row_list), grid=(...  23.5 us
    pallas_call x1, Pallas kernels, gather_own(): pl.pallas_call(gather_kernel, grid_spec=pltpu.PrefetchScalarGridSpec(num_...  21.9 us
    scatter-add x1, other arithmetic, body(): lookup_grad = jnp.zeros(embedding.shape, jnp.float32).at[safe_ids].add(jn...  19.1 us

profile of v2, /device:TPU:0, one launch (start us, length us, event | category | flops | bytes accessed | tf_op | source)
XLA Modules:
  0.0 337.4 jit_solution(2818262369745362881)
XLA Ops:
  0.7 1.3 compare_select_fusion
  1.9 21.9 %gather_own.1.own_ref = bf16[1024,512]{1,0:T(8,128)(2,1)} custom-call(s32[1024]{0:T(1024)} %bitcast.72, f32[8000,512]{1,0:T(8,128)} %table_ref.1), custom_call_target="tpu_custom_call" | custom-call | tf_op jit(solution)/shard_map/gather_own/pallas_call | solution.py:888
  23.8 30.0 %opening.1 = (bf16[1024,512]{1,0:T(8,128)(2,1)}, bf16[4,128,1536]{2,1,0:T(8,128)(2,1)}) custom-call(bf16[1024,512]{1,0:T(8,128)(2,1)} %gather_own.1.own_ref, f32[128,1536]{1,0:T(8,128)} %refs_5_.1), custom_call_target="tpu_custom_call" | custom-call | tf_op jit(solution)/shard_map/opening/pallas_call | solution.py:1020
  53.8 1.2 multiply_sine_fusion
  55.1 0.0 copy-start.5
  55.1 46.6 %layer_forward.1 = (bf16[1024,512]{1,0:T(8,128)(2,1)}, bf16[3,512,1024]{2,1,0:T(8,128)(2,1)}, f32[8,1,1024]{2,1,0:T(1,128)}, bf16[512,1024]{1,0:T(8,128)(2,1)}, ...) custom-call(bf16[1024,512]{1,0:T(8,128)(2,1)} %get-tuple-element.76., ...), custom_call_target="tpu_custom_call" | custom-call | tf_op jit(solution)/shard_map/layer_forward/pallas_call | solution.py:651
  101.7 0.0 copy-done.5
  101.7 0.6 broadcast_subtract_fusion.target_ref
  102.3 58.5 %vocabulary_head.1 = (f32[8000,512]{1,0:T(8,128)}, f32[512,1024]{1,0:T(8,128)}, f32[8,128]{1,0:T(8,128)}) custom-call(bf16[1024,512]{1,0:T(8,128)(2,1)} %get-tuple-element.78.n3_ref, s32[1,1024]{1,0:T(1,128)} %broadcast_subtract_fusion.target_ref, f32[8000,512]{1,0:T(8,128)} %table_ref.1), custom_call_target="tpu_custom_call" | custom-call | tf_op jit(solution)/shard_map/vocabulary_head/pallas_call | solution.py:1218
  160.8 1.2 slice.27
  162.0 0.0 copy-start.1
  162.0 48.7 %layer_backward.1 = (f32[1024,512]{1,0:T(8,128)}, f32[128,1536]{1,0:T(8,128)}, f32[128,512]{1,0:T(8,128)}, f32[128,2048]{1,0:T(8,128)}, f32[512,512]{1,0:T(8,128)}, /*index=5*/f32[8,512]{1,0:T(8,128)}) custom-call(f32[512,1024]{1,0:T(8,128)} %get-tuple-element.81.refs_0_, f32[1024,512]{1,0:T(8,128)} %get-tuple-element.82.refs_1_, ...), custom_call_target="tpu_custom_call" | custom-call | tf_op jit(solution)/shard_map/layer_backward/pallas_call | solution.py:833
  210.7 0.0 copy-done.1
  210.7 19.1 %scatter_custom_fusion.refs_0_ = f32[8000,512]{1,0:T(8,128)} fusion(f32[8000,512]{1,0:T(8,128)} %get-tuple-element.80, s32[1024]{0:T(1024)S(1)} %bitcast.77, f32[1024,512]{1,0:T(8,128)} %get-tuple-element.93, f32[]{:T(128)} %constant.6.clone.1, pred[1024]{0:T(1024)(128)(4,1)S(1)} %compare_and_fusion), kind=kCustom, calls=%fused_computation.1 | custom fusion | flops 1048576 | bytes 18482688 | tf_op jit(solution)/shard_map/scatter-add | solution.py:1314
  229.8 0.0 copy-start.4
  229.8 16.4 %sketch.1 = (f32[8,8192]{1,0:T(8,128)}, f32[8,8192]{1,0:T(8,128)}, f32[8,896]{1,0:T(8,128)}, f32[8,896]{1,0:T(8,128)}, f32[8,512]{1,0:T(8,128)}) custom-call(f32[8000,512]{1,0:T(8,128)} %scatter_custom_fusion.refs_0_, f32[128,1536]{1,0:T(8,128)} %get-tuple-element.94.refs_1_, f32[128,512]{1,0:T(8,128)} %get-tuple-element.95.refs_2_, ...), custom_call_target="tpu_custom_call" | custom-call | tf_op jit(solution)/shard_map/sketch/pallas_call | solution.py:138
  246.2 0.0 copy-done.4
  246.3 0.1 reshape.117
  246.3 0.6 pad.4.gains_ref
  246.9 26.0 %basis.1 = (f32[8,8192]{1,0:T(8,128)}, f32[8,896]{1,0:T(8,128)}, f32[8,256]{1,0:T(8,128)}, f32[8,128]{1,0:T(8,128)}) custom-call(f32[8,8192]{1,0:T(8,128)} %get-tuple-element.98.gq_ref, f32[8,8192]{1,0:T(8,128)} %get-tuple-element.99.eq_ref, f32[8,896]{1,0:T(8,128)} %get-tuple-element.100.gs_ref, f32[8,896]{1,0:T(8,128)} %get-tuple-element.101.es_ref, ...), custom_call_target="tpu_custom_call" | custom-call | tf_op jit(solution)/shard_map/basis/pallas_call | solution.py:316
  272.9 1.2 slice.29
  274.1 23.5 %residual.1 = (f32[8000,512]{1,0:T(8,128)}, f32[128,1536]{1,0:T(8,128)}, f32[128,512]{1,0:T(8,128)}, f32[128,2048]{1,0:T(8,128)}, f32[512,512]{1,0:T(8,128)}, /*...) custom-call(f32[8000,512]{1,0:T(8,128)} %scatter_custom_fusion.refs_0_, ...), custom_call_target="tpu_custom_call" | custom-call | tf_op jit(solution)/shard_map/residual/pallas_call | solution.py:378
  297.6 18.4 %mean_right.1.refs_11_ = f32[8,5120]{1,0:T(8,128)} custom-call(f32[8,512]{1,0:T(8,128)} %get-tuple-element.107.r0, f32[8,1536]{1,0:T(8,128)} %get-tuple-element.108.r1, f32[8,512]{1,0:T(8,128)} %get-tuple-element.109.r2, f32[8,2048]{1,0:T(8,128)} %get-tuple-element.110.r3, f32[8,512]{1,0:T(8,128)} %get-tuple-element.111.r4), custom_call_target="tpu_custom_call" | custom-call | tf_op jit(solution)/shard_map/mean_right/pallas_call | solution.py:417
  316.1 0.0 copy-start.2
  316.1 0.0 copy-start.3
  316.1 0.0 copy-start
  316.1 18.7 %update.1 = (f32[8000,512]{1,0:T(8,128)}, f32[128,1536]{1,0:T(8,128)}, f32[128,512]{1,0:T(8,128)}, f32[128,2048]{1,0:T(8,128)}, f32[512,512]{1,0:T(8,128)}, /*in...) custom-call(bf16[8000,512]{1,0:T(8,128)(2,1)} %refs_0_.1, ...), custom_call_target="tpu_custom_call" | custom-call | tf_op jit(solution)/shard_map/update/pallas_call | solution.py:459
  334.8 0.0 copy-done.2
  334.8 0.1 div.24
  334.9 0.0 copy-done.3
  334.9 0.6 broadcast_multiply_fusion
  335.5 0.0 copy-done
  335.5 0.6 slice_bitcast_fusion.2
  336.1 0.6 slice_bitcast_fusion.1
  336.7 0.6 slice_bitcast_fusion
  (5 shorter events, 0.0 us)
Async XLA Ops:
  55.1 46.6 %copy-start.5 = (s32[1,1024]{1,0:T(1,128)S(1)}, s32[1,1024]{1,0:T(1,128)}, u32[]{:S(2)}) copy-start(s32[1,1024]{1,0:T(1,128)} %param.25) | copy-start | bytes 12292
  162.0 48.7 %copy-start.1 = (s32[1,1024]{1,0:T(1,128)S(1)}, s32[1,1024]{1,0:T(1,128)}, u32[]{:S(2)}) copy-start(s32[1,1024]{1,0:T(1,128)} %get-tuple-element.131) | copy-start | bytes 12292
  229.8 16.4 %copy-start.4 = (f32[8,512]{1,0:T(8,128)S(1)}, f32[8,512]{1,0:T(8,128)}, u32[]{:S(2)}) copy-start(f32[8,512]{1,0:T(8,128)} %get-tuple-element.102) | copy-start | bytes 49156
  316.1 18.7 %copy-start.2 = (f32[8,256]{1,0:T(8,128)S(1)}, f32[8,256]{1,0:T(8,128)}, u32[]{:S(2)}) copy-start(f32[8,256]{1,0:T(8,128)} %get-tuple-element.117) | copy-start | bytes 24580
  316.1 18.8 %copy-start.3 = (bf16[3,512]{1,0:T(4,128)(2,1)S(1)}, bf16[3,512]{1,0:T(4,128)(2,1)}, u32[]{:S(2)}) copy-start(bf16[3,512]{1,0:T(4,128)(2,1)} %param.37) | copy-start | bytes 9220
  316.1 19.4 %copy-start = (f32[8,5120]{1,0:T(8,128)S(1)}, f32[8,5120]{1,0:T(8,128)}, u32[]{:S(2)}) copy-start(f32[8,5120]{1,0:T(8,128)} %mean_right.1.refs_11_) | copy-start | bytes 491524

commit v3 on v2

--- a/solution.py
+++ b/solution.py
@@ -96,63 +96,8 @@
     return places, at
 
 
-def sketch_kernel(rows, row_list, *refs):
-    grads, errs, starts = refs[0:5], refs[5:10], refs[10:15]
-    gq_ref, eq_ref, gs_ref, es_ref, sq_ref = refs[15:20]
-    step = pl.program_id(0)
-    places, _ = small_places(row_list)
-
-    @pl.when(step == 0)
-    def _():
-        gs_ref[...] = jnp.zeros_like(gs_ref)
-        es_ref[...] = jnp.zeros_like(es_ref)
-        total = jnp.zeros(sq_ref.shape, F32)
-        for k in range(4):
-            grad = grads[k + 1][...]
-            start_t = starts[k + 1][...]
-            at = pl.ds(places[k], row_list[k])
-            gs_ref[:, at] = left_of(grad, start_t)
-            es_ref[:, at] = left_of_bf16(errs[k + 1][...], start_t)
-            total = total + fold_squares(grad)
-        sq_ref[...] = total
-
-    start_t = starts[0][...]
-    grad = keep_rows(grads[0][...], step * TB, rows)
-    err = keep_rows(errs[0][...].astype(F32), step * TB, rows).astype(BF16)
-    gq_ref[...] = left_of(grad, start_t)
-    eq_ref[...] = left_of_bf16(err, start_t)
-    sq_ref[...] += fold_squares(grad)
-
-
 def whole(shape):
     return pl.BlockSpec(shape, lambda *_: (0,) * len(shape))
-
-
-def sketch(grads, errs, starts_t):
-    rows, width = grads[0].shape
-    blocks = pl.cdiv(rows, TB)
-    row_list = [g.shape[0] for g in grads[1:]]
-    _, small = small_places(row_list)
-    block = pl.BlockSpec((TB, width), lambda i: (i, 0))
-    lanes = pl.BlockSpec((RK, TB), lambda i: (0, i))
-    return pl.pallas_call(
-        functools.partial(sketch_kernel, rows, row_list),
-        grid=(blocks,),
-        in_specs=[block]
-        + [whole(g.shape) for g in grads[1:]]
-        + [block]
-        + [whole(e.shape) for e in errs[1:]]
-        + [whole(s.shape) for s in starts_t],
-        out_specs=[lanes, lanes, whole((RK, small)), whole((RK, small)), whole((8, 512))],
-        out_shape=[
-            jax.ShapeDtypeStruct((RK, blocks * TB), F32),
-            jax.ShapeDtypeStruct((RK, blocks * TB), F32),
-            jax.ShapeDtypeStruct((RK, small), F32),
-            jax.ShapeDtypeStruct((RK, small), F32),
-            jax.ShapeDtypeStruct((8, 512), F32),
-        ],
-        name="sketch",
-    )(*grads, *errs, *starts_t)
 
 
 def clip_of(norm_tile):
@@ -176,55 +121,6 @@
     return parts
 
 
-def ring_sum(x, landing, y, send_sem, land_sem, spread_sem, gather_sem, axis, count):
-    me = lax.axis_index(axis)
-    first = []
-    for step in range(1, count):
-        peer = lax.rem(me + step, count)
-        copy = pltpu.make_async_remote_copy(
-            src_ref=x.at[peer],
-            dst_ref=landing.at[step],
-            send_sem=send_sem.at[step],
-            recv_sem=land_sem.at[step],
-            device_id={axis: peer},
-            device_id_type=MESH_ID,
-        )
-        copy.start()
-        first.append(copy)
-    total = x[me]
-    for step in range(1, count):
-        first[step - 1].wait_recv()
-        total = total + landing[step]
-    y[me] = total
-    second = []
-    for step in range(1, count):
-        peer = lax.rem(me + step, count)
-        copy = pltpu.make_async_remote_copy(
-            src_ref=y.at[me],
-            dst_ref=y.at[me],
-            send_sem=spread_sem.at[step],
-            recv_sem=gather_sem.at[step],
-            device_id={axis: peer},
-            device_id_type=MESH_ID,
-        )
-        copy.start()
-        second.append(copy)
-    for copy in first:
-        copy.wait_send()
-    for step in range(1, count):
-        source = lax.rem(me - step + count, count)
-        pltpu.make_async_remote_copy(
-            src_ref=y.at[source],
-            dst_ref=y.at[source],
-            send_sem=spread_sem.at[step],
-            recv_sem=gather_sem.at[step],
-            device_id={axis: source},
-            device_id_type=MESH_ID,
-        ).wait_recv()
-    for copy in second:
-        copy.wait_send()
-
-
 def greet(axes):
     barrier = pltpu.get_barrier_semaphore()
     greeted = 0
@@ -241,234 +137,244 @@
     pl.semaphore_wait(barrier, greeted)
 
 
-def basis_kernel(
-    workers, shards, row_list, gains_at,
-    gq_ref, eq_ref, gs_ref, es_ref, gains_ref, sq_ref,
-    ph_ref, phs_ref, gsum_ref, norm_ref,
-    x, landing, y, small, sq_all, send_sem, land_sem, spread_sem, gather_sem, sq_send, sq_recv,
-):
-    greet((("rep", workers), ("voc", shards)))
-    shard = lax.axis_index("voc")
-    own = jnp.sum(sq_ref[...].reshape(8, 4, 128), axis=1)
-    own = jnp.sum(jnp.sum(own, axis=0, keepdims=True), axis=1, keepdims=True)
-    sq_all[shard] = jnp.broadcast_to(own, (8, 128))
+def ring_copies(axis, count, src, dst, send_sem, recv_sem, place):
+    me = lax.axis_index(axis)
     copies = []
-    for step in range(1, shards):
-        peer = lax.rem(shard + step, shards)
-        copy = pltpu.make_async_remote_copy(
-            src_ref=sq_all.at[shard],
-            dst_ref=sq_all.at[shard],
-            send_sem=sq_send.at[step],
-            recv_sem=sq_recv.at[step],
-            device_id={"voc": peer},
-            device_id_type=MESH_ID,
+    for step in range(1, count):
+        peer = lax.rem(me + step, count)
+        from_at, to_at = place(me, peer, step)
+        copies.append(
+            pltpu.make_async_remote_copy(
+                src_ref=src.at[from_at], dst_ref=dst.at[to_at],
+                send_sem=send_sem.at[step], recv_sem=recv_sem.at[step],
+                device_id={axis: peer}, device_id_type=MESH_ID,
+            )
         )
+    return copies
+
+
+def ring_start(axis, count, x, landing, sems):
+    for copy in ring_copies(axis, count, x, landing, sems[0], sems[1], lambda me, peer, step: (peer, step)):
         copy.start()
-        copies.append(copy)
-    gains = gains_ref[...]
-    total = jnp.sum(jnp.sum(gains * gains, axis=0, keepdims=True), axis=1, keepdims=True)
-    small[...] = jnp.zeros_like(small)
-    for step in range(1, shards):
-        source = lax.rem(shard - step + shards, shards)
+
+
+def ring_middle(axis, count, x, landing, y, sems):
+    me = lax.axis_index(axis)
+    firsts = ring_copies(axis, count, x, landing, sems[0], sems[1], lambda me, peer, step: (peer, step))
+    total = x[me].astype(F32)
+    for step in range(1, count):
+        firsts[step - 1].wait_recv()
+        total = total + landing[step].astype(F32)
+    y[me] = total.astype(y.dtype)
+    for copy in ring_copies(axis, count, y, y, sems[2], sems[3], lambda me, peer, step: (me, me)):
+        copy.start()
+    for copy in firsts:
+        copy.wait_send()
+
+
+def ring_end(axis, count, y, sems):
+    me = lax.axis_index(axis)
+    for step in range(1, count):
+        source = lax.rem(me - step + count, count)
         pltpu.make_async_remote_copy(
-            src_ref=sq_all.at[source],
-            dst_ref=sq_all.at[source],
-            send_sem=sq_send.at[step],
-            recv_sem=sq_recv.at[step],
-            device_id={"voc": source},
-            device_id_type=MESH_ID,
+            src_ref=y.at[source], dst_ref=y.at[source],
+            send_sem=sems[2].at[step], recv_sem=sems[3].at[step],
+            device_id={axis: source}, device_id_type=MESH_ID,
         ).wait_recv()
-    for copy in copies:
+    for copy in ring_copies(axis, count, y, y, sems[2], sems[3], lambda me, peer, step: (me, me)):
         copy.wait_send()
-    for peer in range(shards):
-        total = total + sq_all[peer][0:1, 0:1]
-    norm = jnp.sqrt(total)
-    norm_ref[...] = jnp.broadcast_to(norm, (8, 128))
-    clip = jnp.minimum(1.0, CLIP_NORM / norm)
-
-    chunk = gq_ref.shape[1] // workers
-    part = small.shape[1] // workers
-    span = gs_ref.shape[1]
-    small[:, :span] = clip * gs_ref[...] + es_ref[...]
-    small[:, gains_at : gains_at + gains.shape[1]] = clip * gains
-    for j in range(workers):
-        at = slice(j * chunk, (j + 1) * chunk)
-        x[j, :, :chunk] = clip * gq_ref[:, at] + eq_ref[:, at]
-        x[j, :, chunk:] = small[:, j * part : (j + 1) * part]
-    ring_sum(x, landing, y, send_sem, land_sem, spread_sem, gather_sem, "rep", workers)
-    parts = orthonormal_t([y[j, :, :chunk] for j in range(workers)])
-    for j in range(workers):
-        ph_ref[:, j * chunk : (j + 1) * chunk] = parts[j]
-        small[:, j * part : (j + 1) * part] = y[j, :, chunk:]
-    gsum_ref[...] = small[:, gains_at : gains_at + gains.shape[1]]
+
+
+def settle_kernel(workers, shards, rows, row_list, widths, *refs):
+    gq_ref, eq_ref, gs_ref, es_ref, gains_ref, sq_ref = refs[0:6]
+    grads, errs = refs[6:11], refs[11:16]
+    ph, phs, own_ref, mean_ref, norm_ref, gain_ref = refs[16:22]
+    (
+        x, landing, y, small, sq_all, flat, x16, landing16, y16,
+        sem_a, sem_b, sem_c, sem_d, sem_e, sem_f, sem_g, sem_h, sq_send, sq_recv,
+    ) = refs[22:]
+    first_sems, second_sems = (sem_a, sem_b, sem_c, sem_d), (sem_e, sem_f, sem_g, sem_h)
+    step = pl.program_id(0)
+    last = pl.num_programs(0) - 1
     places, _ = small_places(row_list)
-    for place, rows in zip(places, row_list):
-        lanes = round_up(rows, 128)
-        phs_ref[:, place : place + lanes] = orthonormal_t([small[:, place : place + lanes]])[0]
-
-
-def basis(sketches, gains, row_list, workers, shards):
+    starts = [sum(widths[:k]) for k in range(5)]
+    gains_at = gs_ref.shape[1]
+    at = pl.multiple_of(step * TB, TB)
+
+    @pl.when(step == 0)
+    def _():
+        greet((("rep", workers), ("voc", shards)))
+        shard = lax.axis_index("voc")
+        own = jnp.sum(sq_ref[...].reshape(8, 4, 128), axis=1)
+        own = jnp.sum(jnp.sum(own, axis=0, keepdims=True), axis=1, keepdims=True)
+        sq_all[shard] = jnp.broadcast_to(own, (8, 128))
+        copies = ring_copies("voc", shards, sq_all, sq_all, sq_send, sq_recv, lambda me, peer, step: (me, me))
+        for copy in copies:
+            copy.start()
+        gains = gains_ref[...]
+        total = jnp.sum(jnp.sum(gains * gains, axis=0, keepdims=True), axis=1, keepdims=True)
+        small[...] = jnp.zeros_like(small)
+        for gap in range(1, shards):
+            source = lax.rem(shard - gap + shards, shards)
+            pltpu.make_async_remote_copy(
+                src_ref=sq_all.at[source], dst_ref=sq_all.at[source],
+                send_sem=sq_send.at[gap], recv_sem=sq_recv.at[gap],
+                device_id={"voc": source}, device_id_type=MESH_ID,
+            ).wait_recv()
+        for copy in copies:
+            copy.wait_send()
+        for peer in range(shards):
+            total = total + sq_all[peer][0:1, 0:1]
+        norm = jnp.sqrt(total)
+        norm_ref[...] = jnp.broadcast_to(norm, (8, 128))
+        clip = jnp.minimum(1.0, CLIP_NORM / norm)
+
+        chunk = gq_ref.shape[1] // workers
+        part = small.shape[1] // workers
+        small[:, :gains_at] = clip * gs_ref[...] + es_ref[...]
+        small[:, gains_at : gains_at + gains.shape[1]] = clip * gains
+        for j in range(workers):
+            lanes = slice(j * chunk, (j + 1) * chunk)
+            x[j, :, :chunk] = clip * gq_ref[:, lanes] + eq_ref[:, lanes]
+            x[j, :, chunk:] = small[:, j * part : (j + 1) * part]
+        ring_start("rep", workers, x, landing, first_sems)
+        ring_middle("rep", workers, x, landing, y, first_sems)
+        ring_end("rep", workers, y, first_sems)
+        parts = orthonormal_t([y[j, :, :chunk] for j in range(workers)])
+        for j in range(workers):
+            ph[:, j * chunk : (j + 1) * chunk] = parts[j]
+            small[:, j * part : (j + 1) * part] = y[j, :, chunk:]
+        gain_ref[...] = small[:, gains_at : gains_at + gains.shape[1]] * (1.0 / workers)
+        flat[...] = jnp.zeros_like(flat)
+        for k in range(4):
+            place, size = places[k], row_list[k]
+            basis_t = orthonormal_t([small[:, place : place + round_up(size, 128)]])[0]
+            phs[:, place : place + round_up(size, 128)] = basis_t
+            basis_t = basis_t[:, :size]
+            matrix = clip * grads[k + 1][...] + errs[k + 1][...].astype(F32)
+            right_t = right_of(basis_t, matrix)
+            flat[:, starts[k + 1] : starts[k + 1] + widths[k + 1]] = right_t
+
+    clip = clip_of(norm_ref[...])
+    matrix = clip * grads[0][...] + errs[0][...].astype(F32)
+    matrix = keep_rows(matrix, step * TB, rows)
+    flat[:, : widths[0]] += right_of(ph[:, pl.ds(at, TB)], matrix)
+
+    @pl.when(step == last)
+    def _():
+        half = x16.shape[2]
+        for j in range(workers):
+            low, high = j * 2 * half, (j * 2 + 1) * half
+            pair = jnp.concatenate([flat[:, low : low + half], flat[:, high : high + half]], axis=0)
+            x16[j] = pair.astype(BF16)
+        ring_start("rep", workers, x16, landing16, second_sems)
+        own_ref[...] = flat[...]
+        ring_middle("rep", workers, x16, landing16, y16, second_sems)
+        ring_end("rep", workers, y16, second_sems)
+        for j in range(workers):
+            pair = y16[j].astype(F32) * (1.0 / workers)
+            low, high = j * 2 * half, (j * 2 + 1) * half
+            mean_ref[:, low : low + half] = pair[:8]
+            mean_ref[:, high : high + half] = pair[8:]
+
+
+def finish_kernel(rows, row_list, widths, *refs):
+    grads, errs, moms, weights = refs[0:5], refs[5:10], refs[10:15], refs[15:19]
+    ph_ref, phs_ref, own_ref, mean_ref, norm_ref, gain_ref, gain_mom_ref = refs[19:26]
+    new_errs, new_moms, changed, rights = refs[26:31], refs[31:36], refs[36:41], refs[41:46]
+    gain_change_ref, next_gain_ref = refs[46:48]
+    step = pl.program_id(0)
+    places, _ = small_places(row_list)
+    starts = [sum(widths[:k]) for k in range(5)]
+    clip = clip_of(norm_ref[...])
+
+    def settle_one(k, basis_t):
+        lanes = slice(starts[k], starts[k] + widths[k])
+        matrix = clip * grads[k][...] + errs[k][...].astype(F32)
+        new_errs[k][...] = matrix - product_of(basis_t, own_ref[:, lanes])
+        moved = MOMENTUM * moms[k][...].astype(F32) + product_of(basis_t, mean_ref[:, lanes])
+        new_moms[k][...] = moved
+        change = -LEARN_RATE * moved
+        changed[k][...] = weights[k - 1][...] + change if k else change
+
+    @pl.when(step == 0)
+    def _():
+        moved = MOMENTUM * gain_mom_ref[...].astype(F32) + gain_ref[: gain_mom_ref.shape[0], :]
+        next_gain_ref[...] = moved
+        gain_change_ref[...] = -LEARN_RATE * moved
+        for k in range(5):
+            rights[k][...] = mean_ref[:, starts[k] : starts[k] + widths[k]]
+        for k in range(1, 5):
+            settle_one(k, phs_ref[:, places[k - 1] : places[k - 1] + row_list[k - 1]])
+
+    settle_one(0, ph_ref[...])
+
+
+def held(shape):
+    return pl.BlockSpec(shape, lambda *_: (0,) * len(shape), pipeline_mode=pl.Buffered(1))
+
+
+def settle(sketches, gains, gain_mom, grads, errs, moms, weights, workers, shards):
     gq, eq, gs, es, sq = sketches
-    gains_at = gs.shape[1]
-    small = round_up(gains_at + gains.shape[1], workers * 128)
-    lanes = (gq.shape[1] + small) // workers
-    vmem = pl.BlockSpec(memory_space=pltpu.VMEM)
-    return pl.pallas_call(
-        functools.partial(basis_kernel, workers, shards, row_list, gains_at),
-        in_specs=[vmem] * 6,
-        out_specs=[vmem] * 4,
-        out_shape=[
-            jax.ShapeDtypeStruct(gq.shape, F32),
-            jax.ShapeDtypeStruct(gs.shape, F32),
-            jax.ShapeDtypeStruct(gains.shape, F32),
-            jax.ShapeDtypeStruct((8, 128), F32),
-        ],
-        scratch_shapes=[
-            pltpu.VMEM((workers, RK, lanes), F32),
-            pltpu.VMEM((workers, RK, lanes), F32),
-            pltpu.VMEM((workers, RK, lanes), F32),
-            pltpu.VMEM((RK, small), F32),
-            pltpu.VMEM((shards, 8, 128), F32),
-        ]
-        + [pltpu.SemaphoreType.DMA((workers,))] * 4
-        + [pltpu.SemaphoreType.DMA((shards,))] * 2,
-        compiler_params=pltpu.CompilerParams(collective_id=1, has_side_effects=True),
-        name="basis",
-    )(gq, eq, gs, es, gains, sq)
-
-
-def residual_kernel(rows, row_list, *refs):
-    grads, errs = refs[0:5], refs[5:10]
-    ph_ref, phs_ref, norm_ref = refs[10:13]
-    outs, rights = refs[13:18], refs[18:23]
-    kept = refs[23]
-    phase, step = pl.program_id(0), pl.program_id(1)
-    places, _ = small_places(row_list)
-    clip = clip_of(norm_ref[...])
-    at = pl.multiple_of(step * TB, TB)
-
-    @pl.when((phase == 0) & (step == 0))
-    def _():
-        rights[0][...] = jnp.zeros_like(rights[0])
-        for k in range(4):
-            matrix = clip * grads[k + 1][...] + errs[k + 1][...].astype(F32)
-            basis_t = phs_ref[:, places[k] : places[k] + row_list[k]]
-            right_t = right_of(basis_t, matrix)
-            rights[k + 1][...] = right_t
-            outs[k + 1][...] = matrix - product_of(basis_t, right_t)
-
-    @pl.when(phase == 0)
-    def _():
-        matrix = clip * grads[0][...] + errs[0][...].astype(F32)
-        matrix = keep_rows(matrix, step * TB, rows)
-        kept[pl.ds(at, TB), :] = matrix
-        rights[0][...] += right_of(ph_ref[:, pl.ds(at, TB)], matrix)
-
-    @pl.when(phase == 1)
-    def _():
-        outs[0][...] = kept[pl.ds(at, TB), :] - product_of(ph_ref[:, pl.ds(at, TB)], rights[0][...])
-
-
-def residual(grads, errs, ph, phs, norm):
     rows, width = grads[0].shape
     blocks = pl.cdiv(rows, TB)
     row_list = [g.shape[0] for g in grads[1:]]
-    block_in = pl.BlockSpec((TB, width), lambda p, i: (jnp.where(p == 0, i, blocks - 1), 0))
-    block_out = pl.BlockSpec((TB, width), lambda p, i: (jnp.where(p == 0, 0, i), 0))
+    widths = [g.shape[1] for g in grads]
+    small = round_up(gs.shape[1] + gains.shape[1], workers * 128)
+    lanes = (gq.shape[1] + small) // workers
+    right_lanes = round_up(sum(widths), workers * 256)
+    half = right_lanes // workers // 2
+    shape = jax.ShapeDtypeStruct
+    block = pl.BlockSpec((TB, width), lambda i: (i, 0))
+    small_specs = [held(g.shape) for g in grads[1:]]
+    made = [
+        shape((RK, blocks * TB), F32),
+        shape(gs.shape, F32),
+        shape((RK, right_lanes), F32),
+        shape((RK, right_lanes), F32),
+        shape((8, 128), F32),
+        shape(gains.shape, F32),
+    ]
+    operands = (gq, eq, gs, es, gains, sq)
+    sums = pl.pallas_call(
+        functools.partial(settle_kernel, workers, shards, rows, row_list, widths),
+        grid=(blocks,),
+        in_specs=[held(o.shape) for o in operands] + ([block] + small_specs) * 2,
+        out_specs=[held(m.shape) for m in made],
+        out_shape=made,
+        scratch_shapes=[pltpu.VMEM((workers, RK, lanes), F32)] * 3
+        + [
+            pltpu.VMEM((RK, small), F32),
+            pltpu.VMEM((shards, 8, 128), F32),
+            pltpu.VMEM((RK, right_lanes), F32),
+        ]
+        + [pltpu.VMEM((workers, 16, half), BF16)] * 3
+        + [pltpu.SemaphoreType.DMA((workers,))] * 8
+        + [pltpu.SemaphoreType.DMA((shards,))] * 2,
+        compiler_params=pltpu.CompilerParams(
+            collective_id=1, has_side_effects=True, vmem_limit_bytes=60 << 20
+        ),
+        name="settle_sums",
+    )(*operands, *grads, *errs)
+    ph, phs, own, mean, norm, gain = sums
     out = pl.pallas_call(
-        functools.partial(residual_kernel, rows, row_list),
-        grid=(2, blocks),
-        in_specs=[block_in]
-        + [whole(g.shape) for g in grads[1:]]
-        + [block_in]
-        + [whole(e.shape) for e in errs[1:]]
-        + [whole(ph.shape), whole(phs.shape), whole(norm.shape)],
-        out_specs=[block_out]
-        + [whole(g.shape) for g in grads[1:]]
-        + [whole((RK, g.shape[1])) for g in grads],
-        out_shape=[jax.ShapeDtypeStruct(g.shape, F32) for g in grads]
-        + [jax.ShapeDtypeStruct((RK, g.shape[1]), F32) for g in grads],
-        scratch_shapes=[pltpu.VMEM((blocks * TB, width), F32)],
+        functools.partial(finish_kernel, rows, row_list, widths),
+        grid=(blocks,),
+        in_specs=([block] + small_specs) * 3
+        + small_specs
+        + [pl.BlockSpec((RK, TB), lambda i: (0, i))]
+        + [held(m.shape) for m in made[1:]]
+        + [held(gain_mom.shape)],
+        out_specs=([block] + small_specs) * 3
+        + [held((RK, w)) for w in widths]
+        + [held(gain_mom.shape)] * 2,
+        out_shape=[shape(g.shape, F32) for g in grads] * 3
+        + [shape((RK, w), F32) for w in widths]
+        + [shape(gain_mom.shape, F32)] * 2,
         compiler_params=pltpu.CompilerParams(vmem_limit_bytes=60 << 20),
-        name="residual",
-    )(*grads, *errs, ph, phs, norm)
-    return out[:5], out[5:]
-
-
-def mean_right_kernel(workers, r0, r1, r2, r3, r4, out_ref, flat, x, landing, y, s1, s2, s3, s4):
-    greet((("rep", workers),))
-    part = x.shape[2]
-    flat[...] = jnp.zeros_like(flat)
-    at = 0
-    for ref in (r0, r1, r2, r3, r4):
-        flat[:, at : at + ref.shape[1]] = ref[...]
-        at += ref.shape[1]
-    for j in range(workers):
-        x[j] = flat[:, j * part : (j + 1) * part]
-    ring_sum(x, landing, y, s1, s2, s3, s4, "rep", workers)
-    for j in range(workers):
-        out_ref[:, j * part : (j + 1) * part] = y[j] * (1.0 / workers)
-
-
-def mean_right(rights, workers):
-    lanes = round_up(sum(r.shape[1] for r in rights), workers * 128)
-    vmem = pl.BlockSpec(memory_space=pltpu.VMEM)
-    part = (workers, RK, lanes // workers)
-    return pl.pallas_call(
-        functools.partial(mean_right_kernel, workers),
-        in_specs=[vmem] * 5,
-        out_specs=vmem,
-        out_shape=jax.ShapeDtypeStruct((RK, lanes), F32),
-        scratch_shapes=[pltpu.VMEM((RK, lanes), F32)]
-        + [pltpu.VMEM(part, F32)] * 3
-        + [pltpu.SemaphoreType.DMA((workers,))] * 4,
-        compiler_params=pltpu.CompilerParams(collective_id=2, has_side_effects=True),
-        name="mean_right",
-    )(*rights)
-
-
-def update_kernel(row_list, widths, *refs):
-    moms, weights = refs[0:5], refs[5:9]
-    ph_ref, phs_ref, right_ref = refs[9:12]
-    out_moms, outs = refs[12:17], refs[17:22]
-    places, _ = small_places(row_list)
-
-    @pl.when(pl.program_id(0) == 0)
-    def _():
-        at = widths[0]
-        for k in range(4):
-            basis_t = phs_ref[:, places[k] : places[k] + row_list[k]]
-            mean = product_of(basis_t, right_ref[:, at : at + widths[k + 1]])
-            at += widths[k + 1]
-            moved = MOMENTUM * moms[k + 1][...].astype(F32) + mean
-            out_moms[k + 1][...] = moved
-            outs[k + 1][...] = weights[k][...] + -LEARN_RATE * moved
-
-    mean = product_of(ph_ref[...], right_ref[:, : widths[0]])
-    moved = MOMENTUM * moms[0][...].astype(F32) + mean
-    out_moms[0][...] = moved
-    outs[0][...] = -LEARN_RATE * moved
-
-
-def update(moms, weights, ph, phs, right):
-    rows, width = moms[0].shape
-    blocks = pl.cdiv(rows, TB)
-    row_list = [m.shape[0] for m in moms[1:]]
-    widths = [m.shape[1] for m in moms]
-    block = pl.BlockSpec((TB, width), lambda i: (i, 0))
-    out = pl.pallas_call(
-        functools.partial(update_kernel, row_list, widths),
-        grid=(blocks,),
-        in_specs=[block]
-        + [whole(m.shape) for m in moms[1:]]
-        + [whole(w.shape) for w in weights]
-        + [pl.BlockSpec((RK, TB), lambda i: (0, i)), whole(phs.shape), whole(right.shape)],
-        out_specs=([block] + [whole(m.shape) for m in moms[1:]]) * 2,
-        out_shape=[jax.ShapeDtypeStruct(m.shape, F32) for m in moms] * 2,
-        compiler_params=pltpu.CompilerParams(vmem_limit_bytes=60 << 20),
-        name="update",
-    )(*moms, *weights, ph, phs, right)
-    return out[:5], out[5:]
+        name="settle_finish",
+    )(*grads, *errs, *moms, *weights, ph, phs, own, mean, norm, gain, gain_mom)
+    return out[0:5], out[5:10], out[10:15], out[15:20], norm, out[20], out[21]
 
 
 EPS = 1e-06
@@ -526,13 +432,13 @@
     tokens, width = x0_ref.shape
     half = HD // 2
     row_blocks = tokens // QB
-    greet_all(axis, shards)
+    greet_all(shards)
     shard = lax.axis_index(axis)
     spreads = []
     for own, full, sems in ((wo_own, wo_all, wo_sems), (wu_own, wu_all, wu_sems), (wd_own, wd_all, wd_sems)):
         full[shard] = own[...].astype(BF16)
-        spreads.append(Spread(full, axis, shards, sems))
-    pl.semaphore_wait(pltpu.get_barrier_semaphore(), shards - 1)
+        spreads.append(Spread(full, shards, sems))
+    await_all(shards)
     for spread in spreads:
         spread.start()
 
@@ -584,11 +490,16 @@
         lse_ref[head] = jnp.concatenate(lse_parts, axis=1)
 
     heads = width // HD
-    pl.loop(0, heads // 2)(attend)
+    pl.loop(0, heads // 4)(attend)
     spreads[1].relay()
-    pl.loop(heads // 2, heads)(attend)
+    spreads[0].relay_across()
+    pl.loop(heads // 4, heads // 2)(attend)
+    spreads[2].relay()
+    pl.loop(heads // 2, 3 * heads // 4)(attend)
+    spreads[1].relay_across()
+    pl.loop(3 * heads // 4, heads)(attend)
     spreads[0].finish()
-    spreads[2].relay()
+
     @pl.loop(0, row_blocks)
     def _(block):
         rows = pl.ds(pl.multiple_of(block * QB, QB), QB)
@@ -598,6 +509,7 @@
         x2_ref[rows, :] = stream
         n2_ref[rows, :] = scaled_rms(stream, gains_ref[1:2, :]).astype(BF16)
 
+    spreads[2].relay_across()
     spreads[1].finish()
     spreads[2].finish()
     chunk = hid_ref.shape[2]
@@ -647,7 +559,7 @@
     hidden = slices[1].shape[1]
     shape = jax.ShapeDtypeStruct
     chunk = min(512, hidden)
-    sems = pltpu.SemaphoreType.DMA((4, max(2, shards // 2)))
+    sems = pltpu.SemaphoreType.DMA((8, max(2, shards // 2)))
     return pl.pallas_call(
         functools.partial(forward_kernel, shards, axis),
         in_specs=[VM] * 8,
@@ -854,112 +766,227 @@
     )(*moved, gains, cos_t, sin_t, lse)
 
 
-def gather_kernel(ids_ref, table_any, out_ref, rows_ref, sem):
-    count = table_any.shape[0]
-    tokens = out_ref.shape[0]
-    rows_ref[...] = jnp.zeros_like(rows_ref)
-
-    def fetch(token, row):
-        return pltpu.make_async_copy(
-            table_any.at[pl.ds(row, 1), :], rows_ref.at[pl.ds(token, 1), :], sem
-        )
-
-    @pl.loop(0, tokens)
-    def _(token):
-        row = ids_ref[token]
-
-        @pl.when((row >= 0) & (row < count))
+def scatter_sketch_kernel(axis, rows, row_list, ids_ref, *refs):
+    table_any, dx0_ref = refs[0:2]
+    grads, errs, starts = (None, *refs[2:6]), refs[6:11], refs[11:16]
+    full_any, gq_ref, eq_ref, gs_ref, es_ref, sq_ref = refs[16:22]
+    whole_ref, load_sem, store_sem = refs[22:25]
+    phase, step = pl.program_id(0), pl.program_id(1)
+    steps = pl.num_programs(1)
+    places, _ = small_places(row_list)
+    size = rows - (pl.cdiv(rows, TB) - 1) * TB
+
+    def tile_copy(at, count, inward):
+        tile = pl.ds(pl.multiple_of(at * TB, TB), count)
+        if inward:
+            return pltpu.make_async_copy(table_any.at[tile, :], whole_ref.at[tile, :], load_sem.at[at])
+        return pltpu.make_async_copy(whole_ref.at[tile, :], full_any.at[tile, :], store_sem.at[at])
+
+    blocks = pl.cdiv(rows, TB)
+    sizes = [TB] * (blocks - 1) + [size]
+
+    @pl.when((phase == 0) & (step == 0))
+    def _():
+        for at in range(blocks):
+            tile_copy(at, sizes[at], True).start()
+        gs_ref[...] = jnp.zeros_like(gs_ref)
+        es_ref[...] = jnp.zeros_like(es_ref)
+        total = jnp.zeros(sq_ref.shape, F32)
+        for k in range(4):
+            grad = grads[k + 1][...]
+            start_t = starts[k + 1][...]
+            at = pl.ds(places[k], row_list[k])
+            gs_ref[:, at] = left_of(grad, start_t)
+            es_ref[:, at] = left_of_bf16(errs[k + 1][...], start_t)
+            total = total + fold_squares(grad)
+        sq_ref[...] = total
+
+    @pl.when(phase == 0)
+    def _():
+        err = keep_rows(errs[0][...].astype(F32), step * TB, rows).astype(BF16)
+        eq_ref[...] = left_of_bf16(err, starts[0][...])
+
+    @pl.when((phase == 1) & (step == 0))
+    def _():
+        for at in range(blocks):
+            tile_copy(at, sizes[at], True).wait()
+        first = lax.axis_index(axis) * rows if axis else 0
+        if blocks * TB > rows:
+            whole_ref[pl.ds(rows, blocks * TB - rows), :] = jnp.zeros((blocks * TB - rows, whole_ref.shape[1]), F32)
+        spare = blocks * TB
+
+        @pl.loop(0, dx0_ref.shape[0] // 8)
+        def _(group):
+            base = pl.multiple_of(group * 8, 8)
+            for side in range(8):
+                row = ids_ref[base + side] - first
+                row = jnp.where((row >= 0) & (row < rows), row, spare)
+                whole_ref[pl.ds(row, 1), :] += dx0_ref[pl.ds(base + side, 1), :]
+
+    tile = pl.ds(pl.multiple_of(step * TB, TB), TB)
+
+    @pl.when(phase == 1)
+    def _():
+        grad = whole_ref[tile, :]
+        gq_ref[...] = left_of(grad, starts[0][...])
+        sq_ref[...] += fold_squares(grad)
+
+    for at in range(blocks):
+
+        @pl.when((phase == 1) & (step == at))
         def _():
-            fetch(token, row).start()
-
-    @pl.loop(0, tokens)
-    def _(token):
-        row = ids_ref[token]
-
-        @pl.when((row >= 0) & (row < count))
-        def _():
-            fetch(token, row).wait()
-
-    out_ref[...] = rows_ref[...].astype(BF16)
-
-
-def gather_own(ids, table):
-    tokens, width = ids.shape[0], table.shape[1]
-    return pl.pallas_call(
-        gather_kernel,
+            tile_copy(at, sizes[at], False).start()
+
+    @pl.when((phase == 1) & (step == steps - 1))
+    def _():
+        for at in range(blocks):
+            tile_copy(at, sizes[at], False).wait()
+
+
+def scatter_sketch(token_ids, table_grad, dx0, grads, errs, starts_t, axis):
+    rows, width = table_grad.shape
+    blocks = pl.cdiv(rows, TB)
+    row_list = [g.shape[0] for g in grads]
+    _, small = small_places(row_list)
+
+    def whole_at(shape):
+        return pl.BlockSpec(shape, lambda *_: (0,) * len(shape), pipeline_mode=pl.Buffered(1))
+
+    def at_phase(wanted, size, place):
+        def index(p, i, ids):
+            return place(jnp.where(p == wanted, i, jnp.where(p < wanted, 0, blocks - 1)))
+
+        return pl.BlockSpec(size, index)
+
+    shape = jax.ShapeDtypeStruct
+    full, *sketches = pl.pallas_call(
+        functools.partial(scatter_sketch_kernel, axis, rows, row_list),
         grid_spec=pltpu.PrefetchScalarGridSpec(
             num_scalar_prefetch=1,
-            grid=(1,),
-            in_specs=[ANYWHERE],
-            out_specs=whole((tokens, width)),
-            scratch_shapes=[pltpu.VMEM((tokens, width), F32), pltpu.SemaphoreType.DMA],
+            grid=(2, blocks),
+            in_specs=[ANYWHERE, whole_at(dx0.shape)]
+            + [whole_at(g.shape) for g in grads]
+            + [at_phase(0, (TB, width), lambda i: (i, 0))]
+            + [whole_at(e.shape) for e in errs[1:]]
+            + [whole_at(s.shape) for s in starts_t],
+            out_specs=[
+                ANYWHERE,
+                at_phase(1, (RK, TB), lambda i: (0, i)),
+                at_phase(0, (RK, TB), lambda i: (0, i)),
+            ]
+            + [whole_at((RK, small)), whole_at((RK, small)), whole_at((8, 512))],
+            scratch_shapes=[
+                pltpu.VMEM((blocks * TB + 8, width), F32),
+                pltpu.SemaphoreType.DMA((blocks,)),
+                pltpu.SemaphoreType.DMA((blocks,)),
+            ],
         ),
-        out_shape=jax.ShapeDtypeStruct((tokens, width), BF16),
-        name="gather_own",
-    )(ids, table)
+        out_shape=[
+            shape((rows, width), F32),
+            shape((RK, blocks * TB), F32),
+            shape((RK, blocks * TB), F32),
+            shape((RK, small), F32),
+            shape((RK, small), F32),
+            shape((8, 512), F32),
+        ],
+        compiler_params=pltpu.CompilerParams(vmem_limit_bytes=60 << 20),
+        name="scatter_sketch",
+    )(token_ids.reshape(-1), table_grad, dx0, *grads, *errs, *starts_t)
+    return full, sketches
 
 
 class Spread:
-    def __init__(self, full, axis, shards, sems):
-        self.full, self.axis, self.sems = full, axis, sems
-        self.shard = lax.axis_index(axis)
+    def __init__(self, full, shards, sems):
+        self.full, self.sems = full, sems
+        self.shard, self.worker = lax.axis_index("voc"), lax.axis_index("rep")
         self.core = lax.rem(self.shard, 2)
         self.chip = self.shard // 2
-        self.partner = self.shard + 1 - 2 * self.core
         self.chips = shards // 2
-
-    def chip_copy(self, peer_chip, slot, at):
+        self.side = lax.rem(self.worker, 2)
+        self.rows = full.shape[1] // 2
+
+    def region(self, slot, side):
+        return self.full.at[slot, pl.ds(pl.multiple_of(side * self.rows, self.rows), self.rows), :]
+
+    def copy(self, ref, at, pair, peer):
         return pltpu.make_async_remote_copy(
-            src_ref=self.full.at[slot], dst_ref=self.full.at[slot],
-            send_sem=self.sems.at[0, at], recv_sem=self.sems.at[1, at],
-            device_id={self.axis: peer_chip * 2 + self.core}, device_id_type=MESH_ID,
-        )
-
-    def core_copy(self, slot, at):
-        return pltpu.make_async_remote_copy(
-            src_ref=self.full.at[slot], dst_ref=self.full.at[slot],
-            send_sem=self.sems.at[2, at], recv_sem=self.sems.at[3, at],
-            device_id={self.axis: self.partner}, device_id_type=MESH_ID,
+            src_ref=ref, dst_ref=ref, send_sem=self.sems.at[2 * pair, at], recv_sem=self.sems.at[2 * pair + 1, at],
+            device_id=peer, device_id_type=MESH_ID,
         )
 
     def source(self, at):
         return lax.rem(self.chip - at + self.chips, self.chips)
 
+    def own_to_chip(self, at):
+        peer = lax.rem(self.chip + at, self.chips) * 2 + self.core
+        return self.copy(self.region(self.shard, self.side), at, 0, {"voc": peer})
+
+    def from_chip(self, at):
+        slot = self.source(at) * 2 + self.core
+        return self.copy(self.region(slot, self.side), at, 0, {"voc": slot})
+
+    def across(self, at, side):
+        slot = self.source(at) * 2 + self.core
+        return self.copy(self.region(slot, side), at, 1, {"rep": self.worker + 1 - 2 * self.side})
+
+    def to_core(self, at, side, pair, core):
+        slot = self.source(at) * 2 + core
+        return self.copy(self.region(slot, side), at, pair, {"voc": self.shard + 1 - 2 * self.core})
+
+    def own_to_core(self, slot):
+        return self.copy(self.full.at[slot], 0, 2, {"voc": self.shard + 1 - 2 * self.core})
+
     def start(self):
         for at in range(1, self.chips):
-            self.chip_copy(lax.rem(self.chip + at, self.chips), self.shard, at).start()
-        self.core_copy(self.shard, 0).start()
+            self.own_to_chip(at).start()
+        self.own_to_core(self.shard).start()
 
     def relay(self):
         for at in range(1, self.chips):
-            slot = self.source(at) * 2 + self.core
-            self.chip_copy(self.source(at), slot, at).wait_recv()
-            self.core_copy(slot, at).start()
+            self.from_chip(at).wait_recv()
+            self.across(at, self.side).start()
+            self.to_core(at, self.side, 2, self.core).start()
+
+    def relay_across(self):
+        for at in range(1, self.chips):
+            self.across(at, 1 - self.side).wait_recv()
+            self.to_core(at, 1 - self.side, 3, self.core).start()
 
     def finish(self):
-        for at in range(self.chips):
-            slot = self.source(at) * 2 + 1 - self.core
-            self.core_copy(slot, at).wait_recv()
+        self.own_to_core(self.shard + 1 - 2 * self.core).wait_recv()
         for at in range(1, self.chips):
-            self.chip_copy(lax.rem(self.chip + at, self.chips), self.shard, at).wait_send()
-        for at in range(self.chips):
-            self.core_copy(self.source(at) * 2 + self.core, at).wait_send()
-
-
-def greet_all(axis, count):
+            self.to_core(at, self.side, 2, 1 - self.core).wait_recv()
+            self.to_core(at, 1 - self.side, 3, 1 - self.core).wait_recv()
+        self.own_to_core(self.shard).wait_send()
+        for at in range(1, self.chips):
+            self.own_to_chip(at).wait_send()
+            self.across(at, self.side).wait_send()
+            self.to_core(at, self.side, 2, self.core).wait_send()
+            self.to_core(at, 1 - self.side, 3, self.core).wait_send()
+
+
+def greet_all(shards):
     barrier = pltpu.get_barrier_semaphore()
-    me = lax.axis_index(axis)
-    for step in range(1, count):
+    me = lax.axis_index("voc")
+    for step in range(1, shards):
         pl.semaphore_signal(
-            barrier, inc=1, device_id={axis: lax.rem(me + step, count)}, device_id_type=MESH_ID
+            barrier, inc=1, device_id={"voc": lax.rem(me + step, shards)}, device_id_type=MESH_ID
         )
+    worker = lax.axis_index("rep")
+    pl.semaphore_signal(
+        barrier, inc=1, device_id={"rep": worker + 1 - 2 * lax.rem(worker, 2)}, device_id_type=MESH_ID
+    )
+
+
+def await_all(shards):
+    pl.semaphore_wait(pltpu.get_barrier_semaphore(), shards)
 
 
 def open_kernel(
     shards, axis, own_ref, weight_ref, x0_ref, full_ref,
     half_in, sums, core_send, core_recv, chip_send, chip_recv, back_send, back_recv, sems,
 ):
-    greet_all(axis, shards)
+    greet_all(shards)
     shard = lax.axis_index(axis)
     core = lax.rem(shard, 2)
     chip = shard // 2
@@ -968,7 +995,7 @@
     half = own_ref.shape[0] // 2
     own_half = pl.ds(pl.multiple_of(core * half, half), half)
     other_half = pl.ds(pl.multiple_of((1 - core) * half, half), half)
-    spread = Spread(full_ref, axis, shards, sems)
+    spread = Spread(full_ref, shards, sems)
     full_ref[shard] = weight_ref[...].astype(BF16)
 
     def chip_copy(peer_chip, slot, at):
@@ -985,7 +1012,8 @@
             device_id={axis: partner}, device_id_type=MESH_ID,
         )
 
-    pl.semaphore_wait(pltpu.get_barrier_semaphore(), shards - 1)
+    await_all(shards)
+    spread.start()
     first = pltpu.make_async_remote_copy(
         src_ref=own_ref.at[other_half, :], dst_ref=half_in,
         send_sem=core_send, recv_sem=core_recv,
@@ -996,8 +1024,8 @@
     sums[chip] = (own_ref[own_half, :].astype(F32) + half_in[...].astype(F32)).astype(BF16)
     for at in range(1, chips):
         chip_copy(lax.rem(chip + at, chips), chip, at).start()
-    spread.start()
     first.wait_send()
+    spread.relay()
     total = sums[chip].astype(F32)
     for at in range(1, chips):
         source = lax.rem(chip - at + chips, chips)
@@ -1005,7 +1033,7 @@
         total = total + sums[source].astype(F32)
     x0_ref[own_half, :] = total.astype(BF16)
     back_copy(own_half).start()
-    spread.relay()
+    spread.relay_across()
     back_copy(other_half).wait_recv()
     for at in range(1, chips):
         chip_copy(lax.rem(chip + at, chips), chip, at).wait_send()
@@ -1029,7 +1057,7 @@
         + [pltpu.SemaphoreType.DMA] * 2
         + [pltpu.SemaphoreType.DMA((max(2, chips),))] * 2
         + [pltpu.SemaphoreType.DMA] * 2
-        + [pltpu.SemaphoreType.DMA((4, max(2, chips)))],
+        + [pltpu.SemaphoreType.DMA((8, max(2, chips)))],
         compiler_params=pltpu.CompilerParams(collective_id=4, has_side_effects=True),
         name="opening",
     )(own, weight)
@@ -1288,8 +1316,9 @@
     shards = lax.axis_size("voc")
     local_ids = token_ids.reshape(-1) - shard_pos * vocab_rows
     inside = (local_ids >= 0) & (local_ids < vocab_rows)
-    safe_ids = jnp.clip(local_ids, 0, vocab_rows - 1)
-    x0, qkv_all = opening(gather_own(local_ids, embedding), w_qkv, shards, "voc")
+    rows = embedding.at[jnp.clip(local_ids, 0, vocab_rows - 1)].get(mode="promise_in_bounds")
+    own_rows = jnp.where(inside[:, None], rows, 0.0).astype(BF16)
+    x0, qkv_all = opening(own_rows, w_qkv, shards, "voc")
     wqkv = qkv_all.reshape(-1, w_qkv.shape[1])
     half = HD // 2
     angles = (10000.0 ** (-jnp.arange(half).astype(F32) / half))[:, None] * jnp.arange(length).astype(F32)[None, :]
@@ -1307,47 +1336,33 @@
     grad_in, *grad_mats, grad_gains = layer_backward(
         "voc", [w.shape for w in slices], dn3_t, norm_gains, cos_t, sin_t, projections, x0, kept
     )
-    grad_gains = grad_gains[:3]
-    lookup_grad = (
-        jnp.zeros(embedding.shape, jnp.float32)
-        .at[safe_ids]
-        .add(jnp.where(inside[:, None], grad_in, 0.0))
-    )
-    own_grads = [grad_table_head + lookup_grad] + grad_mats
     errors = [e[0] for e in (embed_err, qkv_err, out_err, up_err, down_err)]
     starts_t = [
         f[0].T for f in (embed_factor, qkv_factor, out_factor, up_factor, down_factor)
     ]
-    row_list = [g.shape[0] for g in own_grads[1:]]
-    gains_flat = jnp.pad(grad_gains.reshape(RK, -1), ((0, 0), (0, 64)))
-    sketches = sketch(own_grads, errors, starts_t)
-    ph, phs, gain_sum, norm = basis(sketches, gains_flat, row_list, workers, lax.axis_size("voc"))
-    new_errors, rights = residual(own_grads, errors, ph, phs, norm)
-    right_mean = mean_right(rights, workers)
-    new_moments, changed = update(
+    full_grad, sketches = scatter_sketch(
+        token_ids, grad_table_head, grad_in, grad_mats, errors, starts_t, "voc"
+    )
+    new_errors, new_moments, changed, rights, norm, gain_change, next_gain_mom = settle(
+        sketches,
+        grad_gains,
+        gain_mom,
+        [full_grad, *grad_mats],
+        errors,
         (embed_mom, qkv_mom, out_mom, up_mom, down_mom),
-        (w_qkv, w_out, w_up, w_down),
-        ph,
-        phs,
-        right_mean,
+        slices,
+        workers,
+        shards,
     )
-    total_norm = norm[0, 0]
-    factors, at = [], 0
-    for grad_part in own_grads:
-        factors.append(right_mean[:, at : at + grad_part.shape[1]].T[None])
-        at += grad_part.shape[1]
-    gain_mean = gain_sum[:, :192].reshape(3, -1) / workers
-    next_gain_mom = MOMENTUM * gain_mom.astype(jnp.float32) + gain_mean
-    gain_change = -LEARN_RATE * next_gain_mom
     return (
         loss_value.reshape(1),
-        total_norm.reshape(1),
+        norm[0, 0].reshape(1),
         *changed,
         gain_change,
         *new_moments,
         next_gain_mom,
         *(e[None] for e in new_errors),
-        *factors,
+        *(r.T[None] for r in rights),
     )
 
 

time: 338 us -> 309 us (0.914)
  Pallas kernels: 309 us -> 290 us
  other arithmetic: 22.8 us -> 5.22 us
  local copies, waits for them, and re-layouts: 5.06 us -> 12 us
    scatter-add x1 -> x0, other arithmetic: 19.1 us -> none  [body(): lookup_grad = jnp.zeros(embedding.shape, jnp.float32).at[safe_ids].add(jn...]
    pallas_call x6 -> x3, Pallas kernels: 125 us -> 113 us  [the longest x1 48.7 us: settle(): pl.pallas_call(functools.partial(settle_kernel, workers, shards, rows, ro...]
    gather x0 -> x1, local copies, waits for them, and re-layouts: none -> 9.64 us  [body(): embedding.at[jnp.clip(local_ids, 0, vocab_rows - 1)]]
    pallas_call x1, Pallas kernels: 30 us -> 25.4 us  [opening(): pl.pallas_call(functools.partial(open_kernel, shards, axis), in_specs=[VM...]
where the time goes in v3:
time: 309 us
  Pallas kernels  290 us (94%)
  local copies, waits for them, and re-layouts  12 us (4%)
  other arithmetic  5.22 us (2%)
    pallas_call x1, Pallas kernels, vocabulary_head(): pl.pallas_call(functools.partial(head_kernel, shards, axis), grid=(3, blo...  58.9 us
    pallas_call x1, Pallas kernels, layer_backward(): pl.pallas_call(functools.partial(backward_kernel, shard_axis), in_specs=[...  48.9 us
    pallas_call x1, Pallas kernels, settle(): pl.pallas_call(functools.partial(settle_kernel, workers, shards, rows, ro...  48.7 us
    pallas_call x1, Pallas kernels, layer_forward(): pl.pallas_call(functools.partial(forward_kernel, shards, axis), in_specs=...  44.4 us
    pallas_call x1, Pallas kernels, settle(): pl.pallas_call(functools.partial(finish_kernel, rows, row_list, widths),...  34.6 us
    pallas_call x1, Pallas kernels, scatter_sketch(): pl.pallas_call(functools.partial(scatter_sketch_kernel, axis, rows, row_l...  29.6 us
    pallas_call x1, Pallas kernels, opening(): pl.pallas_call(functools.partial(open_kernel, shards, axis), in_specs=[VM...  25.4 us
    gather x1, local copies, waits for them, and re-layouts, body(): embedding.at[jnp.clip(local_ids, 0, vocab_rows - 1)]  9.64 us

profile of v3, /device:TPU:0, one launch (start us, length us, event | category | flops | bytes accessed | tf_op | source)
XLA Modules:
  0.0 308.6 jit_solution(8617396784072616003)
XLA Ops:
  0.7 0.7 compare_and_fusion
  1.4 1.3 broadcast_subtract_fusion.target_ref
  2.7 0.7 compare_select_fusion
  3.4 1.2 multiply_sine_fusion
  4.6 9.6 %gather_fusion = bf16[1024,512]{1,0:T(8,128)(2,1)S(1)} fusion(f32[8000,512]{1,0:T(8,128)} %table_ref.1, s32[1024]{0:T(1024)S(1)} %broadcast_clamp_fusion), kind=kCustom, calls=%fused_computation | custom fusion | bytes 2101248 | tf_op jit(solution)/shard_map/gather | solution.py:1319
  14.3 1.3 select_convert_fusion.own_ref
  15.6 25.4 %opening.1 = (bf16[1024,512]{1,0:T(8,128)(2,1)}, bf16[4,128,1536]{2,1,0:T(8,128)(2,1)}) custom-call(bf16[1024,512]{1,0:T(8,128)(2,1)} %select_convert_fusion.own_ref, f32[128,1536]{1,0:T(8,128)} %refs_15_.1), custom_call_target="tpu_custom_call" | custom-call | tf_op jit(solution)/shard_map/opening/pallas_call | solution.py:1048
  41.0 44.4 %layer_forward.1 = (bf16[1024,512]{1,0:T(8,128)(2,1)}, bf16[3,512,1024]{2,1,0:T(8,128)(2,1)}, f32[8,1,1024]{2,1,0:T(1,128)}, bf16[512,1024]{1,0:T(8,128)(2,1)}, ...) custom-call(bf16[1024,512]{1,0:T(8,128)(2,1)} %get-tuple-element.81., ...), custom_call_target="tpu_custom_call" | custom-call | tf_op jit(solution)/shard_map/layer_forward/pallas_call | solution.py:563
  85.4 58.9 %vocabulary_head.1 = (f32[8000,512]{1,0:T(8,128)}, f32[512,1024]{1,0:T(8,128)}, f32[8,128]{1,0:T(8,128)}) custom-call(bf16[1024,512]{1,0:T(8,128)(2,1)} %get-tuple-element.83.n3_ref, s32[1,1024]{1,0:T(1,128)} %broadcast_subtract_fusion.target_ref, f32[8000,512]{1,0:T(8,128)} %table_ref.1), custom_call_target="tpu_custom_call" | custom-call | tf_op jit(solution)/shard_map/vocabulary_head/pallas_call | solution.py:1246
  144.3 48.9 %layer_backward.1 = (f32[1024,512]{1,0:T(8,128)}, f32[128,1536]{1,0:T(8,128)}, f32[128,512]{1,0:T(8,128)}, f32[128,2048]{1,0:T(8,128)}, f32[512,512]{1,0:T(8,128)}, /*index=5*/f32[8,512]{1,0:T(8,128)}) custom-call(f32[512,1024]{1,0:T(8,128)} %get-tuple-element.86.refs_0_, f32[1024,512]{1,0:T(8,128)} %get-tuple-element.87.refs_1_, ...), custom_call_target="tpu_custom_call" | custom-call | tf_op jit(solution)/shard_map/layer_backward/pallas_call | solution.py:745
  193.2 1.2 slice.6
  194.4 29.6 %scatter_sketch.1 = (f32[8000,512]{1,0:T(8,128)}, f32[8,8192]{1,0:T(8,128)}, f32[8,8192]{1,0:T(8,128)}, f32[8,896]{1,0:T(8,128)}, f32[8,896]{1,0:T(8,128)}, /*index=5*/f32[8,512]{1,0:T(8,128)}) custom-call(s32[1024]{0:T(1024)} %bitcast.73, f32[8000,512]{1,0:T(8,128)} %get-tuple-element.85.refs_0_, f32[1024,512]{1,0:T(8,128)} %get-tuple-element.98.refs_1_, ...), custom_call_target="tpu_custom_call" | custom-call | tf_op jit(solution)/shard_map/scatter_sketch/pallas_call | solution.py:862
  224.0 48.7 %settle_sums.1 = (f32[8,8192]{1,0:T(8,128)}, f32[8,896]{1,0:T(8,128)}, f32[8,6144]{1,0:T(8,128)}, f32[8,6144]{1,0:T(8,128)}, f32[8,128]{1,0:T(8,128)}, /*index=5*/f32[8,512]{1,0:T(8,128)}) custom-call(f32[8,8192]{1,0:T(8,128)} %get-tuple-element.103.refs_0_, f32[8,8192]{1,0:T(8,128)} %get-tuple-element.104.refs_1_, f32[8,896]{1,0:T(8,128)} %get-tuple-element.105.refs_2_, ...), custom_call_target="tpu_custom_call" | custom-call | tf_op jit(solution)/shard_map/settle_sums/pallas_call | solution.py:339
  272.7 1.2 slice.7
  273.9 34.6 %settle_finish.1 = (f32[8000,512]{1,0:T(8,128)}, f32[128,1536]{1,0:T(8,128)}, f32[128,512]{1,0:T(8,128)}, f32[128,2048]{1,0:T(8,128)}, f32[512,512]{1,0:T(8,128)...) custom-call(f32[8000,512]{1,0:T(8,128)} %get-tuple-element.109.refs_, ...), custom_call_target="tpu_custom_call" | custom-call | tf_op jit(solution)/shard_map/settle_finish/pallas_call | solution.py:360
  (3 shorter events, 0.0 us)

commit v4 on v3

--- a/solution.py
+++ b/solution.py
@@ -2,6 +2,7 @@
 
 import jax
 import jax.numpy as jnp
+import numpy as np
 from jax import lax
 from jax.experimental import pallas as pl
 from jax.experimental.pallas import tpu as pltpu
@@ -190,7 +191,7 @@
     grads, errs = refs[6:11], refs[11:16]
     ph, phs, own_ref, mean_ref, norm_ref, gain_ref = refs[16:22]
     (
-        x, landing, y, small, sq_all, flat, x16, landing16, y16,
+        x, landing, y, small, sq_all, flat, x16, landing16, y16, table16, table_send, table_recv,
         sem_a, sem_b, sem_c, sem_d, sem_e, sem_f, sem_g, sem_h, sq_send, sq_recv,
     ) = refs[22:]
     first_sems, second_sems = (sem_a, sem_b, sem_c, sem_d), (sem_e, sem_f, sem_g, sem_h)
@@ -254,35 +255,62 @@
             matrix = clip * grads[k + 1][...] + errs[k + 1][...].astype(F32)
             right_t = right_of(basis_t, matrix)
             flat[:, starts[k + 1] : starts[k + 1] + widths[k + 1]] = right_t
+        half = x16.shape[2]
+        for j in range(workers):
+            low, high = starts[1] + j * 2 * half, starts[1] + (j * 2 + 1) * half
+            pair = jnp.concatenate([flat[:, low : low + half], flat[:, high : high + half]], axis=0)
+            x16[j] = pair.astype(BF16)
+        ring_start("rep", workers, x16, landing16, second_sems)
 
     clip = clip_of(norm_ref[...])
     matrix = clip * grads[0][...] + errs[0][...].astype(F32)
     matrix = keep_rows(matrix, step * TB, rows)
     flat[:, : widths[0]] += right_of(ph[:, pl.ds(at, TB)], matrix)
 
+    @pl.when(step == last // 2)
+    def _():
+        ring_middle("rep", workers, x16, landing16, y16, second_sems)
+
     @pl.when(step == last)
     def _():
+        me = lax.axis_index("rep")
+        split = widths[0] // 2
+        table16[me] = jnp.concatenate([flat[:, :split], flat[:, split : 2 * split]], axis=0).astype(BF16)
+        copies = ring_copies(
+            "rep", workers, table16, table16, table_send, table_recv, lambda me, peer, step: (me, me)
+        )
+        for copy in copies:
+            copy.start()
+        own_ref[...] = flat[...]
+        ring_end("rep", workers, y16, second_sems)
         half = x16.shape[2]
         for j in range(workers):
-            low, high = j * 2 * half, (j * 2 + 1) * half
-            pair = jnp.concatenate([flat[:, low : low + half], flat[:, high : high + half]], axis=0)
-            x16[j] = pair.astype(BF16)
-        ring_start("rep", workers, x16, landing16, second_sems)
-        own_ref[...] = flat[...]
-        ring_middle("rep", workers, x16, landing16, y16, second_sems)
-        ring_end("rep", workers, y16, second_sems)
-        for j in range(workers):
             pair = y16[j].astype(F32) * (1.0 / workers)
-            low, high = j * 2 * half, (j * 2 + 1) * half
+            low, high = starts[1] + j * 2 * half, starts[1] + (j * 2 + 1) * half
             mean_ref[:, low : low + half] = pair[:8]
             mean_ref[:, high : high + half] = pair[8:]
+        for gap in range(1, workers):
+            source = lax.rem(me - gap + workers, workers)
+            pltpu.make_async_remote_copy(
+                src_ref=table16.at[source], dst_ref=table16.at[source],
+                send_sem=table_send.at[gap], recv_sem=table_recv.at[gap],
+                device_id={"rep": source}, device_id_type=MESH_ID,
+            ).wait_recv()
+        total = table16[0].astype(F32)
+        for j in range(1, workers):
+            total = total + table16[j].astype(F32)
+        total = total * (1.0 / workers)
+        mean_ref[:, :split] = total[:8]
+        mean_ref[:, split : 2 * split] = total[8:]
+        for copy in copies:
+            copy.wait_send()
 
 
 def finish_kernel(rows, row_list, widths, *refs):
     grads, errs, moms, weights = refs[0:5], refs[5:10], refs[10:15], refs[15:19]
-    ph_ref, phs_ref, own_ref, mean_ref, norm_ref, gain_ref, gain_mom_ref = refs[19:26]
-    new_errs, new_moms, changed, rights = refs[26:31], refs[31:36], refs[36:41], refs[41:46]
-    gain_change_ref, next_gain_ref = refs[46:48]
+    ph_ref, phs_ref, own_ref, mean_ref, norm_ref, gain_ref, gain_mom_ref, loss_ref = refs[19:27]
+    new_errs, new_moms, changed, rights = refs[27:32], refs[32:37], refs[37:42], refs[42:47]
+    gain_change_ref, next_gain_ref, loss_out, norm_out = refs[47:51]
     step = pl.program_id(0)
     places, _ = small_places(row_list)
     starts = [sum(widths[:k]) for k in range(5)]
@@ -302,6 +330,8 @@
         moved = MOMENTUM * gain_mom_ref[...].astype(F32) + gain_ref[: gain_mom_ref.shape[0], :]
         next_gain_ref[...] = moved
         gain_change_ref[...] = -LEARN_RATE * moved
+        loss_out[0] = jnp.max(loss_ref[...])
+        norm_out[0] = jnp.max(norm_ref[...])
         for k in range(5):
             rights[k][...] = mean_ref[:, starts[k] : starts[k] + widths[k]]
         for k in range(1, 5):
@@ -314,7 +344,7 @@
     return pl.BlockSpec(shape, lambda *_: (0,) * len(shape), pipeline_mode=pl.Buffered(1))
 
 
-def settle(sketches, gains, gain_mom, grads, errs, moms, weights, workers, shards):
+def settle(loss_tile, sketches, gains, gain_mom, grads, errs, moms, weights, workers, shards):
     gq, eq, gs, es, sq = sketches
     rows, width = grads[0].shape
     blocks = pl.cdiv(rows, TB)
@@ -322,8 +352,9 @@
     widths = [g.shape[1] for g in grads]
     small = round_up(gs.shape[1] + gains.shape[1], workers * 128)
     lanes = (gq.shape[1] + small) // workers
-    right_lanes = round_up(sum(widths), workers * 256)
-    half = right_lanes // workers // 2
+    small_lanes = round_up(sum(widths[1:]), workers * 256)
+    right_lanes = widths[0] + small_lanes
+    half = small_lanes // workers // 2
     shape = jax.ShapeDtypeStruct
     block = pl.BlockSpec((TB, width), lambda i: (i, 0))
     small_specs = [held(g.shape) for g in grads[1:]]
@@ -349,6 +380,8 @@
             pltpu.VMEM((RK, right_lanes), F32),
         ]
         + [pltpu.VMEM((workers, 16, half), BF16)] * 3
+        + [pltpu.VMEM((workers, 16, width // 2), BF16)]
+        + [pltpu.SemaphoreType.DMA((workers,))] * 2
         + [pltpu.SemaphoreType.DMA((workers,))] * 8
         + [pltpu.SemaphoreType.DMA((shards,))] * 2,
         compiler_params=pltpu.CompilerParams(
@@ -364,17 +397,19 @@
         + small_specs
         + [pl.BlockSpec((RK, TB), lambda i: (0, i))]
         + [held(m.shape) for m in made[1:]]
-        + [held(gain_mom.shape)],
+        + [held(gain_mom.shape), held(loss_tile.shape)],
         out_specs=([block] + small_specs) * 3
         + [held((RK, w)) for w in widths]
-        + [held(gain_mom.shape)] * 2,
+        + [held(gain_mom.shape)] * 2
+        + [pl.BlockSpec(memory_space=pltpu.SMEM)] * 2,
         out_shape=[shape(g.shape, F32) for g in grads] * 3
         + [shape((RK, w), F32) for w in widths]
-        + [shape(gain_mom.shape, F32)] * 2,
+        + [shape(gain_mom.shape, F32)] * 2
+        + [shape((1,), F32)] * 2,
         compiler_params=pltpu.CompilerParams(vmem_limit_bytes=60 << 20),
         name="settle_finish",
-    )(*grads, *errs, *moms, *weights, ph, phs, own, mean, norm, gain, gain_mom)
-    return out[0:5], out[5:10], out[10:15], out[15:20], norm, out[20], out[21]
+    )(*grads, *errs, *moms, *weights, ph, phs, own, mean, norm, gain, gain_mom, loss_tile)
+    return out[0:5], out[5:10], out[10:15], out[15:20], *out[20:24]
 
 
 EPS = 1e-06
@@ -470,34 +505,47 @@
 
     spreads[0].relay()
 
-    def attend(head):
-        rows = pl.ds(pl.multiple_of(head * HD, HD), HD)
-        query_t, key_t, value_t = qkv_ref[0, rows, :], qkv_ref[1, rows, :], qkv_ref[2, rows, :]
-        keys = key_t.T
-        mixed_parts, lse_parts = [], []
-        for block in range(row_blocks):
+    @pl.loop(0, width // (2 * HD))
+    def _(pair):
+        @pl.when(pair == 1)
+        def _():
+            spreads[1].relay()
+            spreads[0].relay_across()
+
+        @pl.when(pair == 2)
+        def _():
+            spreads[2].relay()
+
+        @pl.when(pair == 3)
+        def _():
+            spreads[1].relay_across()
+
+        places = [pl.ds(pl.multiple_of((pair * 2 + side) * HD, HD), HD) for side in range(2)]
+        keys = [qkv_ref[1, places[side], :].T for side in range(2)]
+
+        def scores_of(side, block):
             count = (block + 1) * QB
-            scores = causal_tile(
-                nn_dot(keys[:count], query_t[:, block * QB : count]), -1e30
-            )
+            query_t = qkv_ref[0, places[side], block * QB : count]
+            return causal_tile(nn_dot(keys[side][:count], query_t), -1e30)
+
+        work = [(side, block) for side in range(2) for block in range(row_blocks)]
+        ahead = scores_of(*work[0])
+        mixed_parts, lse_parts = ([], []), ([], [])
+        for at, (side, block) in enumerate(work):
+            scores = ahead
+            if at + 1 < len(work):
+                ahead = scores_of(*work[at + 1])
             top = jnp.max(scores, axis=0, keepdims=True)
             weight = jnp.exp(scores - top)
             total = jnp.sum(weight, axis=0, keepdims=True)
             probs = (weight * (1.0 / total)).astype(BF16)
-            mixed_parts.append(nn_dot(value_t[:, :count], probs))
-            lse_parts.append(top + jnp.log(total))
-        mixed_ref[rows, :] = jnp.concatenate(mixed_parts, axis=1).astype(BF16)
-        lse_ref[head] = jnp.concatenate(lse_parts, axis=1)
-
-    heads = width // HD
-    pl.loop(0, heads // 4)(attend)
-    spreads[1].relay()
-    spreads[0].relay_across()
-    pl.loop(heads // 4, heads // 2)(attend)
-    spreads[2].relay()
-    pl.loop(heads // 2, 3 * heads // 4)(attend)
-    spreads[1].relay_across()
-    pl.loop(3 * heads // 4, heads)(attend)
+            value_t = qkv_ref[2, places[side], : (block + 1) * QB]
+            mixed_parts[side].append(nn_dot(value_t, probs))
+            lse_parts[side].append(top + jnp.log(total))
+        for side in range(2):
+            mixed_ref[places[side], :] = jnp.concatenate(mixed_parts[side], axis=1).astype(BF16)
+            lse_ref[pair * 2 + side] = jnp.concatenate(lse_parts[side], axis=1)
+
     spreads[0].finish()
 
     @pl.loop(0, row_blocks)
@@ -677,40 +725,53 @@
     @pl.loop(0, width // (2 * HD))
     def _(pair):
         made = ([], [], [])
-        for side in range(2):
-            head = pair * 2 + side
-            rows = pl.ds(pl.multiple_of(head * HD, HD), HD)
-            query_t, key_t, value_t = qkv_ref[0, rows, :], qkv_ref[1, rows, :], qkv_ref[2, rows, :]
-            dmix_t = dmixed_ref[rows, :]
-            query, key, value, dmix = query_t.T, key_t.T, value_t.T, dmix_t.T
-            lse = lse_ref[head]
-            dquery_parts = []
-            dkey = [None] * row_blocks
-            dvalue = [None] * row_blocks
-            for block in range(row_blocks):
-                count = (block + 1) * QB
-                at = slice(block * QB, count)
-                scores = nn_dot(key[:count], query_t[:, at])
-                probs = causal_tile(jnp.exp(scores - lse[:, at]), 0.0)
-                dprobs = nn_dot(value[:count], dmix_t[:, at])
-                delta = jnp.sum(probs * dprobs, axis=0, keepdims=True)
-                dscores = (probs * (dprobs - delta)).astype(BF16)
-                dquery_parts.append(nn_dot(key_t[:, :count], dscores))
-                more_key = nn_dot(dscores, query[at])
-                more_value = nn_dot(probs.astype(BF16), dmix[at])
-                for piece in range(block + 1):
-                    cut = slice(piece * QB, (piece + 1) * QB)
-                    if dkey[piece] is None:
-                        dkey[piece], dvalue[piece] = more_key[cut], more_value[cut]
-                    else:
-                        dkey[piece] = dkey[piece] + more_key[cut]
-                        dvalue[piece] = dvalue[piece] + more_value[cut]
-            cos_t, sin_t = cos_ref[...], sin_ref[...]
-            dquery_t = jnp.concatenate(dquery_parts, axis=1) * HD ** (-0.5)
-            dkey_t = jnp.concatenate(dkey, axis=0).T
-            made[0].append(turned_back(dquery_t, cos_t, sin_t, half).T)
-            made[1].append(turned_back(dkey_t, cos_t, sin_t, half).T)
-            made[2].append(jnp.concatenate(dvalue, axis=0))
+        places = [pl.ds(pl.multiple_of((pair * 2 + side) * HD, HD), HD) for side in range(2)]
+        natural = [
+            [ref[rows, :].T for ref in (qkv_ref.at[0], qkv_ref.at[1], qkv_ref.at[2], dmixed_ref)]
+            for rows in places
+        ]
+
+        def products_of(side, block):
+            count = (block + 1) * QB
+            at = slice(block * QB, count)
+            _, key, value, _ = natural[side]
+            scores = nn_dot(key[:count], qkv_ref[0, places[side], at])
+            return scores, nn_dot(value[:count], dmixed_ref[places[side], at])
+
+        work = [(side, block) for side in range(2) for block in range(row_blocks)]
+        ahead = products_of(*work[0])
+        dquery_parts = []
+        for place, (side, block) in enumerate(work):
+            if block == 0:
+                dquery_parts = []
+                dkey = [None] * row_blocks
+                dvalue = [None] * row_blocks
+            scores, dprobs = ahead
+            if place + 1 < len(work):
+                ahead = products_of(*work[place + 1])
+            count = (block + 1) * QB
+            at = slice(block * QB, count)
+            query, _, _, dmix = natural[side]
+            probs = causal_tile(jnp.exp(scores - lse_ref[pair * 2 + side][:, at]), 0.0)
+            delta = jnp.sum(probs * dprobs, axis=0, keepdims=True)
+            dscores = (probs * (dprobs - delta)).astype(BF16)
+            dquery_parts.append(nn_dot(qkv_ref[1, places[side], :count], dscores))
+            more_key = nn_dot(dscores, query[at])
+            more_value = nn_dot(probs.astype(BF16), dmix[at])
+            for piece in range(block + 1):
+                cut = slice(piece * QB, (piece + 1) * QB)
+                if dkey[piece] is None:
+                    dkey[piece], dvalue[piece] = more_key[cut], more_value[cut]
+                else:
+                    dkey[piece] = dkey[piece] + more_key[cut]
+                    dvalue[piece] = dvalue[piece] + more_value[cut]
+            if block == row_blocks - 1:
+                cos_t, sin_t = cos_ref[...], sin_ref[...]
+                dquery_t = jnp.concatenate(dquery_parts, axis=1) * HD ** (-0.5)
+                dkey_t = jnp.concatenate(dkey, axis=0).T
+                made[0].append(turned_back(dquery_t, cos_t, sin_t, half).T)
+                made[1].append(turned_back(dkey_t, cos_t, sin_t, half).T)
+                made[2].append(jnp.concatenate(dvalue, axis=0))
         for part in range(3):
             lanes = pl.ds(pl.multiple_of(part * width + pair * 2 * HD, 2 * HD), 2 * HD)
             dpacked_ref[:, lanes] = jnp.concatenate(made[part], axis=1).astype(BF16)
@@ -983,7 +1044,7 @@
 
 
 def open_kernel(
-    shards, axis, own_ref, weight_ref, x0_ref, full_ref,
+    shards, axis, count, ids_ref, rows_ref, weight_ref, x0_ref, full_ref, own_ref,
     half_in, sums, core_send, core_recv, chip_send, chip_recv, back_send, back_recv, sems,
 ):
     greet_all(shards)
@@ -997,6 +1058,10 @@
     other_half = pl.ds(pl.multiple_of((1 - core) * half, half), half)
     spread = Spread(full_ref, shards, sems)
     full_ref[shard] = weight_ref[...].astype(BF16)
+    local = ids_ref[...] - shard * count
+    inside = jnp.where((local >= 0) & (local < count), 1.0, 0.0)
+    inside = jnp.broadcast_to(inside, (8, local.shape[1])).T[:, 0:1]
+    own_ref[...] = jnp.where(inside > 0.5, rows_ref[...], 0.0).astype(BF16)
 
     def chip_copy(peer_chip, slot, at):
         return pltpu.make_async_remote_copy(
@@ -1041,16 +1106,17 @@
     spread.finish()
 
 
-def opening(own, weight, shards, axis):
-    tokens, width = own.shape
+def opening(token_ids, rows, count, weight, shards, axis):
+    tokens, width = rows.shape
     chips = shards // 2
     shape = jax.ShapeDtypeStruct
     return pl.pallas_call(
-        functools.partial(open_kernel, shards, axis),
-        in_specs=[VM] * 2,
+        functools.partial(open_kernel, shards, axis, count),
+        in_specs=[VM] * 3,
         out_specs=[VM] * 2,
         out_shape=[shape((tokens, width), BF16), shape((shards, *weight.shape), BF16)],
         scratch_shapes=[
+            pltpu.VMEM((tokens, width), BF16),
             pltpu.VMEM((tokens // 2, width), BF16),
             pltpu.VMEM((chips, tokens // 2, width), BF16),
         ]
@@ -1060,15 +1126,15 @@
         + [pltpu.SemaphoreType.DMA((8, max(2, chips)))],
         compiler_params=pltpu.CompilerParams(collective_id=4, has_side_effects=True),
         name="opening",
-    )(own, weight)
+    )(token_ids, rows, weight)
 
 
 TOKEN_LANES = 256
 
 
 def vocab_block(rows):
-    best = 16
-    for size in range(16, 1025, 16):
+    best = 8
+    for size in range(8, 1025, 8):
         if rows % size == 0:
             best = size
     return best
@@ -1137,14 +1203,17 @@
 
     def hits(lanes):
         row_at = lax.broadcasted_iota(jnp.int32, (block_rows, TOKEN_LANES), 0)
-        return row_at == target_ref[:, lanes] - step * block_rows
+        return row_at == target_ref[:, lanes] - (shard * (last + 1) + step) * block_rows
 
     @pl.when(phase == 0)
     def _():
         table = table_ref[...].astype(BF16)
+        ahead = nn_dot(table, n3_t[:, :TOKEN_LANES])
         for start in range(0, tokens, TOKEN_LANES):
             lanes = slice(start, start + TOKEN_LANES)
-            logits = nn_dot(table, n3_t[:, lanes])
+            logits = ahead
+            if start + TOKEN_LANES < tokens:
+                ahead = nn_dot(table, n3_t[:, start + TOKEN_LANES : start + 2 * TOKEN_LANES])
             top = jnp.max(logits, axis=0, keepdims=True)
             weight = jnp.exp(logits - top)
             kept[step, :, lanes] = weight
@@ -1237,7 +1306,7 @@
             put.wait()
 
 
-def vocabulary_head(n3, local_targets, table, shards, axis):
+def vocabulary_head(n3, targets, table, shards, axis):
     rows, width = table.shape
     tokens = n3.shape[0]
     size = vocab_block(rows)
@@ -1278,7 +1347,7 @@
             collective_id=3, has_side_effects=True, vmem_limit_bytes=62 << 20
         ),
         name="vocabulary_head",
-    )(n3, local_targets, table)
+    )(n3, targets, table)
 
 
 def body(
@@ -1315,24 +1384,21 @@
     slices = (w_qkv, w_out, w_up, w_down)
     shards = lax.axis_size("voc")
     local_ids = token_ids.reshape(-1) - shard_pos * vocab_rows
-    inside = (local_ids >= 0) & (local_ids < vocab_rows)
-    rows = embedding.at[jnp.clip(local_ids, 0, vocab_rows - 1)].get(mode="promise_in_bounds")
-    own_rows = jnp.where(inside[:, None], rows, 0.0).astype(BF16)
-    x0, qkv_all = opening(own_rows, w_qkv, shards, "voc")
+    rows = embedding.at[local_ids].get(mode="clip")
+    x0, qkv_all = opening(token_ids, rows, vocab_rows, w_qkv, shards, "voc")
     wqkv = qkv_all.reshape(-1, w_qkv.shape[1])
     half = HD // 2
-    angles = (10000.0 ** (-jnp.arange(half).astype(F32) / half))[:, None] * jnp.arange(length).astype(F32)[None, :]
-    cos_t, sin_t = jnp.cos(angles), jnp.sin(angles)
+    inverse = np.float32(10000.0) ** (-np.arange(half, dtype=np.float32) / np.float32(half))
+    angles = inverse[:, None] * np.arange(length, dtype=np.float32)[None, :]
+    cos_t, sin_t = jnp.asarray(np.cos(angles)), jnp.asarray(np.sin(angles))
     *kept, n3, wo, wu, wd, hid = layer_forward(
         x0, norm_gains, cos_t, sin_t, wqkv, slices[1:], shards, "voc"
     )
     kept = (*kept, n3, hid)
     projections = (wqkv, *(w.reshape(-1, w.shape[2]) for w in (wo, wu, wd)))
-    local_targets = target_ids.reshape(1, -1) - shard_pos * vocab_rows
     grad_table_head, dn3_t, loss_tile = vocabulary_head(
-        n3, local_targets, embedding, lax.axis_size("voc"), "voc"
+        n3, target_ids.reshape(1, -1), embedding, lax.axis_size("voc"), "voc"
     )
-    loss_value = loss_tile[0, 0]
     grad_in, *grad_mats, grad_gains = layer_backward(
         "voc", [w.shape for w in slices], dn3_t, norm_gains, cos_t, sin_t, projections, x0, kept
     )
@@ -1343,7 +1409,8 @@
     full_grad, sketches = scatter_sketch(
         token_ids, grad_table_head, grad_in, grad_mats, errors, starts_t, "voc"
     )
-    new_errors, new_moments, changed, rights, norm, gain_change, next_gain_mom = settle(
+    new_errors, new_moments, changed, rights, gain_change, next_gain_mom, loss, norm = settle(
+        loss_tile,
         sketches,
         grad_gains,
         gain_mom,
@@ -1355,8 +1422,8 @@
         shards,
     )
     return (
-        loss_value.reshape(1),
-        norm[0, 0].reshape(1),
+        loss,
+        norm,
         *changed,
         gain_change,
         *new_moments,

time: 309 us -> 288 us (0.932)
  Pallas kernels: 290 us -> 275 us
  other arithmetic: 5.22 us -> 0.7 us
    pallas_call x1, Pallas kernels: 48.9 us -> 42.7 us  [layer_backward(): pl.pallas_call(functools.partial(backward_kernel, shard_axis), in_specs=[...]
    pallas_call x1, Pallas kernels: 44.4 us -> 40.3 us  [layer_forward(): pl.pallas_call(functools.partial(forward_kernel, shards, axis), in_specs=...]
    pallas_call x1, Pallas kernels: 48.7 us -> 45.5 us  [settle(): pl.pallas_call(functools.partial(settle_kernel, workers, shards, rows, ro...]
where the time goes in v4:
time: 288 us; the launch traced here: 287 us
  Pallas kernels  275 us (95%)
  local copies, waits for them, and re-layouts  10.9 us (4%)
    pallas_call x1, Pallas kernels, vocabulary_head(): pl.pallas_call(functools.partial(head_kernel, shards, axis), grid=(3, blo...  56.1 us
    pallas_call x1, Pallas kernels, settle(): pl.pallas_call(functools.partial(settle_kernel, workers, shards, rows, ro...  45.5 us
    pallas_call x1, Pallas kernels, layer_backward(): pl.pallas_call(functools.partial(backward_kernel, shard_axis), in_specs=[...  42.7 us
    pallas_call x1, Pallas kernels, layer_forward(): pl.pallas_call(functools.partial(forward_kernel, shards, axis), in_specs=...  40.3 us
    pallas_call x1, Pallas kernels, settle(): pl.pallas_call(functools.partial(finish_kernel, rows, row_list, widths),...  34.6 us
    pallas_call x1, Pallas kernels, scatter_sketch(): pl.pallas_call(functools.partial(scatter_sketch_kernel, axis, rows, row_l...  29.5 us
    pallas_call x1, Pallas kernels, opening(): pl.pallas_call(functools.partial(open_kernel, shards, axis, count), in_sp...  25.8 us
    gather x1, local copies, waits for them, and re-layouts, body(): rows = embedding.at[local_ids].get(mode='clip')  10.9 us

profile of v4, /device:TPU:0, one launch (start us, length us, event | category | flops | bytes accessed | tf_op | source)
XLA Modules:
  0.0 287.1 jit_solution(2284787384108008035)
XLA Ops:
  0.7 0.7 compare_select_fusion
  1.4 10.9 %gather_fusion = f32[1024,512]{1,0:T(8,128)} fusion(f32[8000,512]{1,0:T(8,128)} %table_ref.1, s32[1024]{0:T(1024)S(1)} %broadcast_clamp_fusion), kind=kCustom, calls=%fused_computation | custom fusion | bytes 4198400 | tf_op jit(solution)/shard_map/gather | solution.py:1387
  12.3 25.8 %opening.1 = (bf16[1024,512]{1,0:T(8,128)(2,1)}, bf16[4,128,1536]{2,1,0:T(8,128)(2,1)}) custom-call(s32[1,1024]{1,0:T(1,128)} %ids_ref.1, f32[1024,512]{1,0:T(8,128)} %gather_fusion, f32[128,1536]{1,0:T(8,128)} %refs_15_.2), custom_call_target="tpu_custom_call" | custom-call | tf_op jit(solution)/shard_map/opening/pallas_call | solution.py:1113
  38.1 40.3 %layer_forward.1 = (bf16[1024,512]{1,0:T(8,128)(2,1)}, bf16[3,512,1024]{2,1,0:T(8,128)(2,1)}, f32[8,1,1024]{2,1,0:T(1,128)}, bf16[512,1024]{1,0:T(8,128)(2,1)}, ...) custom-call(bf16[1024,512]{1,0:T(8,128)(2,1)} %get-tuple-element.83., ...), custom_call_target="tpu_custom_call" | custom-call | tf_op jit(solution)/shard_map/layer_forward/pallas_call | solution.py:611
  78.4 56.1 %vocabulary_head.1 = (f32[8000,512]{1,0:T(8,128)}, f32[512,1024]{1,0:T(8,128)}, f32[8,128]{1,0:T(8,128)}) custom-call(bf16[1024,512]{1,0:T(8,128)(2,1)} %get-tuple-element.85.n3_ref, s32[1,1024]{1,0:T(1,128)} %target_ref.1, f32[8000,512]{1,0:T(8,128)} %table_ref.1), custom_call_target="tpu_custom_call" | custom-call | tf_op jit(solution)/shard_map/vocabulary_head/pallas_call | solution.py:1315
  134.5 42.7 %layer_backward.1 = (f32[1024,512]{1,0:T(8,128)}, f32[128,1536]{1,0:T(8,128)}, f32[128,512]{1,0:T(8,128)}, f32[128,2048]{1,0:T(8,128)}, f32[512,512]{1,0:T(8,128)}, /*index=5*/f32[8,512]{1,0:T(8,128)}) custom-call(f32[512,1024]{1,0:T(8,128)} %get-tuple-element.87.refs_0_, f32[1024,512]{1,0:T(8,128)} %get-tuple-element.88.refs_1_, ...), custom_call_target="tpu_custom_call" | custom-call | tf_op jit(solution)/shard_map/layer_backward/pallas_call | solution.py:806
  177.2 29.5 %scatter_sketch.1 = (f32[8000,512]{1,0:T(8,128)}, f32[8,8192]{1,0:T(8,128)}, f32[8,8192]{1,0:T(8,128)}, f32[8,896]{1,0:T(8,128)}, f32[8,896]{1,0:T(8,128)}, /*index=5*/f32[8,512]{1,0:T(8,128)}) custom-call(s32[1024]{0:T(1024)} %bitcast.70, f32[8000,512]{1,0:T(8,128)} %get-tuple-element.86.refs_0_, f32[1024,512]{1,0:T(8,128)} %get-tuple-element.99.refs_1_, ...), custom_call_target="tpu_custom_call" | custom-call | tf_op jit(solution)/shard_map/scatter_sketch/pallas_call | solution.py:923
  206.8 45.5 %settle_sums.1 = (f32[8,8192]{1,0:T(8,128)}, f32[8,896]{1,0:T(8,128)}, f32[8,6656]{1,0:T(8,128)}, f32[8,6656]{1,0:T(8,128)}, f32[8,128]{1,0:T(8,128)}, /*index=5*/f32[8,512]{1,0:T(8,128)}) custom-call(f32[8,8192]{1,0:T(8,128)} %get-tuple-element.105.refs_0_, f32[8,8192]{1,0:T(8,128)} %get-tuple-element.106.refs_1_, f32[8,896]{1,0:T(8,128)} %get-tuple-element.107.refs_2_, ...), custom_call_target="tpu_custom_call" | custom-call | tf_op jit(solution)/shard_map/settle_sums/pallas_call | solution.py:370
  252.3 34.6 %settle_finish.1 = (f32[8000,512]{1,0:T(8,128)}, f32[128,1536]{1,0:T(8,128)}, f32[128,512]{1,0:T(8,128)}, f32[128,2048]{1,0:T(8,128)}, f32[512,512]{1,0:T(8,128)...) custom-call(f32[8000,512]{1,0:T(8,128)} %get-tuple-element.104.refs_, ...), custom_call_target="tpu_custom_call" | custom-call | tf_op jit(solution)/shard_map/settle_finish/pallas_call | solution.py:393
  (1 shorter events, 0.0 us)

commit v5 on v4

--- a/solution.py
+++ b/solution.py
@@ -22,6 +22,8 @@
 F32 = jnp.float32
 BF16 = jnp.bfloat16
 MESH_ID = pl.DeviceIdType.MESH
+VM = pl.BlockSpec(memory_space=pltpu.VMEM)
+ANYWHERE = pl.BlockSpec(memory_space=pl.ANY)
 
 
 def round_up(value, step):
@@ -188,122 +190,129 @@
 
 def settle_kernel(workers, shards, rows, row_list, widths, *refs):
     gq_ref, eq_ref, gs_ref, es_ref, gains_ref, sq_ref = refs[0:6]
-    grads, errs = refs[6:11], refs[11:16]
+    anys = refs[6:16]
     ph, phs, own_ref, mean_ref, norm_ref, gain_ref = refs[16:22]
     (
         x, landing, y, small, sq_all, flat, x16, landing16, y16, table16, table_send, table_recv,
-        sem_a, sem_b, sem_c, sem_d, sem_e, sem_f, sem_g, sem_h, sq_send, sq_recv,
-    ) = refs[22:]
+        sem_a, sem_b, sem_c, sem_d, sem_e, sem_f, sem_g, sem_h, sq_send, sq_recv, load_sem,
+    ) = refs[22:-10]
+    grads, errs = refs[-10:-5], refs[-5:]
     first_sems, second_sems = (sem_a, sem_b, sem_c, sem_d), (sem_e, sem_f, sem_g, sem_h)
-    step = pl.program_id(0)
-    last = pl.num_programs(0) - 1
     places, _ = small_places(row_list)
     starts = [sum(widths[:k]) for k in range(5)]
     gains_at = gs_ref.shape[1]
-    at = pl.multiple_of(step * TB, TB)
-
-    @pl.when(step == 0)
-    def _():
-        greet((("rep", workers), ("voc", shards)))
-        shard = lax.axis_index("voc")
-        own = jnp.sum(sq_ref[...].reshape(8, 4, 128), axis=1)
-        own = jnp.sum(jnp.sum(own, axis=0, keepdims=True), axis=1, keepdims=True)
-        sq_all[shard] = jnp.broadcast_to(own, (8, 128))
-        copies = ring_copies("voc", shards, sq_all, sq_all, sq_send, sq_recv, lambda me, peer, step: (me, me))
-        for copy in copies:
-            copy.start()
-        gains = gains_ref[...]
-        total = jnp.sum(jnp.sum(gains * gains, axis=0, keepdims=True), axis=1, keepdims=True)
-        small[...] = jnp.zeros_like(small)
-        for gap in range(1, shards):
-            source = lax.rem(shard - gap + shards, shards)
-            pltpu.make_async_remote_copy(
-                src_ref=sq_all.at[source], dst_ref=sq_all.at[source],
-                send_sem=sq_send.at[gap], recv_sem=sq_recv.at[gap],
-                device_id={"voc": source}, device_id_type=MESH_ID,
-            ).wait_recv()
-        for copy in copies:
-            copy.wait_send()
-        for peer in range(shards):
-            total = total + sq_all[peer][0:1, 0:1]
-        norm = jnp.sqrt(total)
-        norm_ref[...] = jnp.broadcast_to(norm, (8, 128))
-        clip = jnp.minimum(1.0, CLIP_NORM / norm)
-
-        chunk = gq_ref.shape[1] // workers
-        part = small.shape[1] // workers
-        small[:, :gains_at] = clip * gs_ref[...] + es_ref[...]
-        small[:, gains_at : gains_at + gains.shape[1]] = clip * gains
-        for j in range(workers):
-            lanes = slice(j * chunk, (j + 1) * chunk)
-            x[j, :, :chunk] = clip * gq_ref[:, lanes] + eq_ref[:, lanes]
-            x[j, :, chunk:] = small[:, j * part : (j + 1) * part]
-        ring_start("rep", workers, x, landing, first_sems)
-        ring_middle("rep", workers, x, landing, y, first_sems)
-        ring_end("rep", workers, y, first_sems)
-        parts = orthonormal_t([y[j, :, :chunk] for j in range(workers)])
-        for j in range(workers):
-            ph[:, j * chunk : (j + 1) * chunk] = parts[j]
-            small[:, j * part : (j + 1) * part] = y[j, :, chunk:]
-        gain_ref[...] = small[:, gains_at : gains_at + gains.shape[1]] * (1.0 / workers)
-        flat[...] = jnp.zeros_like(flat)
-        for k in range(4):
-            place, size = places[k], row_list[k]
-            basis_t = orthonormal_t([small[:, place : place + round_up(size, 128)]])[0]
-            phs[:, place : place + round_up(size, 128)] = basis_t
-            basis_t = basis_t[:, :size]
-            matrix = clip * grads[k + 1][...] + errs[k + 1][...].astype(F32)
-            right_t = right_of(basis_t, matrix)
-            flat[:, starts[k + 1] : starts[k + 1] + widths[k + 1]] = right_t
-        half = x16.shape[2]
-        for j in range(workers):
-            low, high = starts[1] + j * 2 * half, starts[1] + (j * 2 + 1) * half
-            pair = jnp.concatenate([flat[:, low : low + half], flat[:, high : high + half]], axis=0)
-            x16[j] = pair.astype(BF16)
-        ring_start("rep", workers, x16, landing16, second_sems)
-
-    clip = clip_of(norm_ref[...])
-    matrix = clip * grads[0][...] + errs[0][...].astype(F32)
-    matrix = keep_rows(matrix, step * TB, rows)
-    flat[:, : widths[0]] += right_of(ph[:, pl.ds(at, TB)], matrix)
-
-    @pl.when(step == last // 2)
-    def _():
-        ring_middle("rep", workers, x16, landing16, y16, second_sems)
-
-    @pl.when(step == last)
-    def _():
-        me = lax.axis_index("rep")
-        split = widths[0] // 2
-        table16[me] = jnp.concatenate([flat[:, :split], flat[:, split : 2 * split]], axis=0).astype(BF16)
-        copies = ring_copies(
-            "rep", workers, table16, table16, table_send, table_recv, lambda me, peer, step: (me, me)
-        )
-        for copy in copies:
-            copy.start()
-        own_ref[...] = flat[...]
-        ring_end("rep", workers, y16, second_sems)
-        half = x16.shape[2]
-        for j in range(workers):
-            pair = y16[j].astype(F32) * (1.0 / workers)
-            low, high = starts[1] + j * 2 * half, starts[1] + (j * 2 + 1) * half
-            mean_ref[:, low : low + half] = pair[:8]
-            mean_ref[:, high : high + half] = pair[8:]
-        for gap in range(1, workers):
-            source = lax.rem(me - gap + workers, workers)
-            pltpu.make_async_remote_copy(
-                src_ref=table16.at[source], dst_ref=table16.at[source],
-                send_sem=table_send.at[gap], recv_sem=table_recv.at[gap],
-                device_id={"rep": source}, device_id_type=MESH_ID,
-            ).wait_recv()
-        total = table16[0].astype(F32)
-        for j in range(1, workers):
-            total = total + table16[j].astype(F32)
-        total = total * (1.0 / workers)
-        mean_ref[:, :split] = total[:8]
-        mean_ref[:, split : 2 * split] = total[8:]
-        for copy in copies:
-            copy.wait_send()
+    blocks = pl.cdiv(rows, TB)
+    tiles = [pl.ds(at * TB, min(TB, rows - at * TB)) for at in range(blocks)]
+    pairs = [(anys[k].at[tile, :], kept.at[tile, :]) for k, kept in ((0, grads[0]), (5, errs[0])) for tile in tiles]
+    pairs += [(anys[k], grads[k]) for k in range(1, 5)] + [(anys[5 + k], errs[k]) for k in range(1, 5)]
+    loads = [pltpu.make_async_copy(src, dst, load_sem.at[at]) for at, (src, dst) in enumerate(pairs)]
+    for copy in loads:
+        copy.start()
+    greet((("rep", workers), ("voc", shards)))
+    shard = lax.axis_index("voc")
+    own = jnp.sum(sq_ref[...].reshape(8, 4, 128), axis=1)
+    own = jnp.sum(jnp.sum(own, axis=0, keepdims=True), axis=1, keepdims=True)
+    sq_all[shard] = jnp.broadcast_to(own, (8, 128))
+    copies = ring_copies("voc", shards, sq_all, sq_all, sq_send, sq_recv, lambda me, peer, step: (me, me))
+    for copy in copies:
+        copy.start()
+    gains = gains_ref[...]
+    total = jnp.sum(jnp.sum(gains * gains, axis=0, keepdims=True), axis=1, keepdims=True)
+    small[...] = jnp.zeros_like(small)
+    for gap in range(1, shards):
+        source = lax.rem(shard - gap + shards, shards)
+        pltpu.make_async_remote_copy(
+            src_ref=sq_all.at[source], dst_ref=sq_all.at[source],
+            send_sem=sq_send.at[gap], recv_sem=sq_recv.at[gap],
+            device_id={"voc": source}, device_id_type=MESH_ID,
+        ).wait_recv()
+    for copy in copies:
+        copy.wait_send()
+    for peer in range(shards):
+        total = total + sq_all[peer][0:1, 0:1]
+    norm = jnp.sqrt(total)
+    norm_ref[...] = jnp.broadcast_to(norm, (8, 128))
+    clip = jnp.minimum(1.0, CLIP_NORM / norm)
+
+    chunk = gq_ref.shape[1] // workers
+    part = small.shape[1] // workers
+    small[:, :gains_at] = clip * gs_ref[...] + es_ref[...]
+    small[:, gains_at : gains_at + gains.shape[1]] = clip * gains
+    for j in range(workers):
+        lanes = slice(j * chunk, (j + 1) * chunk)
+        x[j, :, :chunk] = clip * gq_ref[:, lanes] + eq_ref[:, lanes]
+        x[j, :, chunk:] = small[:, j * part : (j + 1) * part]
+    ring_start("rep", workers, x, landing, first_sems)
+    ring_middle("rep", workers, x, landing, y, first_sems)
+    for copy in loads:
+        copy.wait()
+    for k in range(1, 5):
+        grads[k][...] = clip * grads[k][...] + errs[k][...].astype(F32)
+
+    @pl.loop(0, blocks)
+    def _(step):
+        tile = pl.ds(pl.multiple_of(step * TB, TB), TB)
+        matrix = clip * grads[0][tile, :] + errs[0][tile, :].astype(F32)
+        grads[0][tile, :] = keep_rows(matrix, step * TB, rows)
+
+    ring_end("rep", workers, y, first_sems)
+    parts = orthonormal_t([y[j, :, :chunk] for j in range(workers)])
+    for j in range(workers):
+        ph[:, j * chunk : (j + 1) * chunk] = parts[j]
+        small[:, j * part : (j + 1) * part] = y[j, :, chunk:]
+    gain_ref[...] = small[:, gains_at : gains_at + gains.shape[1]] * (1.0 / workers)
+    flat[...] = jnp.zeros_like(flat)
+    for k in range(4):
+        place, size = places[k], row_list[k]
+        basis_t = orthonormal_t([small[:, place : place + round_up(size, 128)]])[0]
+        phs[:, place : place + round_up(size, 128)] = basis_t
+        basis_t = basis_t[:, :size]
+        right_t = right_of(basis_t, grads[k + 1][...])
+        flat[:, starts[k + 1] : starts[k + 1] + widths[k + 1]] = right_t
+    half = x16.shape[2]
+    for j in range(workers):
+        low, high = starts[1] + j * 2 * half, starts[1] + (j * 2 + 1) * half
+        pair = jnp.concatenate([flat[:, low : low + half], flat[:, high : high + half]], axis=0)
+        x16[j] = pair.astype(BF16)
+    ring_start("rep", workers, x16, landing16, second_sems)
+
+    @pl.loop(0, blocks)
+    def _(step):
+        tile = pl.ds(pl.multiple_of(step * TB, TB), TB)
+        flat[:, : widths[0]] += right_of(ph[:, tile], grads[0][tile, :])
+
+    me = lax.axis_index("rep")
+    split = widths[0] // 2
+    table16[me] = jnp.concatenate([flat[:, :split], flat[:, split : 2 * split]], axis=0).astype(BF16)
+    copies = ring_copies(
+        "rep", workers, table16, table16, table_send, table_recv, lambda me, peer, step: (me, me)
+    )
+    for copy in copies:
+        copy.start()
+    own_ref[...] = flat[...]
+    ring_middle("rep", workers, x16, landing16, y16, second_sems)
+    ring_end("rep", workers, y16, second_sems)
+    half = x16.shape[2]
+    for j in range(workers):
+        pair = y16[j].astype(F32) * (1.0 / workers)
+        low, high = starts[1] + j * 2 * half, starts[1] + (j * 2 + 1) * half
+        mean_ref[:, low : low + half] = pair[:8]
+        mean_ref[:, high : high + half] = pair[8:]
+    for gap in range(1, workers):
+        source = lax.rem(me - gap + workers, workers)
+        pltpu.make_async_remote_copy(
+            src_ref=table16.at[source], dst_ref=table16.at[source],
+            send_sem=table_send.at[gap], recv_sem=table_recv.at[gap],
+            device_id={"rep": source}, device_id_type=MESH_ID,
+        ).wait_recv()
+    total = table16[0].astype(F32)
+    for j in range(1, workers):
+        total = total + table16[j].astype(F32)
+    total = total * (1.0 / workers)
+    mean_ref[:, :split] = total[:8]
+    mean_ref[:, split : 2 * split] = total[8:]
+    for copy in copies:
+        copy.wait_send()
 
 
 def finish_kernel(rows, row_list, widths, *refs):
@@ -369,9 +378,8 @@
     operands = (gq, eq, gs, es, gains, sq)
     sums = pl.pallas_call(
         functools.partial(settle_kernel, workers, shards, rows, row_list, widths),
-        grid=(blocks,),
-        in_specs=[held(o.shape) for o in operands] + ([block] + small_specs) * 2,
-        out_specs=[held(m.shape) for m in made],
+        in_specs=[VM] * 6 + [ANYWHERE] * 10,
+        out_specs=[VM] * 6,
         out_shape=made,
         scratch_shapes=[pltpu.VMEM((workers, RK, lanes), F32)] * 3
         + [
@@ -383,7 +391,12 @@
         + [pltpu.VMEM((workers, 16, width // 2), BF16)]
         + [pltpu.SemaphoreType.DMA((workers,))] * 2
         + [pltpu.SemaphoreType.DMA((workers,))] * 8
-        + [pltpu.SemaphoreType.DMA((shards,))] * 2,
+        + [pltpu.SemaphoreType.DMA((shards,))] * 2
+        + [pltpu.SemaphoreType.DMA((2 * blocks + 8,))]
+        + [pltpu.VMEM((blocks * TB, width), F32)]
+        + [pltpu.VMEM(g.shape, F32) for g in grads[1:]]
+        + [pltpu.VMEM((blocks * TB, width), BF16)]
+        + [pltpu.VMEM(e.shape, BF16) for e in errs[1:]],
         compiler_params=pltpu.CompilerParams(
             collective_id=1, has_side_effects=True, vmem_limit_bytes=60 << 20
         ),
@@ -596,10 +609,6 @@
 
     for at in range(max(0, chunks - 2), chunks):
         put(at % 2, at).wait()
-
-
-VM = pl.BlockSpec(memory_space=pltpu.VMEM)
-ANYWHERE = pl.BlockSpec(memory_space=pl.ANY)
 
 
 def layer_forward(x0, gains, cos_t, sin_t, wqkv, slices, shards, axis):
@@ -828,80 +837,84 @@
 
 
 def scatter_sketch_kernel(axis, rows, row_list, ids_ref, *refs):
-    table_any, dx0_ref = refs[0:2]
-    grads, errs, starts = (None, *refs[2:6]), refs[6:11], refs[11:16]
+    anys, starts = refs[0:11], refs[11:16]
     full_any, gq_ref, eq_ref, gs_ref, es_ref, sq_ref = refs[16:22]
-    whole_ref, load_sem, store_sem = refs[22:25]
-    phase, step = pl.program_id(0), pl.program_id(1)
-    steps = pl.num_programs(1)
+    dx0_ref, whole_ref, table_err_ref = refs[22:25]
+    grads, errs = refs[25:29], refs[29:33]
+    load_sem, small_sem, store_sem = refs[33:36]
     places, _ = small_places(row_list)
-    size = rows - (pl.cdiv(rows, TB) - 1) * TB
-
-    def tile_copy(at, count, inward):
-        tile = pl.ds(pl.multiple_of(at * TB, TB), count)
-        if inward:
-            return pltpu.make_async_copy(table_any.at[tile, :], whole_ref.at[tile, :], load_sem.at[at])
-        return pltpu.make_async_copy(whole_ref.at[tile, :], full_any.at[tile, :], store_sem.at[at])
-
     blocks = pl.cdiv(rows, TB)
-    sizes = [TB] * (blocks - 1) + [size]
-
-    @pl.when((phase == 0) & (step == 0))
-    def _():
-        for at in range(blocks):
-            tile_copy(at, sizes[at], True).start()
-        gs_ref[...] = jnp.zeros_like(gs_ref)
-        es_ref[...] = jnp.zeros_like(es_ref)
-        total = jnp.zeros(sq_ref.shape, F32)
-        for k in range(4):
-            grad = grads[k + 1][...]
-            start_t = starts[k + 1][...]
-            at = pl.ds(places[k], row_list[k])
-            gs_ref[:, at] = left_of(grad, start_t)
-            es_ref[:, at] = left_of_bf16(errs[k + 1][...], start_t)
-            total = total + fold_squares(grad)
-        sq_ref[...] = total
-
-    @pl.when(phase == 0)
-    def _():
-        err = keep_rows(errs[0][...].astype(F32), step * TB, rows).astype(BF16)
-        eq_ref[...] = left_of_bf16(err, starts[0][...])
-
-    @pl.when((phase == 1) & (step == 0))
-    def _():
-        for at in range(blocks):
-            tile_copy(at, sizes[at], True).wait()
-        first = lax.axis_index(axis) * rows if axis else 0
-        if blocks * TB > rows:
-            whole_ref[pl.ds(rows, blocks * TB - rows), :] = jnp.zeros((blocks * TB - rows, whole_ref.shape[1]), F32)
-        spare = blocks * TB
-
-        @pl.loop(0, dx0_ref.shape[0] // 8)
-        def _(group):
-            base = pl.multiple_of(group * 8, 8)
-            for side in range(8):
-                row = ids_ref[base + side] - first
-                row = jnp.where((row >= 0) & (row < rows), row, spare)
-                whole_ref[pl.ds(row, 1), :] += dx0_ref[pl.ds(base + side, 1), :]
-
-    tile = pl.ds(pl.multiple_of(step * TB, TB), TB)
-
-    @pl.when(phase == 1)
-    def _():
-        grad = whole_ref[tile, :]
-        gq_ref[...] = left_of(grad, starts[0][...])
+    padded = blocks * TB
+    tiles = [pl.ds(at * TB, min(TB, rows - at * TB)) for at in range(blocks)]
+    smalls = [
+        pltpu.make_async_copy(src, dst, small_sem.at[at])
+        for at, (src, dst) in enumerate(zip((*anys[2:6], *anys[7:11], anys[1]), (*grads, *errs, dx0_ref)))
+    ]
+    for copy in smalls[:8]:
+        copy.start()
+    loads = [
+        pltpu.make_async_copy(anys[0].at[tile, :], whole_ref.at[tile, :], load_sem.at[0, at])
+        for at, tile in enumerate(tiles)
+    ]
+    err_loads = [
+        pltpu.make_async_copy(anys[6].at[tile, :], table_err_ref.at[tile, :], load_sem.at[1, at])
+        for at, tile in enumerate(tiles)
+    ]
+    for copy in loads:
+        copy.start()
+    smalls[8].start()
+    for copy in err_loads:
+        copy.start()
+    if padded > rows:
+        rest = pl.ds(rows, padded - rows)
+        whole_ref[rest, :] = jnp.zeros((padded - rows, whole_ref.shape[1]), F32)
+        table_err_ref[rest, :] = jnp.zeros((padded - rows, whole_ref.shape[1]), BF16)
+    gs_ref[...] = jnp.zeros_like(gs_ref)
+    es_ref[...] = jnp.zeros_like(es_ref)
+    for copy in smalls[:8]:
+        copy.wait()
+    total = jnp.zeros(sq_ref.shape, F32)
+    for k in range(4):
+        grad = grads[k][...]
+        start_t = starts[k + 1][...]
+        at = pl.ds(places[k], row_list[k])
+        gs_ref[:, at] = left_of(grad, start_t)
+        es_ref[:, at] = left_of_bf16(errs[k][...], start_t)
+        total = total + fold_squares(grad)
+    sq_ref[...] = total
+    smalls[8].wait()
+    for copy in loads:
+        copy.wait()
+    first = lax.axis_index(axis) * rows if axis else 0
+
+    @pl.loop(0, dx0_ref.shape[0] // 8)
+    def _(group):
+        base = pl.multiple_of(group * 8, 8)
+        for side in range(8):
+            row = ids_ref[base + side] - first
+            row = jnp.where((row >= 0) & (row < rows), row, padded)
+            whole_ref[pl.ds(row, 1), :] += dx0_ref[pl.ds(base + side, 1), :]
+
+    stores = [
+        pltpu.make_async_copy(whole_ref.at[tile, :], full_any.at[tile, :], store_sem.at[at])
+        for at, tile in enumerate(tiles)
+    ]
+    for copy in stores:
+        copy.start()
+    for copy in err_loads:
+        copy.wait()
+
+    @pl.loop(0, blocks)
+    def _(step):
+        at = pl.multiple_of(step * TB, TB)
+        start_t = starts[0][...]
+        grad = whole_ref[pl.ds(at, TB), :]
+        gq_ref[:, pl.ds(at, TB)] = left_of(grad, start_t)
+        eq_ref[:, pl.ds(at, TB)] = left_of_bf16(table_err_ref[pl.ds(at, TB), :], start_t)
         sq_ref[...] += fold_squares(grad)
 
-    for at in range(blocks):
-
-        @pl.when((phase == 1) & (step == at))
-        def _():
-            tile_copy(at, sizes[at], False).start()
-
-    @pl.when((phase == 1) & (step == steps - 1))
-    def _():
-        for at in range(blocks):
-            tile_copy(at, sizes[at], False).wait()
+    for copy in stores:
+        copy.wait()
 
 
 def scatter_sketch(token_ids, table_grad, dx0, grads, errs, starts_t, axis):
@@ -913,43 +926,29 @@
     def whole_at(shape):
         return pl.BlockSpec(shape, lambda *_: (0,) * len(shape), pipeline_mode=pl.Buffered(1))
 
-    def at_phase(wanted, size, place):
-        def index(p, i, ids):
-            return place(jnp.where(p == wanted, i, jnp.where(p < wanted, 0, blocks - 1)))
-
-        return pl.BlockSpec(size, index)
-
     shape = jax.ShapeDtypeStruct
+    made = [(RK, blocks * TB)] * 2 + [(RK, small)] * 2 + [(8, 512)]
     full, *sketches = pl.pallas_call(
         functools.partial(scatter_sketch_kernel, axis, rows, row_list),
         grid_spec=pltpu.PrefetchScalarGridSpec(
             num_scalar_prefetch=1,
-            grid=(2, blocks),
-            in_specs=[ANYWHERE, whole_at(dx0.shape)]
-            + [whole_at(g.shape) for g in grads]
-            + [at_phase(0, (TB, width), lambda i: (i, 0))]
-            + [whole_at(e.shape) for e in errs[1:]]
-            + [whole_at(s.shape) for s in starts_t],
-            out_specs=[
-                ANYWHERE,
-                at_phase(1, (RK, TB), lambda i: (0, i)),
-                at_phase(0, (RK, TB), lambda i: (0, i)),
+            grid=(1,),
+            in_specs=[ANYWHERE] * 11 + [whole_at(s.shape) for s in starts_t],
+            out_specs=[ANYWHERE] + [whole_at(m) for m in made],
+            scratch_shapes=[
+                pltpu.VMEM(dx0.shape, F32),
+                pltpu.VMEM((blocks * TB + 8, width), F32),
+                pltpu.VMEM((blocks * TB, width), BF16),
             ]
-            + [whole_at((RK, small)), whole_at((RK, small)), whole_at((8, 512))],
-            scratch_shapes=[
-                pltpu.VMEM((blocks * TB + 8, width), F32),
-                pltpu.SemaphoreType.DMA((blocks,)),
+            + [pltpu.VMEM(g.shape, F32) for g in grads]
+            + [pltpu.VMEM(e.shape, BF16) for e in errs[1:]]
+            + [
+                pltpu.SemaphoreType.DMA((2, blocks)),
+                pltpu.SemaphoreType.DMA((9,)),
                 pltpu.SemaphoreType.DMA((blocks,)),
             ],
         ),
-        out_shape=[
-            shape((rows, width), F32),
-            shape((RK, blocks * TB), F32),
-            shape((RK, blocks * TB), F32),
-            shape((RK, small), F32),
-            shape((RK, small), F32),
-            shape((8, 512), F32),
-        ],
+        out_shape=[shape((rows, width), F32)] + [shape(m, F32) for m in made],
         compiler_params=pltpu.CompilerParams(vmem_limit_bytes=60 << 20),
         name="scatter_sketch",
     )(token_ids.reshape(-1), table_grad, dx0, *grads, *errs, *starts_t)

time: 288 us -> 277 us (0.962)
  Pallas kernels: 275 us -> 264 us
    pallas_call x1, Pallas kernels: 45.5 us -> 38.1 us  [settle(): pl.pallas_call(functools.partial(settle_kernel, workers, shards, rows, ro...]
where the time goes in v5:
time: 277 us
  Pallas kernels  264 us (95%)
  local copies, waits for them, and re-layouts  10.9 us (4%)
    pallas_call x1, Pallas kernels, vocabulary_head(): pl.pallas_call(functools.partial(head_kernel, shards, axis), grid=(3, blo...  56.1 us
    pallas_call x1, Pallas kernels, layer_backward(): pl.pallas_call(functools.partial(backward_kernel, shard_axis), in_specs=[...  42.7 us
    pallas_call x1, Pallas kernels, layer_forward(): pl.pallas_call(functools.partial(forward_kernel, shards, axis), in_specs=...  40.3 us
    pallas_call x1, Pallas kernels, settle(): pl.pallas_call(functools.partial(settle_kernel, workers, shards, rows, ro...  38.1 us
    pallas_call x1, Pallas kernels, settle(): pl.pallas_call(functools.partial(finish_kernel, rows, row_list, widths),...  34.6 us
    pallas_call x1, Pallas kernels, scatter_sketch(): pl.pallas_call(functools.partial(scatter_sketch_kernel, axis, rows, row_l...  26.7 us
    pallas_call x1, Pallas kernels, opening(): pl.pallas_call(functools.partial(open_kernel, shards, axis, count), in_sp...  25.8 us
    gather x1, local copies, waits for them, and re-layouts, body(): rows = embedding.at[local_ids].get(mode='clip')  10.9 us

profile of v5, /device:TPU:0, one launch (start us, length us, event | category | flops | bytes accessed | tf_op | source)
XLA Modules:
  0.0 276.8 jit_solution(9507776064561419442)
XLA Ops:
  0.7 0.7 compare_select_fusion
  1.4 10.9 %gather_fusion = f32[1024,512]{1,0:T(8,128)} fusion(f32[8000,512]{1,0:T(8,128)} %table_ref.1, s32[1024]{0:T(1024)S(1)} %broadcast_clamp_fusion), kind=kCustom, calls=%fused_computation | custom fusion | bytes 4198400 | tf_op jit(solution)/shard_map/gather | solution.py:1386
  12.3 25.8 %opening.1 = (bf16[1024,512]{1,0:T(8,128)(2,1)}, bf16[4,128,1536]{2,1,0:T(8,128)(2,1)}) custom-call(s32[1,1024]{1,0:T(1,128)} %ids_ref.1, f32[1024,512]{1,0:T(8,128)} %gather_fusion, f32[128,1536]{1,0:T(8,128)} %refs_15_.2), custom_call_target="tpu_custom_call" | custom-call | tf_op jit(solution)/shard_map/opening/pallas_call | solution.py:1112
  38.1 40.3 %layer_forward.1 = (bf16[1024,512]{1,0:T(8,128)(2,1)}, bf16[3,512,1024]{2,1,0:T(8,128)(2,1)}, f32[8,1,1024]{2,1,0:T(1,128)}, bf16[512,1024]{1,0:T(8,128)(2,1)}, ...) custom-call(bf16[1024,512]{1,0:T(8,128)(2,1)} %get-tuple-element.83., ...), custom_call_target="tpu_custom_call" | custom-call | tf_op jit(solution)/shard_map/layer_forward/pallas_call | solution.py:620
  78.4 56.1 %vocabulary_head.1 = (f32[8000,512]{1,0:T(8,128)}, f32[512,1024]{1,0:T(8,128)}, f32[8,128]{1,0:T(8,128)}) custom-call(bf16[1024,512]{1,0:T(8,128)(2,1)} %get-tuple-element.85.n3_ref, s32[1,1024]{1,0:T(1,128)} %target_ref.1, f32[8000,512]{1,0:T(8,128)} %table_ref.1), custom_call_target="tpu_custom_call" | custom-call | tf_op jit(solution)/shard_map/vocabulary_head/pallas_call | solution.py:1314
  134.5 42.7 %layer_backward.1 = (f32[1024,512]{1,0:T(8,128)}, f32[128,1536]{1,0:T(8,128)}, f32[128,512]{1,0:T(8,128)}, f32[128,2048]{1,0:T(8,128)}, f32[512,512]{1,0:T(8,128)}, /*index=5*/f32[8,512]{1,0:T(8,128)}) custom-call(f32[512,1024]{1,0:T(8,128)} %get-tuple-element.87.refs_0_, f32[1024,512]{1,0:T(8,128)} %get-tuple-element.88.refs_1_, ...), custom_call_target="tpu_custom_call" | custom-call | tf_op jit(solution)/shard_map/layer_backward/pallas_call | solution.py:815
  177.2 26.7 %scatter_sketch.1 = (f32[8000,512]{1,0:T(8,128)}, f32[8,8192]{1,0:T(8,128)}, f32[8,8192]{1,0:T(8,128)}, f32[8,896]{1,0:T(8,128)}, f32[8,896]{1,0:T(8,128)}, /*index=5*/f32[8,512]{1,0:T(8,128)}) custom-call(s32[1024]{0:T(1024)} %bitcast.70, f32[8000,512]{1,0:T(8,128)} %get-tuple-element.86.refs_0_, f32[1024,512]{1,0:T(8,128)} %get-tuple-element.99.refs_1_, ...), custom_call_target="tpu_custom_call" | custom-call | tf_op jit(solution)/shard_map/scatter_sketch/pallas_call | solution.py:931
  203.9 38.1 %settle_sums.1 = (f32[8,8192]{1,0:T(8,128)}, f32[8,896]{1,0:T(8,128)}, f32[8,6656]{1,0:T(8,128)}, f32[8,6656]{1,0:T(8,128)}, f32[8,128]{1,0:T(8,128)}, /*index=5*/f32[8,512]{1,0:T(8,128)}) custom-call(f32[8,8192]{1,0:T(8,128)} %get-tuple-element.105.refs_0_, f32[8,8192]{1,0:T(8,128)} %get-tuple-element.106.refs_1_, f32[8,896]{1,0:T(8,128)} %get-tuple-element.107.refs_2_, ...), custom_call_target="tpu_custom_call" | custom-call | tf_op jit(solution)/shard_map/settle_sums/pallas_call | solution.py:379
  242.1 34.6 %settle_finish.1 = (f32[8000,512]{1,0:T(8,128)}, f32[128,1536]{1,0:T(8,128)}, f32[128,512]{1,0:T(8,128)}, f32[128,2048]{1,0:T(8,128)}, f32[512,512]{1,0:T(8,128)...) custom-call(f32[8000,512]{1,0:T(8,128)} %get-tuple-element.104.refs_, ...), custom_call_target="tpu_custom_call" | custom-call | tf_op jit(solution)/shard_map/settle_finish/pallas_call | solution.py:406
  (1 shorter events, 0.0 us)

commit v6 on v5

--- a/solution.py
+++ b/solution.py
@@ -1043,24 +1043,46 @@
 
 
 def open_kernel(
-    shards, axis, count, ids_ref, rows_ref, weight_ref, x0_ref, full_ref, own_ref,
+    shards, axis, count, ids_ref, lanes_ref, table_any, weight_ref, x0_ref, full_ref,
+    own_ref, rows_ref, mask_ref, table_ref, table_sem,
     half_in, sums, core_send, core_recv, chip_send, chip_recv, back_send, back_recv, sems,
 ):
+    tile_rows = count // table_sem.shape[0]
+    loads = [
+        pltpu.make_async_copy(
+            table_any.at[pl.ds(at * tile_rows, tile_rows), :],
+            table_ref.at[pl.ds(at * tile_rows, tile_rows), :],
+            table_sem.at[at],
+        )
+        for at in range(table_sem.shape[0])
+    ]
+    for load in loads:
+        load.start()
     greet_all(shards)
     shard = lax.axis_index(axis)
     core = lax.rem(shard, 2)
     chip = shard // 2
     partner = shard + 1 - 2 * core
     chips = shards // 2
-    half = own_ref.shape[0] // 2
+    half = x0_ref.shape[0] // 2
     own_half = pl.ds(pl.multiple_of(core * half, half), half)
     other_half = pl.ds(pl.multiple_of((1 - core) * half, half), half)
     spread = Spread(full_ref, shards, sems)
     full_ref[shard] = weight_ref[...].astype(BF16)
-    local = ids_ref[...] - shard * count
+    local = lanes_ref[...] - shard * count
     inside = jnp.where((local >= 0) & (local < count), 1.0, 0.0)
-    inside = jnp.broadcast_to(inside, (8, local.shape[1])).T[:, 0:1]
-    own_ref[...] = jnp.where(inside > 0.5, rows_ref[...], 0.0).astype(BF16)
+    mask_ref[...] = jnp.broadcast_to(inside, (128, local.shape[1])).T
+
+    def take(side):
+        @pl.loop(0, half // 8)
+        def _(group):
+            base = pl.multiple_of(side * half + group * 8, 8)
+            for within in range(8):
+                row = jnp.clip(ids_ref[base + within] - shard * count, 0, count - 1)
+                rows_ref[pl.ds(base + within, 1), :] = table_ref[pl.ds(row, 1), :]
+
+        rows = pl.ds(pl.multiple_of(side * half, half), half)
+        own_ref[rows, :] = jnp.where(mask_ref[rows, 0:1] > 0.5, rows_ref[rows, :], 0.0).astype(BF16)
 
     def chip_copy(peer_chip, slot, at):
         return pltpu.make_async_remote_copy(
@@ -1078,12 +1100,16 @@
 
     await_all(shards)
     spread.start()
+    for load in loads:
+        load.wait()
+    take(1 - core)
     first = pltpu.make_async_remote_copy(
         src_ref=own_ref.at[other_half, :], dst_ref=half_in,
         send_sem=core_send, recv_sem=core_recv,
         device_id={axis: partner}, device_id_type=MESH_ID,
     )
     first.start()
+    take(core)
     first.wait_recv()
     sums[chip] = (own_ref[own_half, :].astype(F32) + half_in[...].astype(F32)).astype(BF16)
     for at in range(1, chips):
@@ -1105,17 +1131,21 @@
     spread.finish()
 
 
-def opening(token_ids, rows, count, weight, shards, axis):
-    tokens, width = rows.shape
+def opening(token_ids, table, weight, shards, axis):
+    tokens, (count, width) = token_ids.shape[1], table.shape
     chips = shards // 2
     shape = jax.ShapeDtypeStruct
     return pl.pallas_call(
         functools.partial(open_kernel, shards, axis, count),
-        in_specs=[VM] * 3,
+        in_specs=[pl.BlockSpec(memory_space=pltpu.SMEM), VM, ANYWHERE, VM],
         out_specs=[VM] * 2,
         out_shape=[shape((tokens, width), BF16), shape((shards, *weight.shape), BF16)],
         scratch_shapes=[
             pltpu.VMEM((tokens, width), BF16),
+            pltpu.VMEM((tokens, width), F32),
+            pltpu.VMEM((tokens, 128), F32),
+            pltpu.VMEM((count, width), F32),
+            pltpu.SemaphoreType.DMA((4,)),
             pltpu.VMEM((tokens // 2, width), BF16),
             pltpu.VMEM((chips, tokens // 2, width), BF16),
         ]
@@ -1123,9 +1153,11 @@
         + [pltpu.SemaphoreType.DMA((max(2, chips),))] * 2
         + [pltpu.SemaphoreType.DMA] * 2
         + [pltpu.SemaphoreType.DMA((8, max(2, chips)))],
-        compiler_params=pltpu.CompilerParams(collective_id=4, has_side_effects=True),
+        compiler_params=pltpu.CompilerParams(
+            collective_id=4, has_side_effects=True, vmem_limit_bytes=60 << 20
+        ),
         name="opening",
-    )(token_ids, rows, weight)
+    )(token_ids.reshape(-1), token_ids, table, weight)
 
 
 TOKEN_LANES = 256
@@ -1377,14 +1409,10 @@
 ):
     seq_count, length = token_ids.shape
     tok_count = seq_count * length
-    vocab_rows = embedding.shape[0]
-    shard_pos = lax.axis_index("voc")
     workers = lax.axis_size("rep")
     slices = (w_qkv, w_out, w_up, w_down)
     shards = lax.axis_size("voc")
-    local_ids = token_ids.reshape(-1) - shard_pos * vocab_rows
-    rows = embedding.at[local_ids].get(mode="clip")
-    x0, qkv_all = opening(token_ids, rows, vocab_rows, w_qkv, shards, "voc")
+    x0, qkv_all = opening(token_ids, embedding, w_qkv, shards, "voc")
     wqkv = qkv_all.reshape(-1, w_qkv.shape[1])
     half = HD // 2
     inverse = np.float32(10000.0) ** (-np.arange(half, dtype=np.float32) / np.float32(half))

time: 277 us -> 271 us (0.978)
  local copies, waits for them, and re-layouts: 10.9 us -> 0 us
  Pallas kernels: 264 us -> 269 us
    gather x1 -> x0, local copies, waits for them, and re-layouts: 10.9 us -> none  [body(): rows = embedding.at[local_ids].get(mode='clip')]
    pallas_call x1, Pallas kernels: 25.8 us -> 30.9 us  [opening(): pl.pallas_call(functools.partial(open_kernel, shards, axis, count), in_sp...]
where the time goes in v6:
time: 271 us; the launch traced here: 270 us
  Pallas kernels  269 us (99%)
    pallas_call x1, Pallas kernels, vocabulary_head(): pl.pallas_call(functools.partial(head_kernel, shards, axis), grid=(3, blo...  56.1 us
    pallas_call x1, Pallas kernels, layer_backward(): pl.pallas_call(functools.partial(backward_kernel, shard_axis), in_specs=[...  42.7 us
    pallas_call x1, Pallas kernels, layer_forward(): pl.pallas_call(functools.partial(forward_kernel, shards, axis), in_specs=...  40.7 us
    pallas_call x1, Pallas kernels, settle(): pl.pallas_call(functools.partial(settle_kernel, workers, shards, rows, ro...  37.5 us
    pallas_call x1, Pallas kernels, settle(): pl.pallas_call(functools.partial(finish_kernel, rows, row_list, widths),...  34.6 us
    pallas_call x1, Pallas kernels, opening(): pl.pallas_call(functools.partial(open_kernel, shards, axis, count), in_sp...  30.9 us
    pallas_call x1, Pallas kernels, scatter_sketch(): pl.pallas_call(functools.partial(scatter_sketch_kernel, axis, rows, row_l...  26.7 us

profile of v6, /device:TPU:0, one launch (start us, length us, event | category | flops | bytes accessed | tf_op | source)
XLA Modules:
  0.0 270.1 jit_solution(8284455485382244105)
XLA Ops:
  0.7 30.9 %opening.1 = (bf16[1024,512]{1,0:T(8,128)(2,1)}, bf16[4,128,1536]{2,1,0:T(8,128)(2,1)}) custom-call(s32[1024]{0:T(1024)} %bitcast.67, s32[1,1024]{1,0:T(1,128)} %lanes_ref.1, f32[8000,512]{1,0:T(8,128)} %table_ref.1, f32[128,1536]{1,0:T(8,128)} %refs_15_.2), custom_call_target="tpu_custom_call" | custom-call | tf_op jit(solution)/shard_map/opening/pallas_call | solution.py:1138
  31.6 40.7 %layer_forward.1 = (bf16[1024,512]{1,0:T(8,128)(2,1)}, bf16[3,512,1024]{2,1,0:T(8,128)(2,1)}, f32[8,1,1024]{2,1,0:T(1,128)}, bf16[512,1024]{1,0:T(8,128)(2,1)}, ...) custom-call(bf16[1024,512]{1,0:T(8,128)(2,1)} %get-tuple-element.83., ...), custom_call_target="tpu_custom_call" | custom-call | tf_op jit(solution)/shard_map/layer_forward/pallas_call | solution.py:620
  72.3 56.1 %vocabulary_head.1 = (f32[8000,512]{1,0:T(8,128)}, f32[512,1024]{1,0:T(8,128)}, f32[8,128]{1,0:T(8,128)}) custom-call(bf16[1024,512]{1,0:T(8,128)(2,1)} %get-tuple-element.85.n3_ref, s32[1,1024]{1,0:T(1,128)} %target_ref.1, f32[8000,512]{1,0:T(8,128)} %table_ref.1), custom_call_target="tpu_custom_call" | custom-call | tf_op jit(solution)/shard_map/vocabulary_head/pallas_call | solution.py:1346
  128.4 42.7 %layer_backward.1 = (f32[1024,512]{1,0:T(8,128)}, f32[128,1536]{1,0:T(8,128)}, f32[128,512]{1,0:T(8,128)}, f32[128,2048]{1,0:T(8,128)}, f32[512,512]{1,0:T(8,128)}, /*index=5*/f32[8,512]{1,0:T(8,128)}) custom-call(f32[512,1024]{1,0:T(8,128)} %get-tuple-element.87.refs_0_, f32[1024,512]{1,0:T(8,128)} %get-tuple-element.88.refs_1_, ...), custom_call_target="tpu_custom_call" | custom-call | tf_op jit(solution)/shard_map/layer_backward/pallas_call | solution.py:815
  171.2 26.7 %scatter_sketch.1 = (f32[8000,512]{1,0:T(8,128)}, f32[8,8192]{1,0:T(8,128)}, f32[8,8192]{1,0:T(8,128)}, f32[8,896]{1,0:T(8,128)}, f32[8,896]{1,0:T(8,128)}, /*index=5*/f32[8,512]{1,0:T(8,128)}) custom-call(s32[1024]{0:T(1024)} %bitcast.68, f32[8000,512]{1,0:T(8,128)} %get-tuple-element.86.refs_0_, f32[1024,512]{1,0:T(8,128)} %get-tuple-element.99.refs_1_, ...), custom_call_target="tpu_custom_call" | custom-call | tf_op jit(solution)/shard_map/scatter_sketch/pallas_call | solution.py:931
  197.9 37.5 %settle_sums.1 = (f32[8,8192]{1,0:T(8,128)}, f32[8,896]{1,0:T(8,128)}, f32[8,6656]{1,0:T(8,128)}, f32[8,6656]{1,0:T(8,128)}, f32[8,128]{1,0:T(8,128)}, /*index=5*/f32[8,512]{1,0:T(8,128)}) custom-call(f32[8,8192]{1,0:T(8,128)} %get-tuple-element.105.refs_0_, f32[8,8192]{1,0:T(8,128)} %get-tuple-element.106.refs_1_, f32[8,896]{1,0:T(8,128)} %get-tuple-element.107.refs_2_, ...), custom_call_target="tpu_custom_call" | custom-call | tf_op jit(solution)/shard_map/settle_sums/pallas_call | solution.py:379
  235.3 34.6 %settle_finish.1 = (f32[8000,512]{1,0:T(8,128)}, f32[128,1536]{1,0:T(8,128)}, f32[128,512]{1,0:T(8,128)}, f32[128,2048]{1,0:T(8,128)}, f32[512,512]{1,0:T(8,128)...) custom-call(f32[8000,512]{1,0:T(8,128)} %get-tuple-element.104.refs_, ...), custom_call_target="tpu_custom_call" | custom-call | tf_op jit(solution)/shard_map/settle_finish/pallas_call | solution.py:406

commit v7 on v6

--- a/solution.py
+++ b/solution.py
@@ -474,9 +474,15 @@
 def forward_kernel(
     shards, axis,
     x0_ref, gains_ref, cos_ref, sin_ref, wqkv_ref, wo_own, wu_own, wd_own,
-    n1_ref, qkv_ref, lse_ref, mixed_ref, x1_ref, n2_ref, x2_ref, n3_ref, wo_all, wu_all, wd_all, hid_any,
-    hid_ref, hid_sem, wo_sems, wu_sems, wd_sems,
+    *refs,
 ):
+    outs, hid_any = refs[:11], refs[11]
+    made = refs[12:23]
+    n1_ref, qkv_ref, lse_ref, mixed_ref, x1_ref, n2_ref, x2_ref, n3_ref, wo_all, wu_all, wd_all = made
+    hid_ref, hid_sem, wo_sems, wu_sems, wd_sems, out_sem = refs[23:]
+    leaving = [
+        pltpu.make_async_copy(src, dst, out_sem.at[at]) for at, (src, dst) in enumerate(zip(made, outs))
+    ]
     tokens, width = x0_ref.shape
     half = HD // 2
     row_blocks = tokens // QB
@@ -571,8 +577,12 @@
         n2_ref[rows, :] = scaled_rms(stream, gains_ref[1:2, :]).astype(BF16)
 
     spreads[2].relay_across()
+    for at in (1, 3, 0, 2, 4, 5, 8):
+        leaving[at].start()
     spreads[1].finish()
     spreads[2].finish()
+    leaving[9].start()
+    leaving[10].start()
     chunk = hid_ref.shape[2]
     chunks = wu_all.shape[2] // chunk
     parts = chunk // wd_all.shape[1]
@@ -607,8 +617,12 @@
         rows = pl.ds(pl.multiple_of(block * QB, QB), QB)
         n3_ref[rows, :] = scaled_rms(x2_ref[rows, :], gains_ref[2:3, :]).astype(BF16)
 
+    leaving[6].start()
+    leaving[7].start()
     for at in range(max(0, chunks - 2), chunks):
         put(at % 2, at).wait()
+    for copy in leaving:
+        copy.wait()
 
 
 def layer_forward(x0, gains, cos_t, sin_t, wqkv, slices, shards, axis):
@@ -617,28 +631,29 @@
     shape = jax.ShapeDtypeStruct
     chunk = min(512, hidden)
     sems = pltpu.SemaphoreType.DMA((8, max(2, shards // 2)))
+    made = [
+        shape((tokens, width), BF16),
+        shape((3, width, tokens), BF16),
+        shape((width // HD, 1, tokens), F32),
+        shape((width, tokens), BF16),
+        shape((tokens, width), F32),
+        shape((tokens, width), BF16),
+        shape((tokens, width), F32),
+        shape((tokens, width), BF16),
+    ] + [shape((shards, *w.shape), BF16) for w in slices]
     return pl.pallas_call(
         functools.partial(forward_kernel, shards, axis),
         in_specs=[VM] * 8,
-        out_specs=[VM] * 11 + [ANYWHERE],
-        out_shape=[
-            shape((tokens, width), BF16),
-            shape((3, width, tokens), BF16),
-            shape((width // HD, 1, tokens), F32),
-            shape((width, tokens), BF16),
-            shape((tokens, width), F32),
-            shape((tokens, width), BF16),
-            shape((tokens, width), F32),
-            shape((tokens, width), BF16),
-        ]
-        + [shape((shards, *w.shape), BF16) for w in slices]
-        + [shape((tokens, hidden), F32)],
-        scratch_shapes=[
+        out_specs=[ANYWHERE] * 12,
+        out_shape=made + [shape((tokens, hidden), F32)],
+        scratch_shapes=[pltpu.VMEM(m.shape, m.dtype) for m in made]
+        + [
             pltpu.VMEM((2, tokens, chunk), F32),
             pltpu.SemaphoreType.DMA((2,)),
             sems,
             sems,
             sems,
+            pltpu.SemaphoreType.DMA((len(made),)),
         ],
         compiler_params=pltpu.CompilerParams(
             collective_id=5, has_side_effects=True, vmem_limit_bytes=60 << 20
@@ -662,7 +677,7 @@
         pltpu.make_async_copy(src, dst, load_sem.at[at])
         for at, (src, dst) in enumerate(zip(anys, kept))
     ]
-    for load in loads:
+    for load in loads[:5]:
         load.start()
 
     def block_rows(block):
@@ -670,6 +685,8 @@
 
     loads[0].wait()
     loads[1].wait()
+    for load in loads[5:]:
+        load.start()
     ggains_ref[...] = jnp.zeros_like(ggains_ref)
 
     @pl.loop(0, row_blocks)

time: 271 us -> 266 us (0.982)
  Pallas kernels: 269 us -> 265 us
    pallas_call x1, Pallas kernels: 40.7 us -> 37.1 us  [layer_forward(): pl.pallas_call(functools.partial(forward_kernel, shards, axis), in_specs=...]
where the time goes in v7:
time: 266 us
  Pallas kernels  265 us (100%)
    pallas_call x1, Pallas kernels, vocabulary_head(): pl.pallas_call(functools.partial(head_kernel, shards, axis), grid=(3, blo...  55.7 us
    pallas_call x1, Pallas kernels, layer_backward(): pl.pallas_call(functools.partial(backward_kernel, shard_axis), in_specs=[...  42.7 us
    pallas_call x1, Pallas kernels, settle(): pl.pallas_call(functools.partial(settle_kernel, workers, shards, rows, ro...  37.3 us
    pallas_call x1, Pallas kernels, layer_forward(): pl.pallas_call(functools.partial(forward_kernel, shards, axis), in_specs=...  37.1 us
    pallas_call x1, Pallas kernels, settle(): pl.pallas_call(functools.partial(finish_kernel, rows, row_list, widths),...  34.6 us
    pallas_call x1, Pallas kernels, opening(): pl.pallas_call(functools.partial(open_kernel, shards, axis, count), in_sp...  30.9 us
    pallas_call x1, Pallas kernels, scatter_sketch(): pl.pallas_call(functools.partial(scatter_sketch_kernel, axis, rows, row_l...  26.8 us

profile of v7, /device:TPU:0, one launch (start us, length us, event | category | flops | bytes accessed | tf_op | source)
XLA Modules:
  0.0 266.0 jit_solution(6464995221485960067)
XLA Ops:
  0.7 30.9 %opening.1 = (bf16[1024,512]{1,0:T(8,128)(2,1)}, bf16[4,128,1536]{2,1,0:T(8,128)(2,1)}) custom-call(s32[1024]{0:T(1024)} %bitcast.67, s32[1,1024]{1,0:T(1,128)} %lanes_ref.1, f32[8000,512]{1,0:T(8,128)} %table_ref.1, f32[128,1536]{1,0:T(8,128)} %refs_15_.2), custom_call_target="tpu_custom_call" | custom-call | tf_op jit(solution)/shard_map/opening/pallas_call | solution.py:1155
  31.6 37.1 %layer_forward.1 = (bf16[1024,512]{1,0:T(8,128)(2,1)}, bf16[3,512,1024]{2,1,0:T(8,128)(2,1)}, f32[8,1,1024]{2,1,0:T(1,128)}, bf16[512,1024]{1,0:T(8,128)(2,1)}, ...) custom-call(bf16[1024,512]{1,0:T(8,128)(2,1)} %get-tuple-element.83., ...), custom_call_target="tpu_custom_call" | custom-call | tf_op jit(solution)/shard_map/layer_forward/pallas_call | solution.py:644
  68.6 55.7 %vocabulary_head.1 = (f32[8000,512]{1,0:T(8,128)}, f32[512,1024]{1,0:T(8,128)}, f32[8,128]{1,0:T(8,128)}) custom-call(bf16[1024,512]{1,0:T(8,128)(2,1)} %get-tuple-element.85.n3_ref, s32[1,1024]{1,0:T(1,128)} %target_ref.1, f32[8000,512]{1,0:T(8,128)} %table_ref.1), custom_call_target="tpu_custom_call" | custom-call | tf_op jit(solution)/shard_map/vocabulary_head/pallas_call | solution.py:1363
  124.4 42.7 %layer_backward.1 = (f32[1024,512]{1,0:T(8,128)}, f32[128,1536]{1,0:T(8,128)}, f32[128,512]{1,0:T(8,128)}, f32[128,2048]{1,0:T(8,128)}, f32[512,512]{1,0:T(8,128)}, /*index=5*/f32[8,512]{1,0:T(8,128)}) custom-call(f32[512,1024]{1,0:T(8,128)} %get-tuple-element.87.refs_0_, f32[1024,512]{1,0:T(8,128)} %get-tuple-element.88.refs_1_, ...), custom_call_target="tpu_custom_call" | custom-call | tf_op jit(solution)/shard_map/layer_backward/pallas_call | solution.py:832
  167.1 26.8 %scatter_sketch.1 = (f32[8000,512]{1,0:T(8,128)}, f32[8,8192]{1,0:T(8,128)}, f32[8,8192]{1,0:T(8,128)}, f32[8,896]{1,0:T(8,128)}, f32[8,896]{1,0:T(8,128)}, /*index=5*/f32[8,512]{1,0:T(8,128)}) custom-call(s32[1024]{0:T(1024)} %bitcast.68, f32[8000,512]{1,0:T(8,128)} %get-tuple-element.86.refs_0_, f32[1024,512]{1,0:T(8,128)} %get-tuple-element.99.refs_1_, ...), custom_call_target="tpu_custom_call" | custom-call | tf_op jit(solution)/shard_map/scatter_sketch/pallas_call | solution.py:948
  193.9 37.3 %settle_sums.1 = (f32[8,8192]{1,0:T(8,128)}, f32[8,896]{1,0:T(8,128)}, f32[8,6656]{1,0:T(8,128)}, f32[8,6656]{1,0:T(8,128)}, f32[8,128]{1,0:T(8,128)}, /*index=5*/f32[8,512]{1,0:T(8,128)}) custom-call(f32[8,8192]{1,0:T(8,128)} %get-tuple-element.105.refs_0_, f32[8,8192]{1,0:T(8,128)} %get-tuple-element.106.refs_1_, f32[8,896]{1,0:T(8,128)} %get-tuple-element.107.refs_2_, ...), custom_call_target="tpu_custom_call" | custom-call | tf_op jit(solution)/shard_map/settle_sums/pallas_call | solution.py:379
  231.2 34.6 %settle_finish.1 = (f32[8000,512]{1,0:T(8,128)}, f32[128,1536]{1,0:T(8,128)}, f32[128,512]{1,0:T(8,128)}, f32[128,2048]{1,0:T(8,128)}, f32[512,512]{1,0:T(8,128)...) custom-call(f32[8000,512]{1,0:T(8,128)} %get-tuple-element.104.refs_, ...), custom_call_target="tpu_custom_call" | custom-call | tf_op jit(solution)/shard_map/settle_finish/pallas_call | solution.py:406
